TPU v7x, 32 devices: a whole 2x2x4 slice. The times are simulated.
32 devices in a mesh: rows: 4 (over y, x), mp: 8 (over z, core).
Axes of the slice: x: 2, y: 2, z: 4, core: 2. Of those that a mesh axis runs over, the one named last changes fastest.
Arguments:
- inputs: bfloat16 [8192, 2048], P(('rows', 'mp')), may hold values from -6 to 6
- cotangent: bfloat16 [8192, 2048], P(('rows', 'mp')), may hold values from -6 to 6
- corpus_ids: int32 [4], P('rows'), may hold values from 0 to 3
- corpus_weight: float32 [4], replicated, may hold values from 0.5 to 2
- attn_gain: bfloat16 [2048], P(('rows', 'mp')), may hold values from 0.099609375 to 1.8984375
- qkv_weight: bfloat16 [2048, 1920], P(('rows', 'mp')), may hold values from -0.125 to 0.125
- out_weight: bfloat16 [1280, 2048], P(('rows', 'mp')), may hold values from -2.5 to 2.5
- ffn_gain: bfloat16 [2048], P(('rows', 'mp')), may hold values from 0.099609375 to 1.8984375
- gate_weight: bfloat16 [2048, 6144], P(None, 'mp'), may hold values from -0.125 to 0.125
- up_weight: bfloat16 [2048, 6144], P(None, 'mp'), may hold values from -0.125 to 0.125
- down_weight: bfloat16 [6144, 2048], P('mp'), may hold values from -0.078125 to 0.078125
Outputs:
- outputs: bfloat16 [8192, 2048], P(('rows', 'mp'))
- input_grad: float32 [8192, 2048], P(('rows', 'mp'))
- qkv_grad: float32 [2048, 1920], P(('rows', 'mp'))
- proj_grad: float32 [1280, 2048], P(('rows', 'mp'))
- gate_grad: float32 [2048, 6144], P(None, 'mp')
- up_grad: float32 [2048, 6144], P(None, 'mp')
- down_grad: float32 [6144, 2048], P('mp')
- attn_gain_grad: float32 [2048], P(('rows', 'mp'))
- ffn_gain_grad: float32 [2048], P(('rows', 'mp'))
All inputs are finite; a program needn't handle non-finite values.
Results may differ from a plain program's by a relative error of at most 0.015.
Values may be sent and summed in bfloat16 or wider, within the bound.
A program may use at most 256 MiB of HBM per device.

v0:
```python
import jax
import jax.numpy as jnp
from jax import lax
from jax.sharding import PartitionSpec as P

HEADS = 20
KV_HEADS = 5
HEAD_DIM = 64
LEN = 2048
QBLOCK = 512
QBLOCKS = 4


EPS = 1e-05
THETA = 10000.0


def rotation(positions):
    half_dim = HEAD_DIM // 2
    freqs = jnp.exp(-jnp.log(THETA) * (2.0 * jnp.arange(half_dim, dtype=jnp.float32)) / HEAD_DIM)
    angles = positions.astype(jnp.float32)[:, None] * freqs[None, :]
    return (jnp.cos(angles), jnp.sin(angles))


def rotate(values_in, cosine, sine_part):
    half_dim = HEAD_DIM // 2
    first = values_in[..., :half_dim]
    second = values_in[..., half_dim:]
    return jnp.concatenate(
        [first * cosine - second * sine_part, second * cosine + first * sine_part], axis=-1
    )


def rotate_back(values_in, cosine, sine_part):
    half_dim = HEAD_DIM // 2
    first = values_in[..., :half_dim]
    second = values_in[..., half_dim:]
    return jnp.concatenate(
        [first * cosine + second * sine_part, second * cosine - first * sine_part], axis=-1
    )


def project_kv(normed, weight_kv, positions):
    row_count = normed.shape[0]
    kv_width = KV_HEADS * HEAD_DIM
    kv_raw = jnp.dot(normed, weight_kv, preferred_element_type=jnp.float32)
    cosine, sine_part = rotation(positions)
    keys_part = rotate(
        kv_raw[:, :kv_width].reshape(row_count, KV_HEADS, HEAD_DIM),
        cosine[:, None, :],
        sine_part[:, None, :],
    )
    return jnp.concatenate(
        [keys_part.reshape(row_count, kv_width), kv_raw[:, kv_width:]], axis=1
    ).astype(jnp.bfloat16)


def key_slices(kv_all, seq_start, kv_head, length):
    keys_part = lax.dynamic_slice(kv_all, (seq_start, kv_head * HEAD_DIM), (length, HEAD_DIM))
    values_part = lax.dynamic_slice(
        kv_all, (seq_start, (KV_HEADS + kv_head) * HEAD_DIM), (length, HEAD_DIM)
    )
    return (keys_part, values_part)


def masked_scores(queries, keys_part, block_index, length):
    scores = jnp.einsum(
        "qd,kd->qk", queries, keys_part, preferred_element_type=jnp.float32
    ) * HEAD_DIM ** (-0.5)
    allowed = jnp.arange(length)[None, :] <= block_index * QBLOCK + jnp.arange(QBLOCK)[:, None]
    return jnp.where(allowed, scores, -1e30)


def forward_branch(block_index):
    length = (block_index + 1) * QBLOCK

    def branch(queries, kv_all, seq_start, kv_head):
        keys_part, values_part = key_slices(kv_all, seq_start, kv_head, length)
        scores = masked_scores(queries, keys_part, block_index, length)
        row_max = jnp.max(scores, axis=1, keepdims=True)
        exponent = jnp.exp(scores - row_max)
        row_total = jnp.sum(exponent, axis=1, keepdims=True)
        probabilities = (exponent / row_total).astype(jnp.bfloat16)
        output = jnp.dot(probabilities, values_part, preferred_element_type=jnp.float32).astype(
            jnp.bfloat16
        )
        return (output, (row_max + jnp.log(row_total))[:, 0])

    return branch


def backward_branch(block_index):
    length = (block_index + 1) * QBLOCK

    def branch(queries, grad_output, log_total, kv_all, seq_start, kv_head):
        keys_part, values_part = key_slices(kv_all, seq_start, kv_head, length)
        scores = masked_scores(queries, keys_part, block_index, length)
        probabilities = jnp.exp(scores - log_total[:, None])
        grad_probs = jnp.einsum(
            "qd,kd->qk", grad_output, values_part, preferred_element_type=jnp.float32
        )
        row_delta = jnp.sum(probabilities * grad_probs, axis=1, keepdims=True)
        grad_scores = (probabilities * (grad_probs - row_delta)).astype(jnp.bfloat16)
        grad_queries = jnp.dot(
            grad_scores, keys_part, preferred_element_type=jnp.float32
        ) * HEAD_DIM ** (-0.5)
        grad_keys = jnp.einsum(
            "qk,qd->kd", grad_scores, queries, preferred_element_type=jnp.float32
        ) * HEAD_DIM ** (-0.5)
        grad_values = jnp.einsum(
            "qk,qd->kd",
            probabilities.astype(jnp.bfloat16),
            grad_output,
            preferred_element_type=jnp.float32,
        )
        padding = ((0, LEN - length), (0, 0))
        return (grad_queries, jnp.pad(grad_keys, padding), jnp.pad(grad_values, padding))

    return branch


def add_window(target, update, start_row, start_col):
    current = lax.dynamic_slice(target, (start_row, start_col), update.shape)
    return lax.dynamic_update_slice(target, current + update, (start_row, start_col))


def on_device(
    inputs,
    cotangent,
    corpus_ids,
    corpus_weight,
    attn_gain,
    qkv_weight,
    out_weight,
    ffn_gain,
    gate_weight,
    up_weight,
    down_weight,
):
    tok_dev = inputs.shape[0]
    group_rows = tok_dev * lax.axis_size("mp")
    offset = lax.axis_index("mp") * tok_dev
    seq_group = corpus_ids.shape[0]
    corpora_count = corpus_weight.shape[0]
    sequences_all = seq_group * lax.axis_size("rows")
    q_width = HEADS * HEAD_DIM
    kv_width = KV_HEADS * HEAD_DIM
    group_size = HEADS // KV_HEADS
    model_width = inputs.shape[1]
    tiles_dev = HEADS * QBLOCKS // lax.axis_size("mp")
    first_tile = lax.axis_index("mp") * tiles_dev
    chosen = (corpus_ids[:, None] == jnp.arange(corpora_count)[None, :]).astype(jnp.float32)
    counts = lax.psum(jnp.sum(chosen, axis=0), "rows")
    count_seq = jnp.sum(chosen * counts[None, :], axis=1)
    weight_seq = jnp.sum(chosen * corpus_weight[None, :], axis=1)
    seq_scale = weight_seq * sequences_all / (corpora_count * count_seq)
    qkv_full, out_full, gain_one, gain_two = (
        lax.all_gather(qkv_weight, ("rows", "mp"), axis=0, tiled=True),
        lax.all_gather(out_weight, ("rows", "mp"), axis=0, tiled=True),
        lax.all_gather(attn_gain, ("rows", "mp"), axis=0, tiled=True),
        lax.all_gather(ffn_gain, ("rows", "mp"), axis=0, tiled=True),
    )
    gain_one = gain_one.astype(jnp.float32)
    gain_two = gain_two.astype(jnp.float32)
    weight_kv = qkv_full[:, q_width:]
    residual = inputs.astype(jnp.float32)
    inverse_one = lax.rsqrt(jnp.mean(residual * residual, axis=-1, keepdims=True) + EPS)
    normed_one = (residual * inverse_one * gain_one).astype(jnp.bfloat16)
    local_pos = (offset + jnp.arange(tok_dev)) % LEN
    normed_all, kv_all = (
        lax.all_gather(normed_one, "mp", axis=0, tiled=True),
        lax.all_gather(project_kv(normed_one, weight_kv, local_pos), "mp", axis=0, tiled=True),
    )
    count_items = tiles_dev * seq_group
    forward_list = [forward_branch(b) for b in range(QBLOCKS)]
    backward_list = [backward_branch(b) for b in range(QBLOCKS)]

    def item_info(item_index):
        tile_index = first_tile + item_index // seq_group
        seq_start = item_index % seq_group * LEN
        head_index = tile_index // QBLOCKS
        block_index = tile_index % QBLOCKS
        return (head_index, block_index, seq_start, seq_start + block_index * QBLOCK)

    def forward_item(partial_value, item_index):
        head_index, block_index, seq_start, row_start = item_info(item_index)
        rows_in = lax.dynamic_slice(normed_all, (row_start, 0), (QBLOCK, model_width))
        weight_q = lax.dynamic_slice(qkv_full, (0, head_index * HEAD_DIM), (model_width, HEAD_DIM))
        raw_queries = jnp.dot(rows_in, weight_q, preferred_element_type=jnp.float32)
        cosine, sine_part = rotation(block_index * QBLOCK + jnp.arange(QBLOCK))
        queries = rotate(raw_queries, cosine, sine_part).astype(jnp.bfloat16)
        output, log_total = lax.switch(
            block_index, forward_list, queries, kv_all, seq_start, head_index // group_size
        )
        weight_o = lax.dynamic_slice(out_full, (head_index * HEAD_DIM, 0), (HEAD_DIM, model_width))
        partial_value = add_window(
            partial_value,
            jnp.dot(output, weight_o, preferred_element_type=jnp.float32),
            row_start,
            0,
        )
        return (partial_value, (queries, output, log_total))

    attn_partial, (kept_queries, kept_outputs, kept_totals) = lax.scan(
        forward_item, jnp.zeros((group_rows, model_width), jnp.float32), jnp.arange(count_items)
    )
    attn_sum = lax.psum_scatter(attn_partial, "mp", scatter_dimension=0, tiled=True)
    middle = residual + attn_sum
    inverse_two = lax.rsqrt(jnp.mean(middle * middle, axis=-1, keepdims=True) + EPS)
    normed_two = (middle * inverse_two * gain_two).astype(jnp.bfloat16)
    normed_mid = lax.all_gather(normed_two, "mp", axis=0, tiled=True)
    gate_val = jnp.dot(normed_mid, gate_weight, preferred_element_type=jnp.float32)
    up_val = jnp.dot(normed_mid, up_weight, preferred_element_type=jnp.float32)
    hidden = (jax.nn.silu(gate_val) * up_val).astype(jnp.bfloat16)
    ffn_part = jnp.dot(hidden, down_weight, preferred_element_type=jnp.float32)
    ffn_sum = lax.psum_scatter(
        ffn_part.astype(jnp.bfloat16), "mp", scatter_dimension=0, tiled=True
    ).astype(jnp.float32)
    outputs = (middle + ffn_sum).astype(jnp.bfloat16)
    seq_local = (offset + jnp.arange(tok_dev)) // LEN
    token_scale = jnp.sum(
        (seq_local[:, None] == jnp.arange(seq_group)[None, :]).astype(jnp.float32)
        * seq_scale[None, :],
        axis=1,
    )
    grad_out = cotangent.astype(jnp.float32) * token_scale[:, None]
    grad_all = lax.all_gather(grad_out.astype(jnp.bfloat16), "mp", axis=0, tiled=True)
    grad_hidden = jnp.einsum("td,fd->tf", grad_all, down_weight, preferred_element_type=jnp.float32)
    down_grad = jnp.einsum("tf,td->fd", hidden, grad_all, preferred_element_type=jnp.float32)
    sigmoid_val = jax.nn.sigmoid(gate_val)
    grad_gate = (
        grad_hidden * up_val * (sigmoid_val * (1.0 + gate_val * (1.0 - sigmoid_val)))
    ).astype(jnp.bfloat16)
    grad_up = (grad_hidden * (gate_val * sigmoid_val)).astype(jnp.bfloat16)
    gate_grad = jnp.einsum("td,tf->df", normed_mid, grad_gate, preferred_element_type=jnp.float32)
    up_grad = jnp.einsum("td,tf->df", normed_mid, grad_up, preferred_element_type=jnp.float32)
    mid_partial = jnp.einsum(
        "tf,df->td", grad_gate, gate_weight, preferred_element_type=jnp.float32
    )
    mid_partial = mid_partial + jnp.einsum(
        "tf,df->td", grad_up, up_weight, preferred_element_type=jnp.float32
    )
    grad_normed_two = lax.psum_scatter(mid_partial, "mp", scatter_dimension=0, tiled=True)
    scaled_two = grad_normed_two * gain_two
    ffn_gain_part = jnp.sum(grad_normed_two * middle * inverse_two, axis=0)
    grad_middle = (
        grad_out
        + inverse_two * scaled_two
        - middle * inverse_two**3 * jnp.mean(scaled_two * middle, axis=-1, keepdims=True)
    )
    grad_attn_all = lax.all_gather(grad_middle.astype(jnp.bfloat16), "mp", axis=0, tiled=True)

    def backward_item(carried, item_index):
        input_partial, kv_partial, q_grad_w, o_grad_w = carried
        head_index, block_index, seq_start, row_start = item_info(item_index)
        queries = kept_queries[item_index]
        output = kept_outputs[item_index]
        log_total = kept_totals[item_index]
        grad_rows = lax.dynamic_slice(grad_attn_all, (row_start, 0), (QBLOCK, model_width))
        weight_o = lax.dynamic_slice(out_full, (head_index * HEAD_DIM, 0), (HEAD_DIM, model_width))
        grad_output = jnp.einsum(
            "td,hd->th", grad_rows, weight_o, preferred_element_type=jnp.float32
        ).astype(jnp.bfloat16)
        o_grad_w = add_window(
            o_grad_w,
            jnp.einsum("th,td->hd", output, grad_rows, preferred_element_type=jnp.float32),
            head_index * HEAD_DIM,
            0,
        )
        kv_head = head_index // group_size
        grad_queries, grad_keys, grad_values = lax.switch(
            block_index, backward_list, queries, grad_output, log_total, kv_all, seq_start, kv_head
        )
        cosine, sine_part = rotation(block_index * QBLOCK + jnp.arange(QBLOCK))
        grad_raw = rotate_back(grad_queries, cosine, sine_part).astype(jnp.bfloat16)
        rows_in = lax.dynamic_slice(normed_all, (row_start, 0), (QBLOCK, model_width))
        weight_q = lax.dynamic_slice(qkv_full, (0, head_index * HEAD_DIM), (model_width, HEAD_DIM))
        input_partial = add_window(
            input_partial,
            jnp.einsum("th,dh->td", grad_raw, weight_q, preferred_element_type=jnp.float32),
            row_start,
            0,
        )
        q_grad_w = add_window(
            q_grad_w,
            jnp.einsum("td,th->dh", rows_in, grad_raw, preferred_element_type=jnp.float32),
            0,
            head_index * HEAD_DIM,
        )
        kv_partial = add_window(kv_partial, grad_keys, seq_start, kv_head * HEAD_DIM)
        kv_partial = add_window(kv_partial, grad_values, seq_start, (KV_HEADS + kv_head) * HEAD_DIM)
        return ((input_partial, kv_partial, q_grad_w, o_grad_w), None)

    start_state = (
        jnp.zeros((group_rows, model_width), jnp.float32),
        jnp.zeros((group_rows, 2 * kv_width), jnp.float32),
        jnp.zeros((model_width, q_width), jnp.float32),
        jnp.zeros((q_width, model_width), jnp.float32),
    )
    (input_partial, kv_partial, q_grad_w, o_grad_w), unused = lax.scan(
        backward_item, start_state, jnp.arange(count_items)
    )
    input_sum, kv_sum = (
        lax.psum_scatter(input_partial, "mp", scatter_dimension=0, tiled=True),
        lax.psum_scatter(kv_partial, "mp", scatter_dimension=0, tiled=True),
    )
    cos_local, sin_local = rotation(local_pos)
    grad_keys_local = rotate_back(
        kv_sum[:, :kv_width].reshape(tok_dev, KV_HEADS, HEAD_DIM),
        cos_local[:, None, :],
        sin_local[:, None, :],
    )
    grad_kv = jnp.concatenate(
        [grad_keys_local.reshape(tok_dev, kv_width), kv_sum[:, kv_width:]], axis=1
    ).astype(jnp.bfloat16)
    grad_normed_one = input_sum + jnp.einsum(
        "tk,dk->td", grad_kv, weight_kv, preferred_element_type=jnp.float32
    )
    kv_grad_w = jnp.einsum("td,tk->dk", normed_one, grad_kv, preferred_element_type=jnp.float32)
    qkv_grad_full = jnp.concatenate([q_grad_w, kv_grad_w], axis=1)
    scaled_one = grad_normed_one * gain_one
    attn_gain_part = jnp.sum(grad_normed_one * residual * inverse_one, axis=0)
    input_grad = (
        grad_middle
        + inverse_one * scaled_one
        - residual * inverse_one**3 * jnp.mean(scaled_one * residual, axis=-1, keepdims=True)
    )
    qkv_grad, proj_grad, attn_gain_grad, ffn_gain_grad = (
        lax.psum_scatter(qkv_grad_full, ("rows", "mp"), scatter_dimension=0, tiled=True),
        lax.psum_scatter(o_grad_w, ("rows", "mp"), scatter_dimension=0, tiled=True),
        lax.psum_scatter(attn_gain_part, ("rows", "mp"), scatter_dimension=0, tiled=True),
        lax.psum_scatter(ffn_gain_part, ("rows", "mp"), scatter_dimension=0, tiled=True),
    )
    gate_grad, up_grad, down_grad = (
        lax.psum(gate_grad.astype(jnp.bfloat16), "rows").astype(jnp.float32),
        lax.psum(up_grad.astype(jnp.bfloat16), "rows").astype(jnp.float32),
        lax.psum(down_grad.astype(jnp.bfloat16), "rows").astype(jnp.float32),
    )
    return (
        outputs,
        input_grad,
        qkv_grad,
        proj_grad,
        gate_grad,
        up_grad,
        down_grad,
        attn_gain_grad,
        ffn_gain_grad,
    )


def solution(mesh):
    in_specs = (
        P(("rows", "mp"), None),
        P(("rows", "mp"), None),
        P("rows"),
        P(),
        P(("rows", "mp")),
        P(("rows", "mp"), None),
        P(("rows", "mp"), None),
        P(("rows", "mp")),
        P(None, "mp"),
        P(None, "mp"),
        P("mp", None),
    )
    out_specs = (
        P(("rows", "mp"), None),
        P(("rows", "mp"), None),
        P(("rows", "mp"), None),
        P(("rows", "mp"), None),
        P(None, "mp"),
        P(None, "mp"),
        P("mp", None),
        P(("rows", "mp")),
        P(("rows", "mp")),
    )
    return jax.shard_map(
        on_device, mesh=mesh, in_specs=in_specs, out_specs=out_specs, check_vma=False
    )
```

profile of v0, /device:TPU:0, one launch (start us, length us, event | category | flops | bytes accessed | tf_op | source)
XLA Modules:
  0.0 2238.0 jit_solution(10643275704402246868)
XLA Ops:
  10.4 43.2 %all-reduce.11 = (bf16[2048]{0:T(1024)(128)(2,1)S(1)}, bf16[2048]{0:T(1024)(128)(2,1)S(1)}) all-reduce(bf16[2048]{0:T(1024)(128)(2,1)S(1)} %dynamic-update-slice, bf16[2048]{0:T(1024)(128)(2,1)S(1)} %dynamic-update-slice.1), channel_id=1, replica_groups=mesh['rows'=4,'mp'=8] {'rows','mp'}, use_global_device_ids=true, to_apply=%add.6 | all-reduce | flops 4096 | bytes 16384
  59.7 29.9 %all-gather.10.cloned.1.call-done = bf16[2048,1920]{1,0:T(8,128)(2,1)} async-done(((bf16[64,1920]{1,0:T(8,128)(2,1)}), bf16[2048,1920]{1,0:T(8,128)(2,1)}) %all-gather.10.cloned.1.call-update) | async-done | bytes 7864336 | tf_op jit(solution)/shard_map/all_gather | solution.py:158
  97.7 58.8 %all-gather.14.cloned.1.call-done = bf16[1280,2048]{1,0:T(8,128)(2,1)} async-done(((bf16[40,2048]{1,0:T(8,128)(2,1)}), bf16[1280,2048]{1,0:T(8,128)(2,1)}) %all-gather.14.cloned.1.call-update) | async-done | bytes 5242896 | tf_op jit(solution)/shard_map/all_gather | solution.py:159
  156.5 82.6 %all-gather.8.cloned.1.call-done = bf16[2048,2048]{1,0:T(8,128)(2,1)} async-done(((bf16[256,2048]{1,0:T(8,128)(2,1)}), bf16[2048,2048]{1,0:T(8,128)(2,1)}) %all-gather.8.cloned.1.call-update) | async-done | bytes 8388624 | tf_op jit(solution)/shard_map/all_gather | solution.py:171
  239.1 34.5 %all-gather.12.cloned.1.call-done = bf16[2048,640]{1,0:T(8,128)(2,1)} async-done(((bf16[256,640]{1,0:T(8,128)(2,1)}), bf16[2048,640]{1,0:T(8,128)(2,1)}) %all-gather.12.cloned.1.call-update) | async-done | bytes 2621456 | tf_op jit(solution)/shard_map/all_gather | solution.py:172
  273.6 7.9 broadcast.482.clone
  281.5 150.9 %while.42 = (s32[]{:T(128)}, f32[2048,2048]{1,0:T(8,128)}, bf16[10,512,64]{1,2,0:T(8,128)(2,1)}, bf16[10,512,64]{1,2,0:T(8,128)(2,1)}, f32[10,512]{1,0:T(8,128)S...) while((s32[]{:T(128)}, f32[2048,2048]{1,0:T(8,128)}, ...), condition=%wide.region_14.15_spmd, body=%wide.region_1.14_spmd.sunk | while | flops 547767360 | bytes 25982072 | solution.py:204
  305.6 5.0 add_dynamic-update-slice_fusion.8
  314.9 5.5 conditional.17
  330.5 6.2 conditional.17
  375.8 5.5 conditional.17
  382.1 5.0 add_dynamic-update-slice_fusion.8
  391.4 6.2 conditional.17
  427.4 5.0 add_dynamic-update-slice_fusion.8
  432.5 169.8 %reduce-scatter.8.cloned.1.call-done = f32[256,2048]{1,0:T(8,128)} async-done(((f32[2048,2048]{1,0:T(8,128)}), f32[256,2048]{1,0:T(8,128)}) %reduce-scatter.8.cloned.1.call-update) | async-done | bytes 2097168 | tf_op jit(solution)/shard_map/reduce_scatter | solution.py:207
  607.7 9.9 psum.28
  622.9 64.7 %all-gather.16.cloned.1.call-done = bf16[2048,2048]{1,0:T(8,128)(2,1)} async-done(((bf16[256,2048]{1,0:T(8,128)(2,1)}), bf16[2048,2048]{1,0:T(8,128)(2,1)}) %all-gather.16.cloned.1.call-update) | async-done | bytes 8388624 | tf_op jit(solution)/shard_map/all_gather | solution.py:211
  687.6 11.8 fusion.167
  699.4 8.5 fusion.166
  707.9 62.5 %all-gather.18.cloned.1.call-done = bf16[2048,2048]{1,0:T(8,128)(2,1)} async-done(((bf16[256,2048]{1,0:T(8,128)(2,1)}), bf16[2048,2048]{1,0:T(8,128)(2,1)}) %all-gather.18.cloned.1.call-update) | async-done | bytes 8388624 | tf_op jit(solution)/shard_map/all_gather | solution.py:227
  770.4 15.7 multiply_convert_fusion.2
  786.1 13.3 fusion.168
  799.4 14.1 convolution_add_fusion.2
  813.6 10.8 convolution_convert_fusion
  824.5 156.0 %reduce-scatter.12.cloned.1.call-done = f32[256,2048]{1,0:T(8,128)} async-done(((f32[2048,2048]{1,0:T(8,128)}), f32[256,2048]{1,0:T(8,128)}) %reduce-scatter.12.cloned.1.call-update) | async-done | bytes 2097168 | tf_op jit(solution)/shard_map/reduce_scatter | solution.py:243
  983.3 87.6 %reduce-scatter.10.cloned.1.call-done = bf16[256,2048]{1,0:T(8,128)(2,1)} async-done(((bf16[2048,2048]{1,0:T(8,128)(2,1)}), bf16[256,2048]{1,0:T(8,128)(2,1)}) %reduce-scatter.10.cloned.1.call-update) | async-done | bytes 1048592 | tf_op jit(solution)/shard_map/reduce_scatter | solution.py:216
  1077.9 78.2 %all-gather.20.cloned.1.call-done = bf16[2048,2048]{1,0:T(8,128)(2,1)} async-done(((bf16[256,2048]{1,0:T(8,128)(2,1)}), bf16[2048,2048]{1,0:T(8,128)(2,1)}) %all-gather.20.cloned.1.call-update) | async-done | bytes 8388624 | tf_op jit(solution)/shard_map/all_gather | solution.py:251
  1159.1 5.2 broadcast_in_dim.139
  1164.3 5.3 broadcast_in_dim.138
  1169.6 7.9 broadcast.482
  1177.5 293.2 %while.43 = (s32[]{:T(128)}, f32[2048,2048]{1,0:T(8,128)}, f32[2048,640]{0,1:T(8,128)}, f32[2048,1280]{0,1:T(8,128)}, f32[1280,2048]{1,0:T(8,128)}, /*index=5*/s...) while((s32[]{:T(128)}, f32[2048,2048]{1,0:T(8,128)}, ...), condition=%wide.region_32.33_spmd, body=%wide.region_23.32_spmd.sunk | while | flops 1220625536 | bytes 55792484 | solution.py:300
  1183.3 6.6 conditional.18
  1200.1 5.1 add_dynamic-update-slice_fusion.9
  1210.8 7.9 conditional.18
  1229.0 5.2 add_dynamic-update-slice_fusion.9
  1239.8 9.2 conditional.18
  1259.2 5.1 add_dynamic-update-slice_fusion.9
  1270.0 10.5 conditional.18
  1290.7 5.1 add_dynamic-update-slice_fusion.9
  1301.4 6.6 conditional.18
  1318.2 5.1 add_dynamic-update-slice_fusion.9
  1329.0 7.9 conditional.18
  1347.1 5.2 add_dynamic-update-slice_fusion.9
  1357.9 9.2 conditional.18
  1377.3 5.1 add_dynamic-update-slice_fusion.9
  1388.1 10.5 conditional.18
  1408.8 5.1 add_dynamic-update-slice_fusion.9
  1419.5 6.6 conditional.18
  1436.3 5.1 add_dynamic-update-slice_fusion.9
  1447.1 7.9 conditional.18
  1465.3 5.2 add_dynamic-update-slice_fusion.9
  1470.7 12.2 convolution_convert_fusion.1
  1482.9 8.5 convolution_convert_fusion.2
  1491.4 8.5 convolution_convert_fusion.3
  1501.3 11.6 copy.61
  1512.9 21.2 reduce-scatter.16.cloned.1.call-done
  1540.1 6.3 pad_maximum_fusion.4
  1546.4 180.2 %all-reduce.15.cloned.1.call-done = (bf16[2048,768]{1,0:T(8,128)(2,1)}, bf16[2048,768]{1,0:T(8,128)(2,1)}, bf16[768,2048]{1,0:T(8,128)(2,1)}) async-done(((bf16[2048,768]{1,0:T(8,128)(2,1)}, bf16[2048,768]{1,0:T(8,128)(2,1)}, bf16[768,2048]{1,0:T(8,128)(2,1)}), (bf16[2048,768]{1,0:T(8,128)(2,1)}, bf16[2048,768]{1,0:T(8,128)(2,1)}, bf16[768,2048]{1,0:T(8,128)(2,1)})) %all-reduce.15.cloned.1.call-update) | async-done | bytes 9437200 | tf_op jit(solution)/shard_map/psum | solution.py:335
  1726.6 5.2 convert_element_type.262
  1739.3 158.0 %reduce-scatter.14.cloned.1.call-done = f32[256,2048]{1,0:T(8,128)} async-done(((f32[2048,2048]{1,0:T(8,128)}), f32[256,2048]{1,0:T(8,128)}) %reduce-scatter.14.cloned.1.call-update) | async-done | bytes 2097168 | tf_op jit(solution)/shard_map/reduce_scatter | solution.py:304
  1897.2 5.1 fusion.153
  1902.3 38.8 %all-reduce.10 = (f32[2048]{0:T(1024)S(1)}, f32[2048]{0:T(1024)S(1)}) all-reduce(f32[2048]{0:T(1024)S(1)} %get-tuple-element.1396, f32[2048]{0:T(1024)S(1)} %copy-done.14), channel_id=9, replica_groups=mesh['rows'=4,'mp'=8] {'rows','mp'}, use_global_device_ids=true, to_apply=%region_42.43.clone | all-reduce | flops 4096 | bytes 32768
  1947.0 109.4 %reduce-scatter.20.cloned.1.call-done = f32[40,2048]{1,0:T(8,128)} async-done(((f32[1280,2048]{1,0:T(8,128)}), f32[40,2048]{1,0:T(8,128)}) %reduce-scatter.20.cloned.1.call-update) | async-done | bytes 327696 | tf_op jit(solution)/shard_map/reduce_scatter | solution.py:330
  2056.3 174.8 %reduce-scatter.18.cloned.1.call-done = f32[64,1920]{1,0:T(8,128)} async-done(((f32[2048,1920]{1,0:T(8,128)}), f32[64,1920]{1,0:T(8,128)}) %reduce-scatter.18.cloned.1.call-update) | async-done | bytes 491536 | tf_op jit(solution)/shard_map/reduce_scatter | solution.py:329
  (466 shorter events, 428.6 us)
Async XLA Ops:
  7.2 763.2 %copy-start = (bf16[768,2048]{1,0:T(8,128)(2,1)S(1)}, bf16[768,2048]{1,0:T(8,128)(2,1)}, u32[]{:S(2)}) copy-start(bf16[768,2048]{1,0:T(8,128)(2,1)} %param.33) | copy-start | bytes 9437188
  7.2 82.5 %all-gather.10.cloned.1.call-start = ((), (), s32[]{:S(2)}) async-start(), calls=%async_computation.8 | async-start | bytes 8110080 | tf_op jit(solution)/shard_map/all_gather | solution.py:158
  7.9 148.6 %all-gather.14.cloned.1.call-start = ((), (), s32[]{:S(2)}) async-start(), calls=%async_computation.10 | async-start | bytes 5406720 | tf_op jit(solution)/shard_map/all_gather | solution.py:159
  8.7 230.4 %all-gather.8.cloned.1.call-start = ((), (), s32[]{:S(2)}) async-start(), calls=%async_computation.7 | async-start | bytes 9437184 | tf_op jit(solution)/shard_map/all_gather | solution.py:171
  53.6 2.1 copy-start.12
  55.7 0.5 copy-start.15
  58.8 214.7 %all-gather.12.cloned.1.call-start = ((), (), s32[]{:S(2)}) async-start(), calls=%async_computation.9 | async-start | bytes 2949120 | tf_op jit(solution)/shard_map/all_gather | solution.py:172
  97.4 504.8 %reduce-scatter.8.cloned.1.call-start = ((), (), s32[]{:S(2)}) async-start(), calls=%async_computation.11 | async-start | bytes 18874368 | tf_op jit(solution)/shard_map/reduce_scatter | solution.py:207
  432.4 255.2 %all-gather.16.cloned.1.call-start = ((), (), s32[]{:S(2)}) async-start(), calls=%async_computation.12 | async-start | bytes 9437184 | tf_op jit(solution)/shard_map/all_gather | solution.py:211
  604.5 1.3 copy-start.3
  604.5 13.1 copy-start.23
  607.0 163.4 %all-gather.18.cloned.1.call-start = ((), (), s32[]{:S(2)}) async-start(), calls=%async_computation.14 | async-start | bytes 9437184 | tf_op jit(solution)/shard_map/all_gather | solution.py:227
  622.7 357.9 %reduce-scatter.12.cloned.1.call-start = ((), (), s32[]{:S(2)}) async-start(), calls=%async_computation.15 | async-start | bytes 18874368 | tf_op jit(solution)/shard_map/reduce_scatter | solution.py:243
  687.6 11.8 copy-start.18
  687.6 11.8 copy-start.20
  770.4 15.7 copy-start.21
  786.1 13.3 copy-start.24
  786.1 13.3 copy-start.22
  813.6 257.2 %reduce-scatter.10.cloned.1.call-start = ((), (), s32[]{:S(2)}) async-start(), calls=%async_computation.13 | async-start | bytes 9437184 | tf_op jit(solution)/shard_map/reduce_scatter | solution.py:216
  824.4 156.1 %copy-start.4 = (f32[256,2048]{1,0:T(8,128)S(1)}, f32[256,2048]{1,0:T(8,128)}, u32[]{:S(2)}) copy-start(f32[256,2048]{1,0:T(8,128)} %copy-done.3) | copy-start | bytes 6291460
  824.5 246.3 %copy-start.7 = (bf16[256,2048]{1,0:T(8,128)(2,1)S(1)}, bf16[256,2048]{1,0:T(8,128)(2,1)}, u32[]{:S(2)}) copy-start(bf16[256,2048]{1,0:T(8,128)(2,1)} %param.24) | copy-start | bytes 3145732
  824.5 331.6 %all-gather.20.cloned.1.call-start = ((), (), s32[]{:S(2)}) async-start(), calls=%async_computation.16 | async-start | bytes 9437184 | tf_op jit(solution)/shard_map/all_gather | solution.py:251
  1075.5 458.6 %reduce-scatter.16.cloned.1.call-start = ((), (), s32[]{:S(2)}) async-start(), calls=%async_computation.18 | async-start | bytes 5898240 | tf_op jit(solution)/shard_map/reduce_scatter | solution.py:305
  1470.7 12.2 copy-start.25
  1470.7 255.9 %all-reduce.15.cloned.1.call-start = ((), (), s32[]{:S(2)}) async-start(), calls=%async_computation.21 | async-start | bytes 18874368 | tf_op jit(solution)/shard_map/psum | solution.py:335
  1470.7 12.2 copy-start.19
  1482.9 8.5 copy-start.26
  1499.9 397.3 %reduce-scatter.14.cloned.1.call-start = ((), (), s32[]{:S(2)}) async-start(), calls=%async_computation.17 | async-start | bytes 18874368 | tf_op jit(solution)/shard_map/reduce_scatter | solution.py:304
  1500.7 555.7 %reduce-scatter.20.cloned.1.call-start = ((), (), s32[]{:S(2)}) async-start(), calls=%async_computation.20 | async-start | bytes 10813440 | tf_op jit(solution)/shard_map/reduce_scatter | solution.py:330
  1501.2 729.9 %reduce-scatter.18.cloned.1.call-start = ((), (), s32[]{:S(2)}) async-start(), calls=%async_computation.19 | async-start | bytes 16220160 | tf_op jit(solution)/shard_map/reduce_scatter | solution.py:329
  1501.3 34.8 %copy-start.10 = (f32[256,32]{0,1:T(8,128)S(1)}, f32[256,32]{0,1:T(8,128)}, u32[]{:S(2)}) copy-start(f32[256,32]{0,1:T(8,128)} %get-tuple-element.1491) | copy-start | bytes 98308
  1501.3 34.8 %copy-start.11 = (f32[256,32]{0,1:T(8,128)S(1)}, f32[256,32]{0,1:T(8,128)}, u32[]{:S(2)}) copy-start(f32[256,32]{0,1:T(8,128)} %get-tuple-element.1492) | copy-start | bytes 98308
  1501.3 34.9 %copy-start.6 = (bf16[256,2048]{1,0:T(8,128)(2,1)S(1)}, bf16[256,2048]{1,0:T(8,128)(2,1)}, u32[]{:S(2)}) copy-start(bf16[256,2048]{1,0:T(8,128)(2,1)} %fusion.148) | copy-start | bytes 3145732
  1536.1 4.0 copy-start.2
  1726.6 5.2 copy-start.9
  1731.8 3.9 copy-start.8
  1735.7 161.5 %copy-start.5 = (bf16[256,2048]{1,0:T(8,128)(2,1)S(1)}, bf16[256,2048]{1,0:T(8,128)(2,1)}, u32[]{:S(2)}) copy-start(bf16[256,2048]{1,0:T(8,128)(2,1)} %param.23) | copy-start | bytes 3145732
  1735.7 161.5 %copy-start.13 = (f32[2048]{0:T(1024)S(1)}, f32[2048]{0:T(1024)}, u32[]{:S(2)}) copy-start(f32[2048]{0:T(1024)} %copy-done.12) | copy-start | bytes 24580
  1735.7 161.5 %copy-start.16 = (f32[256]{0:T(256)S(1)}, f32[256]{0:T(256)}, u32[]{:S(2)}) copy-start(f32[256]{0:T(256)} %copy-done.15) | copy-start | bytes 3076
  1739.2 163.1 %copy-start.14 = (f32[2048]{0:T(1024)S(1)}, f32[2048]{0:T(1024)}, u32[]{:S(2)}) copy-start(f32[2048]{0:T(1024)} %get-tuple-element.1394) | copy-start | bytes 24580
  1739.3 203.1 %copy-start.17 = (f32[256]{0:T(256)S(1)}, f32[256]{0:T(256)}, u32[]{:S(2)}) copy-start(f32[256]{0:T(256)} %get-tuple-element.1493) | copy-start | bytes 3076
  1942.3 288.8 %copy-start.1 = (bf16[768,2048]{1,0:T(8,128)(2,1)S(1)}, bf16[768,2048]{1,0:T(8,128)(2,1)}, u32[]{:S(2)}) copy-start(bf16[768,2048]{1,0:T(8,128)(2,1)} %param.33) | copy-start | bytes 9437188
Sparse Core Ops, SparseCore 0:
  11.0 78.5 all-gather.9
  92.5 63.9 all-gather.13
  158.1 80.9 all-gather.7
  241.1 32.3 all-gather.11
  432.5 169.6 reduce-scatter.7
  607.1 80.4 all-gather.15
  689.8 80.5 all-gather.17
  813.7 166.7 reduce-scatter.11
  982.8 87.9 reduce-scatter.9
  1075.6 80.4 all-gather.19
  1470.8 63.3 reduce-scatter.15
  1538.4 188.0 all-reduce.14
  1728.9 168.2 reduce-scatter.13
  1899.9 156.3 reduce-scatter.19
  2062.8 168.3 reduce-scatter.17
where the time goes:
time: 2250 us; the launch traced here: 2240 us
  waiting for transfers between devices  1470 us (65%)
  matrix products  430 us (19%)
  other arithmetic  110 us (5%)
  blocking collectives  91.9 us (4%)
  local copies, waits for them, and re-layouts  82.2 us (4%)
  loops' own time  36 us (2%)
    psum x1, waiting for transfers between devices, on_device(): lax.psum(gate_grad.astype(jnp.bfloat16), 'rows').astype(jnp.float32)  180 us
    reduce_scatter x1, waiting for transfers between devices, on_device(): lax.psum_scatter(qkv_grad_full, ('rows', 'mp'), scatter_dimension=0, tile...  175 us
    reduce_scatter x1, waiting for transfers between devices, on_device(): lax.psum_scatter(attn_partial, 'mp', scatter_dimension=0, tiled=True)  170 us
    reduce_scatter x1, waiting for transfers between devices, on_device(): lax.psum_scatter(input_partial, 'mp', scatter_dimension=0, tiled=True)  158 us
    reduce_scatter x1, waiting for transfers between devices, on_device(): lax.psum_scatter(mid_partial, 'mp', scatter_dimension=0, tiled=True)  156 us
    reduce_scatter x1, waiting for transfers between devices, on_device(): lax.psum_scatter(o_grad_w, ('rows', 'mp'), scatter_dimension=0, tiled=True)  109 us
    reduce_scatter x1, waiting for transfers between devices, on_device(): lax.psum_scatter(ffn_part.astype(jnp.bfloat16), 'mp', scatter_dimension=0...  87.6 us
    all_gather x1, waiting for transfers between devices, on_device(): lax.all_gather(normed_one, 'mp', axis=0, tiled=True)  82.6 us
  transfers between devices with their start and end apart: 15, of which 15 were waited for; matrix products, arithmetic and copies ran while one was open for 6% of the time, Pallas kernels for 0%

commit v1 on v0

v1 whole, which is shorter than its diff:
```python
import functools

import jax
import jax.numpy as jnp
from jax import lax
from jax.experimental import pallas as pl
from jax.experimental.pallas import tpu as pltpu
from jax.sharding import PartitionSpec as P

HEADS = 20
KV_HEADS = 5
HEAD_DIM = 64
GROUP = HEADS // KV_HEADS
Q_WIDTH = HEADS * HEAD_DIM
KV_WIDTH = KV_HEADS * HEAD_DIM
LEN = 2048
BLOCK = 128
KTILE = 256
EPS = 1e-05
THETA = 10000.0
LANES = GROUP * BLOCK
SLAB = 2 * HEAD_DIM

MESH = pl.DeviceIdType.MESH
F32 = jnp.float32
BF16 = jnp.bfloat16
VMEM_LIMIT = 62 * 1024 * 1024


def rope_tables(positions):
    half_dim = HEAD_DIM // 2
    freqs = jnp.exp(-jnp.log(THETA) * (2.0 * jnp.arange(half_dim, dtype=F32)) / HEAD_DIM)
    angles = positions.astype(F32)[:, None] * freqs[None, :]
    cosine, sine = jnp.cos(angles), jnp.sin(angles)
    ones, zeros = jnp.ones_like(cosine), jnp.zeros_like(cosine)
    head_cos = jnp.concatenate([cosine, cosine], axis=1)
    head_sin = jnp.concatenate([-sine, sine], axis=1)
    cos_q = jnp.concatenate([head_cos, head_cos], axis=1)
    sin_q = jnp.concatenate([head_sin, head_sin], axis=1)
    cos_kv = jnp.concatenate([head_cos, ones, ones], axis=1)
    sin_kv = jnp.concatenate([head_sin, zeros, zeros], axis=1)
    return (cos_q, sin_q, cos_kv, sin_kv)


def swap_halves(slab):
    lane = lax.broadcasted_iota(jnp.int32, slab.shape, 1)
    half_dim = HEAD_DIM // 2
    up = pltpu.roll(slab, SLAB - half_dim, 1)
    down = pltpu.roll(slab, half_dim, 1)
    return jnp.where(lane % HEAD_DIM < half_dim, up, down)


def qkv_kernel(x_ref, gain_ref, w_ref, cos_q, sin_q, cos_kv, sin_kv, normed_ref, inv_ref, q_ref, kv_ref):
    x = x_ref[...].astype(F32)
    inverse = lax.rsqrt(jnp.mean(x * x, axis=-1, keepdims=True) + EPS)
    normed = (x * inverse * gain_ref[...]).astype(BF16)
    normed_ref[...] = normed
    inv_ref[...] = inverse
    for s in range(Q_WIDTH // 256):
        part = jnp.dot(normed, w_ref[:, s * 256 : (s + 1) * 256], preferred_element_type=F32)
        for t in range(2):
            slab = part[:, t * SLAB : (t + 1) * SLAB]
            col = s * 256 + t * SLAB
            turned = slab * cos_q[...] + swap_halves(slab) * sin_q[...]
            q_ref[:, col : col + SLAB] = (turned.astype(BF16).astype(F32) * HEAD_DIM ** (-0.5)).astype(BF16)
    part = jnp.dot(normed, w_ref[:, Q_WIDTH : Q_WIDTH + 2 * KV_WIDTH], preferred_element_type=F32)
    for g in range(KV_HEADS):
        slab = part[:, g * SLAB : (g + 1) * SLAB]
        turned = slab * cos_kv[...] + swap_halves(slab) * sin_kv[...]
        kv_ref[:, g * SLAB : (g + 1) * SLAB] = turned.astype(BF16)


def qkv_project(x, gain, weight, tables):
    rows, width = x.shape
    return pl.pallas_call(
        qkv_kernel,
        out_shape=(
            jax.ShapeDtypeStruct((rows, width), BF16),
            jax.ShapeDtypeStruct((rows, 1), F32),
            jax.ShapeDtypeStruct((rows, Q_WIDTH), BF16),
            jax.ShapeDtypeStruct((rows, 2 * KV_WIDTH), BF16),
        ),
        compiler_params=pltpu.CompilerParams(vmem_limit_bytes=VMEM_LIMIT),
        name="qkv_project",
    )(x, gain, weight, *tables)


def heads_to_lanes(rows_part):
    turned = rows_part.T
    return jnp.concatenate(
        [turned[h * HEAD_DIM : (h + 1) * HEAD_DIM, :] for h in range(GROUP)], axis=1
    )


def lanes_to_heads(lanes_part):
    stacked = jnp.concatenate(
        [lanes_part[:, h * BLOCK : (h + 1) * BLOCK] for h in range(GROUP)], axis=0
    )
    return stacked.T


def causal(tile, block):
    key_pos = tile * KTILE + lax.broadcasted_iota(jnp.int32, (KTILE, LANES), 0)
    query_pos = block * BLOCK + lax.broadcasted_iota(jnp.int32, (KTILE, LANES), 1) % BLOCK
    return key_pos <= query_pos


def over_rows(left, right):
    return lax.dot_general(left, right, (((0,), (0,)), ((), ())), preferred_element_type=F32)


def attend_kernel(block_ref, q_ref, kv_ref, o_ref, total_ref):
    subs = q_ref.shape[0] // BLOCK
    for sub in range(subs):
        block = block_ref[sub]
        queries = heads_to_lanes(q_ref[sub * BLOCK : (sub + 1) * BLOCK, :].astype(F32))
        queries = jnp.concatenate([queries, jnp.zeros_like(queries)], axis=0).astype(BF16)

        def step(tile, carry, masked):
            top, total, acc = carry
            kv = kv_ref[pl.ds(pl.multiple_of(tile * KTILE, KTILE), KTILE), :]
            scores = jnp.dot(kv, queries, preferred_element_type=F32)
            if masked:
                scores = jnp.where(causal(tile, block), scores, -1e30)
            new_top = jnp.maximum(top, jnp.max(scores, axis=0, keepdims=True))
            decay = jnp.exp(top - new_top)
            probs = jnp.exp(scores - new_top)
            total = decay * total + jnp.sum(probs, axis=0, keepdims=True)
            acc = decay * acc + over_rows(kv, probs.astype(BF16))
            return (new_top, total, acc)

        start = (
            jnp.full((1, LANES), -1e30, F32),
            jnp.zeros((1, LANES), F32),
            jnp.zeros((SLAB, LANES), F32),
        )
        full = block * BLOCK // KTILE
        carry = lax.fori_loop(0, full, lambda t, c: step(t, c, False), start)
        top, total, acc = step(full, carry, True)
        out = acc[HEAD_DIM:, :] / total
        o_ref[sub * BLOCK : (sub + 1) * BLOCK, :] = lanes_to_heads(out).astype(BF16)
        total_ref[sub : sub + 1, :] = top + jnp.log(total)


def attend(blocks, q, kv_all):
    rows = q.shape[0]
    subs = rows // BLOCK
    return pl.pallas_call(
        attend_kernel,
        grid_spec=pltpu.PrefetchScalarGridSpec(
            num_scalar_prefetch=1,
            grid=(KV_HEADS,),
            in_specs=[
                pl.BlockSpec((rows, GROUP * HEAD_DIM), lambda g, b: (0, g)),
                pl.BlockSpec((LEN, SLAB), lambda g, b: (0, g)),
            ],
            out_specs=[
                pl.BlockSpec((rows, GROUP * HEAD_DIM), lambda g, b: (0, g)),
                pl.BlockSpec((None, subs, LANES), lambda g, b: (g, 0, 0)),
            ],
        ),
        out_shape=(
            jax.ShapeDtypeStruct((rows, Q_WIDTH), BF16),
            jax.ShapeDtypeStruct((KV_HEADS, subs, LANES), F32),
        ),
        compiler_params=pltpu.CompilerParams(vmem_limit_bytes=VMEM_LIMIT),
        cost_estimate=pl.CostEstimate(
            flops=60_000_000_000, bytes_accessed=8_000_000, transcendentals=6_000_000
        ),
        name="attend",
    )(blocks, q, kv_all)


def block_of(device, sub, subs):
    if subs == 2:
        return 2 * device if sub == 0 else 2 * lax.axis_size("mp") - 1 - 2 * device
    return subs * device + sub


def attend_back_kernel(
    q_ref,
    kv_ref,
    o_ref,
    do_ref,
    total_ref,
    cos_q,
    sin_q,
    cos_kv,
    sin_kv,
    grad_ref,
    dkv_acc,
    own_part,
    twin_out,
    twin_in,
    sum_out,
    sum_in,
    mine,
    twin_send,
    twin_recv,
    sum_send,
    sum_recv,
):
    subs = q_ref.shape[0] // BLOCK
    chips = lax.axis_size("mp") // 2
    me = lax.axis_index("mp")
    row = lax.axis_index("rows")
    chip = me // 2
    core = me % 2
    twin = (row, me + 1 - 2 * core)
    width = GROUP * HEAD_DIM

    barrier = pltpu.get_barrier_semaphore()
    pl.semaphore_signal(barrier, inc=1, device_id=twin, device_id_type=MESH)
    for step in range(1, chips):
        pl.semaphore_signal(
            barrier,
            inc=1,
            device_id=(row, 2 * ((chip + step) % chips) + core),
            device_id_type=MESH,
        )
    pl.semaphore_wait(barrier, chips)

    def twin_copy(g):
        return pltpu.make_async_remote_copy(
            src_ref=twin_out.at[g % 2],
            dst_ref=twin_in.at[g],
            send_sem=twin_send.at[g % 2],
            recv_sem=twin_recv.at[g],
            device_id=twin,
            device_id_type=MESH,
        )

    def sum_copy(g, step):
        return pltpu.make_async_remote_copy(
            src_ref=sum_out.at[g, step - 1],
            dst_ref=sum_in.at[g, step - 1],
            send_sem=sum_send.at[g, step - 1],
            recv_sem=sum_recv.at[g, step - 1],
            device_id=(row, 2 * ((chip + step) % chips) + core),
            device_id_type=MESH,
        )

    def combine(g):
        twin_copy(g).wait_recv()
        for step in range(1, chips):
            goal = (chip + step) % chips
            sum_out[g, step - 1] = (
                own_part[g % 2, goal] + twin_in[g, goal].astype(F32)
            ).astype(BF16)
            sum_copy(g, step).start()
        mine[g] = own_part[g % 2, chip] + twin_in[g, chip].astype(F32)

    def head_step(g, _):
        cols = pl.ds(pl.multiple_of(g * width, width), width)
        pair = pl.ds(pl.multiple_of(g * SLAB, SLAB), SLAB)
        dkv_acc[...] = jnp.zeros_like(dkv_acc)
        for sub in range(subs):
            rows = slice(sub * BLOCK, (sub + 1) * BLOCK)
            block = block_of(me, sub, subs)
            queries = heads_to_lanes(q_ref[rows, cols].astype(F32))
            grads = heads_to_lanes(do_ref[rows, cols].astype(F32))
            outs = heads_to_lanes(o_ref[rows, cols].astype(F32))
            delta = jnp.sum(grads * outs, axis=0, keepdims=True)
            empty = jnp.zeros_like(queries)
            queries = jnp.concatenate([queries, empty], axis=0)
            grads = jnp.concatenate([empty, grads], axis=0)
            query_rows = queries.T.astype(BF16)
            grad_rows = grads.T.astype(BF16)
            queries = queries.astype(BF16)
            grads = grads.astype(BF16)
            log_total = total_ref[g, sub : sub + 1, :]

            def step(tile, dq, masked):
                keys = pl.ds(pl.multiple_of(tile * KTILE, KTILE), KTILE)
                kv = kv_ref[keys, pair]
                scores = jnp.dot(kv, queries, preferred_element_type=F32)
                probs = jnp.exp(scores - log_total)
                if masked:
                    probs = jnp.where(causal(tile, block), probs, 0.0)
                grad_probs = jnp.dot(kv, grads, preferred_element_type=F32)
                grad_scores = (probs * (grad_probs - delta)).astype(BF16)
                dkv_acc[keys, :] += jnp.dot(
                    grad_scores, query_rows, preferred_element_type=F32
                ) + jnp.dot(probs.astype(BF16), grad_rows, preferred_element_type=F32)
                return dq + over_rows(kv, grad_scores)

            full = block * BLOCK // KTILE
            dq = lax.fori_loop(
                0, full, lambda t, c: step(t, c, False), jnp.zeros((SLAB, LANES), F32)
            )
            dq = step(full, dq, True)
            dq = lanes_to_heads(dq[:HEAD_DIM, :]) * HEAD_DIM ** (-0.5)
            for t in range(width // SLAB):
                slab = dq[:, t * SLAB : (t + 1) * SLAB]
                turned = slab * cos_q[rows, :] - swap_halves(slab) * sin_q[rows, :]
                first = pl.multiple_of(g * width + t * SLAB, SLAB)
                grad_ref[rows, pl.ds(first, SLAB)] = turned.astype(BF16)

        @pl.when(g >= 2)
        def _():
            twin_copy(g - 2).wait_send()

        for goal in range(chips):
            for sub in range(subs):
                first = block_of(2 * goal + core, sub, subs) * BLOCK
                own_part[g % 2, goal, sub] = dkv_acc[pl.ds(pl.multiple_of(first, BLOCK), BLOCK), :]
                first = block_of(2 * goal + 1 - core, sub, subs) * BLOCK
                twin_out[g % 2, goal, sub] = dkv_acc[
                    pl.ds(pl.multiple_of(first, BLOCK), BLOCK), :
                ].astype(BF16)
        twin_copy(g).start()

        @pl.when(g >= 1)
        def _():
            combine(g - 1)

        return 0

    lax.fori_loop(0, KV_HEADS, head_step, 0)
    combine(KV_HEADS - 1)

    for g in range(KV_HEADS):
        total = mine[g]
        for step in range(1, chips):
            sum_copy(g, step).wait_recv()
            total = total + sum_in[g, step - 1].astype(F32)
        slab = total.reshape(subs * BLOCK, SLAB)
        turned = slab * cos_kv[...] - swap_halves(slab) * sin_kv[...]
        first = Q_WIDTH + g * SLAB
        grad_ref[:, first : first + SLAB] = turned.astype(BF16)
    for g in range(KV_HEADS):
        for step in range(1, chips):
            sum_copy(g, step).wait_send()
    for g in range(KV_HEADS - 2, KV_HEADS):
        twin_copy(g).wait_send()


def attend_back(q, kv_all, o, grad_o, totals, tables):
    rows = q.shape[0]
    subs = rows // BLOCK
    chips = lax.axis_size("mp") // 2
    vmem = pl.BlockSpec(memory_space=pltpu.VMEM)
    dma = pltpu.SemaphoreType.DMA
    part = (chips, subs, BLOCK, SLAB)
    return pl.pallas_call(
        attend_back_kernel,
        in_specs=[vmem] * 9,
        out_specs=vmem,
        out_shape=jax.ShapeDtypeStruct((rows, Q_WIDTH + 2 * KV_WIDTH), BF16),
        scratch_shapes=[
            pltpu.VMEM((LEN, SLAB), F32),
            pltpu.VMEM((2,) + part, F32),
            pltpu.VMEM((2,) + part, BF16),
            pltpu.VMEM((KV_HEADS,) + part, BF16),
            pltpu.VMEM((KV_HEADS, chips - 1) + part[1:], BF16),
            pltpu.VMEM((KV_HEADS, chips - 1) + part[1:], BF16),
            pltpu.VMEM((KV_HEADS,) + part[1:], F32),
            dma((2,)),
            dma((KV_HEADS,)),
            dma((KV_HEADS, chips - 1)),
            dma((KV_HEADS, chips - 1)),
        ],
        compiler_params=pltpu.CompilerParams(
            collective_id=3, has_side_effects=True, vmem_limit_bytes=VMEM_LIMIT
        ),
        cost_estimate=pl.CostEstimate(
            flops=120_000_000_000, bytes_accessed=12_000_000, transcendentals=6_000_000
        ),
        name="attend_back",
    )(q, kv_all, o, grad_o, totals, *tables)


def pack_kv(columns):
    lead = columns.shape[:-1]
    kv = columns[..., Q_WIDTH:].reshape(*lead, 2, KV_HEADS, HEAD_DIM)
    kv = jnp.swapaxes(kv, -3, -2).reshape(*lead, 2 * KV_WIDTH)
    return jnp.concatenate([columns[..., :Q_WIDTH], kv], axis=-1)


def unpack_kv(columns):
    lead = columns.shape[:-1]
    kv = columns[..., Q_WIDTH:].reshape(*lead, KV_HEADS, 2, HEAD_DIM)
    kv = jnp.swapaxes(kv, -3, -2).reshape(*lead, 2 * KV_WIDTH)
    return jnp.concatenate([columns[..., :Q_WIDTH], kv], axis=-1)


def dot(left, right):
    return jnp.dot(left, right, preferred_element_type=F32)


def dot_nt(left, right):
    return lax.dot_general(left, right, (((1,), (1,)), ((), ())), preferred_element_type=F32)


def dot_tn(left, right):
    return lax.dot_general(left, right, (((0,), (0,)), ((), ())), preferred_element_type=F32)


def half_of(ref, chip, core, sub, rows):
    tokens = ref.shape[0] // (lax.axis_size("mp") // 2)
    start = chip * tokens + core * (tokens // 2) + sub * rows
    return ref.at[pl.ds(pl.multiple_of(start, rows), rows)]


def ffn_kernel(
    subs,
    scale_ref,
    x_ref,
    cot_ref,
    gate_ref,
    up_ref,
    down_ref,
    part_ref,
    sum_ref,
    gate_out,
    up_out,
    down_out,
    x_all,
    hid,
    dgate,
    dup,
    cot_buf,
    part_buf,
    own_buf,
    twin_buf,
    twin_in,
    send_buf,
    sums_in,
    cot_cols,
    wide_buf,
    tall_buf,
    x_send,
    x_recv,
    twin_x_send,
    twin_x_recv,
    twin_send,
    twin_recv,
    sum_send,
    sum_recv,
    cot_sem,
    part_sem,
    cols_sem,
    out_sem,
):
    chips = lax.axis_size("mp") // 2
    me = lax.axis_index("mp")
    row = lax.axis_index("rows")
    chip = me // 2
    core = me % 2
    rows = x_ref.shape[0] // subs
    units = chips * subs
    twin = (row, me + 1 - 2 * core)

    def on_chip(other):
        return (row, 2 * other + core)

    barrier = pltpu.get_barrier_semaphore()
    pl.semaphore_signal(barrier, inc=1, device_id=twin, device_id_type=MESH)
    for step in range(1, chips):
        pl.semaphore_signal(
            barrier, inc=1, device_id=on_chip((chip + step) % chips), device_id_type=MESH
        )
    pl.semaphore_wait(barrier, chips)

    def order(i):
        near = jnp.minimum(chip, chips - 1 - chip)
        long_side = jnp.where(chip < chips - 1 - chip, 1, -1)
        j = i - subs
        paired = j < 2 * subs * near
        rest = j - 2 * subs * near
        dist = jnp.where(paired, j // (2 * subs) + 1, near + 1 + rest // subs)
        sub = jnp.where(paired, (j % (2 * subs)) // 2, rest % subs)
        side = jnp.where(paired, 1 - 2 * (j % 2), long_side)
        own = i < subs
        return (jnp.where(own, chip, chip + side * dist), jnp.where(own, i, sub))

    def x_copy(other, sub, side, source=None):
        spot = half_of(x_all, other, core, sub, rows)
        return pltpu.make_async_remote_copy(
            src_ref=spot if source is None else source,
            dst_ref=spot,
            send_sem=x_send.at[(side + 1) // 2, other * subs + sub],
            recv_sem=x_recv.at[other * subs + sub],
            device_id=on_chip(chip + side),
            device_id_type=MESH,
        )

    def twin_x_copy(other, sub, source=None):
        spot = half_of(x_all, other, core, sub, rows)
        return pltpu.make_async_remote_copy(
            src_ref=spot if source is None else source,
            dst_ref=spot,
            send_sem=twin_x_send.at[other * subs + sub],
            recv_sem=twin_x_recv.at[other * subs + sub],
            device_id=twin,
            device_id_type=MESH,
        )

    def twin_sum_copy(other, sub, slot):
        return pltpu.make_async_remote_copy(
            src_ref=twin_buf.at[slot],
            dst_ref=twin_in.at[other * subs + sub],
            send_sem=twin_send.at[slot],
            recv_sem=twin_recv.at[other * subs + sub],
            device_id=twin,
            device_id_type=MESH,
        )

    def sum_copy(other, sub):
        return pltpu.make_async_remote_copy(
            src_ref=send_buf.at[other * subs + sub],
            dst_ref=sums_in.at[(chip - other + chips) % chips - 1, sub],
            send_sem=sum_send.at[other * subs + sub],
            recv_sem=sum_recv.at[(chip - other + chips) % chips - 1, sub],
            device_id=on_chip(other),
            device_id_type=MESH,
        )

    def cot_copies(other, sub, slot):
        return [
            pltpu.make_async_copy(
                half_of(cot_ref, other, c, sub, rows),
                cot_buf.at[slot, pl.ds(c * rows, rows)],
                cot_sem.at[slot, c],
            )
            for c in range(2)
        ]

    def part_copies(other, sub, slot):
        return [
            pltpu.make_async_copy(
                part_buf.at[slot, pl.ds(c * rows, rows)],
                half_of(part_ref, other, c, sub, rows),
                part_sem.at[slot, c],
            )
            for c in range(2)
        ]

    for sub in range(subs):
        source = x_ref.at[pl.ds(sub * rows, rows)]

        @pl.when(chip < chips - 1)
        def _():
            x_copy(chip, sub, 1, source).start()

        @pl.when(chip > 0)
        def _():
            x_copy(chip, sub, -1, source).start()

        twin_x_copy(chip, sub, source).start()
    for copy in cot_copies(chip, 0, 0):
        copy.start()
    for sub in range(subs):
        half_of(x_all, chip, core, sub, rows)[...] = x_ref[sub * rows : (sub + 1) * rows, :]

    def reduce_unit(i):
        other, sub = order(i)
        unit = other * subs + sub
        twin_sum_copy(other, sub, i % 2).wait_recv()
        total = own_buf[i % 2] + twin_in[unit].astype(F32)

        @pl.when(other == chip)
        def _():
            sum_ref[pl.ds(pl.multiple_of(sub * rows, rows), rows), :] = total

        @pl.when(other != chip)
        def _():
            send_buf[unit] = total.astype(BF16)
            sum_copy(other, sub).start()

    def unit_step(i, _):
        other, sub = order(i)
        slot = i % 2

        @pl.when(i + 1 < units)
        def _():
            for copy in cot_copies(*order(i + 1), 1 - slot):
                copy.start()

        @pl.when(other != chip)
        def _():
            x_copy(other, sub, 1).wait_recv()
            twin_x_copy(other, sub).start()

            @pl.when((other > chip) & (chip > 0))
            def _():
                x_copy(other, sub, -1).start()

            @pl.when((other < chip) & (chip < chips - 1))
            def _():
                x_copy(other, sub, 1).start()

        twin_x_copy(other, sub).wait_recv()
        for copy in cot_copies(other, sub, slot):
            copy.wait()
        halves = [half_of(x_all, other, c, sub, rows)[...] for c in range(2)]
        x = jnp.concatenate(halves, axis=0)
        gate = dot(x, gate_ref[...])
        up = dot(x, up_ref[...])
        grad = dot_nt(cot_buf[slot], down_ref[...]) * scale_ref[0]
        sig = 1.0 / (1.0 + jnp.exp(-gate))
        act = gate * sig
        h = (act * up).astype(BF16)
        dg = (grad * up * (sig * (1.0 + gate * (1.0 - sig)))).astype(BF16)
        du = (grad * act).astype(BF16)
        for c in range(2):
            piece = slice(c * rows, (c + 1) * rows)
            half_of(hid, other, c, sub, rows)[...] = h[piece]
            half_of(dgate, other, c, sub, rows)[...] = dg[piece]
            half_of(dup, other, c, sub, rows)[...] = du[piece]

        @pl.when(i >= 2)
        def _():
            for copy in part_copies(*order(i - 2), slot):
                copy.wait()

        part_buf[slot] = dot(h, down_ref[...]).astype(BF16)
        for copy in part_copies(other, sub, slot):
            copy.start()

        @pl.when(i >= 2)
        def _():
            twin_sum_copy(*order(i - 2), slot).wait_send()

        dx = dot_nt(dg, gate_ref[...]) + dot_nt(du, up_ref[...])

        @pl.when(core == 0)
        def _():
            own_buf[slot] = dx[:rows]
            twin_buf[slot] = dx[rows:].astype(BF16)

        @pl.when(core == 1)
        def _():
            own_buf[slot] = dx[rows:]
            twin_buf[slot] = dx[:rows].astype(BF16)

        twin_sum_copy(other, sub, slot).start()

        @pl.when(i >= 1)
        def _():
            reduce_unit(i - 1)

        return 0

    lax.fori_loop(0, units, unit_step, 0)
    reduce_unit(units - 1)

    width = x_ref.shape[1]
    ff = gate_ref.shape[1]
    tall = tall_buf.shape[1]
    narrow = tall_buf.shape[2]
    down_cols = cot_cols.shape[2]
    col_steps = width // down_cols

    def cols_copy(j):
        return pltpu.make_async_copy(
            cot_ref.at[:, pl.ds(pl.multiple_of(j * down_cols, down_cols), down_cols)],
            cot_cols.at[j % 2],
            cols_sem.at[j % 2],
        )

    def wide_out(j):
        return pltpu.make_async_copy(
            wide_buf.at[j % 2],
            down_out.at[:, pl.ds(pl.multiple_of(j * down_cols, down_cols), down_cols)],
            out_sem.at[j % 2],
        )

    cols_copy(0).start()

    def down_step(j, _):
        @pl.when(j + 1 < col_steps)
        def _():
            cols_copy(j + 1).start()

        cols_copy(j).wait()

        @pl.when(j >= 2)
        def _():
            wide_out(j - 2).wait()

        wide_buf[j % 2] = (dot_tn(hid[...], cot_cols[j % 2]) * scale_ref[0]).astype(BF16)
        wide_out(j).start()
        return 0

    lax.fori_loop(0, col_steps, down_step, 0)
    for j in range(max(0, col_steps - 2), col_steps):
        wide_out(j).wait()

    pieces = width // tall
    steps = pieces * (ff // narrow)

    for source, target in ((dgate, gate_out), (dup, up_out)):

        def tall_out(j):
            first = pl.multiple_of(j % pieces * tall, tall)
            col = pl.multiple_of(j // pieces * narrow, narrow)
            return pltpu.make_async_copy(
                tall_buf.at[j % 2],
                target.at[pl.ds(first, tall), pl.ds(col, narrow)],
                out_sem.at[j % 2],
            )

        def tall_step(j, _):
            @pl.when(j >= 2)
            def _():
                tall_out(j - 2).wait()

            first = pl.multiple_of(j % pieces * tall, tall)
            col = pl.multiple_of(j // pieces * narrow, narrow)
            tall_buf[j % 2] = dot_tn(
                x_all[:, pl.ds(first, tall)], source[:, pl.ds(col, narrow)]
            ).astype(BF16)
            tall_out(j).start()
            return 0

        lax.fori_loop(0, steps, tall_step, 0)
        for j in range(steps - 2, steps):
            tall_out(j).wait()

    for sub in range(subs):
        total = sum_ref[sub * rows : (sub + 1) * rows, :]
        for step in range(1, chips):
            pltpu.make_async_remote_copy(
                src_ref=send_buf.at[0],
                dst_ref=sums_in.at[step - 1, sub],
                send_sem=sum_send.at[0],
                recv_sem=sum_recv.at[step - 1, sub],
                device_id=twin,
                device_id_type=MESH,
            ).wait_recv()
            total = total + sums_in[step - 1, sub].astype(F32)
        sum_ref[sub * rows : (sub + 1) * rows, :] = total

    def finish(i, _):
        other, sub = order(i)
        twin_x_copy(other, sub).wait_send()

        @pl.when(((other >= chip) & (chip > 0)))
        def _():
            x_copy(other, sub, -1).wait_send()

        @pl.when(((other <= chip) & (chip < chips - 1)))
        def _():
            x_copy(other, sub, 1).wait_send()

        @pl.when(other != chip)
        def _():
            sum_copy(other, sub).wait_send()

        @pl.when(i >= units - 2)
        def _():
            twin_sum_copy(other, sub, i % 2).wait_send()
            for copy in part_copies(other, sub, i % 2):
                copy.wait()

        return 0

    lax.fori_loop(0, units, finish, 0)


def ffn(scale, x, cot_all, gate_weight, up_weight, down_weight):
    tokens, width = cot_all.shape
    rows_dev = x.shape[0]
    chips = lax.axis_size("mp") // 2
    ff = gate_weight.shape[1]
    subs = max(1, rows_dev // BLOCK)
    rows = rows_dev // subs
    units = chips * subs
    narrow = ff // 3
    tall = 512
    down_cols = 512
    vmem = pl.BlockSpec(memory_space=pltpu.VMEM)
    hbm = pl.BlockSpec(memory_space=pl.ANY)
    dma = pltpu.SemaphoreType.DMA
    return pl.pallas_call(
        functools.partial(ffn_kernel, subs),
        out_shape=(
            jax.ShapeDtypeStruct((tokens, width), BF16),
            jax.ShapeDtypeStruct((rows_dev, width), F32),
            jax.ShapeDtypeStruct((width, ff), BF16),
            jax.ShapeDtypeStruct((width, ff), BF16),
            jax.ShapeDtypeStruct((ff, width), BF16),
        ),
        in_specs=[pl.BlockSpec(memory_space=pltpu.SMEM), vmem, hbm, vmem, vmem, vmem],
        out_specs=(hbm, vmem, hbm, hbm, hbm),
        scratch_shapes=[
            pltpu.VMEM((tokens, width), BF16),
            pltpu.VMEM((tokens, ff), BF16),
            pltpu.VMEM((tokens, ff), BF16),
            pltpu.VMEM((tokens, ff), BF16),
            pltpu.VMEM((2, 2 * rows, width), BF16),
            pltpu.VMEM((2, 2 * rows, width), BF16),
            pltpu.VMEM((2, rows, width), F32),
            pltpu.VMEM((2, rows, width), BF16),
            pltpu.VMEM((units, rows, width), BF16),
            pltpu.VMEM((units, rows, width), BF16),
            pltpu.VMEM((chips - 1, subs, rows, width), BF16),
            pltpu.VMEM((2, tokens, down_cols), BF16),
            pltpu.VMEM((2, ff, down_cols), BF16),
            pltpu.VMEM((2, tall, narrow), BF16),
            dma((2, units)),
            dma((units,)),
            dma((units,)),
            dma((units,)),
            dma((2,)),
            dma((units,)),
            dma((units,)),
            dma((chips - 1, subs)),
            dma((2, 2)),
            dma((2, 2)),
            dma((2,)),
            dma((2,)),
        ],
        compiler_params=pltpu.CompilerParams(
            collective_id=1, has_side_effects=True, vmem_limit_bytes=VMEM_LIMIT
        ),
        cost_estimate=pl.CostEstimate(
            flops=60_000_000_000, bytes_accessed=60_000_000, transcendentals=2_000_000
        ),
        name="ffn",
    )(scale.reshape(1), x, cot_all, gate_weight, up_weight, down_weight)


def reduce_kernel(heights, *refs):
    count = len(heights)
    lefts = refs[:count]
    rights = refs[count : 2 * count]
    gains = refs[2 * count]
    outs = refs[2 * count + 1 : 3 * count + 1]
    scratch = refs[3 * count + 1 :]
    per = 17
    chips = lax.axis_size("mp") // 2
    me = lax.axis_index("mp")
    row = lax.axis_index("rows")
    chip = me // 2
    core = me % 2
    down, across = row // 2, row % 2
    twin = (row, me + 1 - 2 * core)
    beside = (row + 1 - 2 * across, me)
    above = ((1 - down) * 2 + across, me)

    barrier = pltpu.get_barrier_semaphore()
    for device in (twin, beside, above):
        pl.semaphore_signal(barrier, inc=1, device_id=device, device_id_type=MESH)
    for step in range(1, chips):
        pl.semaphore_signal(
            barrier,
            inc=1,
            device_id=(row, 2 * ((chip + step) % chips) + core),
            device_id_type=MESH,
        )
    pl.semaphore_wait(barrier, chips + 2)

    streams = []
    for s in range(count):
        streams.append((heights[s], rights[s].shape[1], scratch[s * per : (s + 1) * per]))
    for s in range(count):
        turned = streams[s][2][0]
        turned[...] = lefts[s][...].T

    def target(i):
        return (chip + 1 + i) % chips

    def remote(source, dest, send, recv, device):
        return pltpu.make_async_remote_copy(
            src_ref=source,
            dst_ref=dest,
            send_sem=send,
            recv_sem=recv,
            device_id=device,
            device_id_type=MESH,
        )

    def copies(s, i):
        height, cols, bufs = streams[s]
        (_, own, twin_out, twin_in, out1, in1, out2, in2, out3, in3, s0, r0, s1, r1, s2, r2, s3) = bufs
        goal = target(i)
        return dict(
            twin=lambda: remote(twin_out.at[i], twin_in.at[i], s0.at[i], r0.at[i], twin),
            first=lambda d: remote(
                out1.at[i, d], in1.at[i, d], s1.at[i, d], r1.at[i, d], (beside, above)[d]
            ),
            second=lambda d: remote(
                out2.at[i, d], in2.at[i, d], s2.at[i, d], r2.at[i, d], (above, beside)[d]
            ),
            last=lambda: remote(
                out3.at[i], in3.at[i], s3.at[0, i], s3.at[1, i], (row, 2 * goal + core)
            ),
        )

    def make(s, i):
        height, cols, bufs = streams[s]
        turned, own, twin_out = bufs[:3]
        goal = target(i)
        for r in range(4):
            first = (r * chips + goal) * 2 * height
            lines = pl.ds(pl.multiple_of(first, 16), 2 * height)
            block = dot(turned[lines, :], rights[s][...])
            spare = cols_of(s) - block.shape[1]
            if spare:
                piece = gains[:, pl.ds(pl.multiple_of(first, 128), 2 * height)]
                piece = jnp.concatenate(
                    [piece, jnp.zeros((spare - piece.shape[0], 2 * height), F32)], axis=0
                ).T
                block = jnp.concatenate([block, piece], axis=1)

            @pl.when(core == 0)
            def _():
                own[i, r] = block[:height]
                twin_out[i, r] = block[height:].astype(BF16)

            @pl.when(core == 1)
            def _():
                own[i, r] = block[height:]
                twin_out[i, r] = block[:height].astype(BF16)

        copies(s, i)["twin"]().start()

    def cols_of(s):
        return streams[s][2][1].shape[-1]

    def first_stage(s, i):
        height, cols, bufs = streams[s]
        (_, own, twin_out, twin_in, out1, in1, out2, in2, out3, in3, s0, r0, s1, r1, s2, r2, s3) = bufs
        half = cols_of(s) // 2
        c = copies(s, i)
        c["twin"]().wait_recv()
        for r in range(4):
            own[i, r] = own[i, r] + twin_in[i, r].astype(F32)
        for k in range(2):
            out1[i, 0, k] = own[i, k * 2 + 1 - across, :, :half].astype(BF16)
            out1[i, 1, k] = own[i, (1 - down) * 2 + k, :, half:].astype(BF16)
        for d in range(2):
            c["first"](d).start()

    def second_stage(s, i):
        height, cols, bufs = streams[s]
        (_, own, twin_out, twin_in, out1, in1, out2, in2, out3, in3, s0, r0, s1, r1, s2, r2, s3) = bufs
        half = cols_of(s) // 2
        c = copies(s, i)
        for d in range(2):
            c["first"](d).wait_recv()
        other_down = (1 - down) * 2 + across
        other_across = down * 2 + 1 - across
        out2[i, 0] = (own[i, other_down, :, :half] + in1[i, 0, 1 - down].astype(F32)).astype(BF16)
        out2[i, 1] = (own[i, other_across, :, half:] + in1[i, 1, 1 - across].astype(F32)).astype(BF16)
        for d in range(2):
            c["second"](d).start()

    def third_stage(s, i):
        height, cols, bufs = streams[s]
        (_, own, twin_out, twin_in, out1, in1, out2, in2, out3, in3, s0, r0, s1, r1, s2, r2, s3) = bufs
        half = cols_of(s) // 2
        c = copies(s, i)
        for d in range(2):
            c["second"](d).wait_recv()
        left = own[i, row, :, :half] + in1[i, 0, down].astype(F32) + in2[i, 0].astype(F32)
        right = own[i, row, :, half:] + in1[i, 1, across].astype(F32) + in2[i, 1].astype(F32)

        @pl.when(i < chips - 1)
        def _():
            out3[i, :, :half] = left.astype(BF16)
            out3[i, :, half:] = right.astype(BF16)
            c["last"]().start()

        @pl.when(i == chips - 1)
        def _():
            outs[s][:, :half] = left
            outs[s][:, half:] = right

    def round_step(n, _):
        for stage, work in enumerate((make, first_stage, second_stage, third_stage)):

            @pl.when((n >= stage) & (n < chips + stage))
            def _():
                for s in range(count):
                    work(s, n - stage)

        return 0

    lax.fori_loop(0, chips + 3, round_step, 0)
    for s in range(count):
        in3 = streams[s][2][9]
        for i in range(chips - 1):
            copies(s, i)["last"]().wait_recv()
            outs[s][...] = outs[s][...] + in3[i].astype(F32)

    def finish(i, _):
        for s in range(count):
            c = copies(s, i)
            c["twin"]().wait_send()
            for d in range(2):
                c["first"](d).wait_send()
                c["second"](d).wait_send()

            @pl.when(i < chips - 1)
            def _():
                c["last"]().wait_send()

        return 0

    lax.fori_loop(0, chips, finish, 0)


def reduce_products(pairs, gains):
    chips = lax.axis_size("mp") // 2
    shards = lax.axis_size("rows") * lax.axis_size("mp")
    heights = tuple(left.shape[1] // shards for left, _ in pairs)
    dma = pltpu.SemaphoreType.DMA
    out_shape, scratch = [], []
    for s, (left, right) in enumerate(pairs):
        height = heights[s]
        cols = -(-right.shape[1] // 256) * 256
        half = cols // 2
        out_shape.append(jax.ShapeDtypeStruct((height, cols), F32))
        scratch += [
            pltpu.VMEM((left.shape[1], left.shape[0]), BF16),
            pltpu.VMEM((chips, 4, height, cols), F32),
            pltpu.VMEM((chips, 4, height, cols), BF16),
            pltpu.VMEM((chips, 4, height, cols), BF16),
            pltpu.VMEM((chips, 2, 2, height, half), BF16),
            pltpu.VMEM((chips, 2, 2, height, half), BF16),
            pltpu.VMEM((chips, 2, height, half), BF16),
            pltpu.VMEM((chips, 2, height, half), BF16),
            pltpu.VMEM((chips - 1, height, cols), BF16),
            pltpu.VMEM((chips - 1, height, cols), BF16),
            dma((chips,)),
            dma((chips,)),
            dma((chips, 2)),
            dma((chips, 2)),
            dma((chips, 2)),
            dma((chips, 2)),
            dma((2, chips)),
        ]
    vmem = pl.BlockSpec(memory_space=pltpu.VMEM)
    return pl.pallas_call(
        functools.partial(reduce_kernel, heights),
        out_shape=tuple(out_shape),
        in_specs=[vmem] * (2 * len(pairs) + 1),
        out_specs=(vmem,) * len(pairs),
        scratch_shapes=scratch,
        compiler_params=pltpu.CompilerParams(
            collective_id=2, has_side_effects=True, vmem_limit_bytes=VMEM_LIMIT
        ),
        cost_estimate=pl.CostEstimate(
            flops=50_000_000_000, bytes_accessed=10_000_000, transcendentals=0
        ),
        name="reduce_products",
    )(*[left for left, _ in pairs], *[right for _, right in pairs], gains)


def on_device(
    inputs,
    cotangent,
    corpus_ids,
    corpus_weight,
    attn_gain,
    qkv_weight,
    out_weight,
    ffn_gain,
    gate_weight,
    up_weight,
    down_weight,
):
    both = ("rows", "mp")
    rows_dev, width = inputs.shape
    mp = lax.axis_size("mp")
    me = lax.axis_index("mp")
    row_groups = lax.axis_size("rows")
    corpora = corpus_weight.shape[0]
    subs = rows_dev // BLOCK
    folded = subs == 2
    mirror = [(i, mp - 1 - i) for i in range(mp)]

    def fold(rows):
        if not folded:
            return rows
        return jnp.concatenate(
            [rows[:BLOCK], lax.ppermute(rows[BLOCK:], "mp", mirror)], axis=0
        )

    def to_order(gathered):
        if not folded:
            return gathered
        parts = gathered.reshape(mp, 2, BLOCK, gathered.shape[-1])
        return jnp.stack([parts[:, 0], parts[::-1, 1]], axis=1).reshape(gathered.shape)

    if folded:
        blocks = jnp.stack([2 * me, 2 * mp - 1 - 2 * me]).astype(jnp.int32)
    else:
        blocks = (subs * me + jnp.arange(subs)).astype(jnp.int32)
    positions = (blocks[:, None] * BLOCK + jnp.arange(BLOCK)[None, :]).reshape(-1)

    shard_rows = qkv_weight.shape[0]
    ident = jnp.broadcast_to(corpus_ids.astype(BF16)[:1, None], (shard_rows, 1))
    spare = (-(Q_WIDTH + 2 * KV_WIDTH + 3)) % 128
    shard = jnp.concatenate(
        [
            pack_kv(qkv_weight),
            attn_gain[:, None],
            ffn_gain[:, None],
            ident,
            jnp.zeros((shard_rows, spare), BF16),
        ],
        axis=1,
    )
    qkv_cols = Q_WIDTH + 2 * KV_WIDTH
    qkv_ext = lax.all_gather(shard, both, axis=0, tiled=True)
    qkv_full = qkv_ext[:, :qkv_cols]
    extras = qkv_ext[:, qkv_cols : qkv_cols + 3].astype(F32).T
    gain_one, gain_two = extras[0:1], extras[1:2]
    all_ids = extras[2].reshape(row_groups, -1)[:, 0]
    my_id = corpus_ids[0].astype(F32)
    count = jnp.sum((all_ids == my_id).astype(F32))
    weight_seq = jnp.sum(
        jnp.where(jnp.arange(corpora) == corpus_ids[0], corpus_weight, 0.0)
    )
    seq_scale = weight_seq * row_groups / (corpora * count)

    x = fold(inputs)
    cot = fold(cotangent)
    cot_all = lax.all_gather(cot, "mp", axis=0, tiled=True)
    out_full = lax.all_gather(out_weight, both, axis=0, tiled=True)
    tables = rope_tables(positions)
    normed_one, inverse_one, q, kv = qkv_project(x, gain_one, qkv_full, tables)
    kv_all = to_order(lax.all_gather(kv, "mp", axis=0, tiled=True))
    o, totals = attend(blocks, q, kv_all)

    residual = x.astype(F32)
    middle = residual + dot(o, out_full)
    inverse_two = lax.rsqrt(jnp.mean(middle * middle, axis=-1, keepdims=True) + EPS)
    normed_two = (middle * inverse_two * gain_two).astype(BF16)
    ffn_part, grad_normed_two, gate_grad, up_grad, down_grad = ffn(
        seq_scale, normed_two, cot_all, gate_weight, up_weight, down_weight
    )
    ffn_sum = lax.psum_scatter(ffn_part, "mp", scatter_dimension=0, tiled=True)

    grad_out = cot.astype(F32) * seq_scale
    scaled_two = grad_normed_two * gain_two
    ffn_gain_part = jnp.sum(grad_normed_two * middle * inverse_two, axis=0)
    grad_middle = (
        grad_out
        + inverse_two * scaled_two
        - middle * inverse_two**3 * jnp.mean(scaled_two * middle, axis=-1, keepdims=True)
    )
    grad_middle_low = grad_middle.astype(BF16)
    grad_o = dot_nt(grad_middle_low, out_full).astype(BF16)
    grad_qkv = attend_back(q, kv_all, o, grad_o, totals, tables)
    grad_normed_one = dot_nt(grad_qkv, qkv_full)
    scaled_one = grad_normed_one * gain_one
    attn_gain_part = jnp.sum(grad_normed_one * residual * inverse_one, axis=0)
    input_grad = (
        grad_middle
        + inverse_one * scaled_one
        - residual * inverse_one**3 * jnp.mean(scaled_one * residual, axis=-1, keepdims=True)
    )
    if folded:
        input_grad = jnp.concatenate(
            [
                input_grad[:BLOCK],
                lax.ppermute(input_grad[BLOCK:].astype(BF16), "mp", mirror).astype(F32),
            ],
            axis=0,
        )
    gain_parts = jnp.concatenate(
        [attn_gain_part[None], ffn_gain_part[None], jnp.zeros((6, width), F32)], axis=0
    )
    if row_groups == 4:
        part, proj_grad = reduce_products(
            ((normed_one, grad_qkv), (o, grad_middle_low)), gain_parts
        )
    else:
        part = jnp.concatenate(
            [dot_tn(normed_one, grad_qkv), gain_parts.T, jnp.zeros((width, 120), F32)], axis=1
        )
        part, proj_grad = (
            lax.psum_scatter(p.astype(BF16), both, scatter_dimension=0, tiled=True).astype(F32)
            for p in (part, dot_tn(o, grad_middle_low))
        )
    qkv_grad = unpack_kv(part[:, :qkv_cols])
    attn_gain_grad = part[:, qkv_cols]
    ffn_gain_grad = part[:, qkv_cols + 1]
    outputs = fold((middle + ffn_sum.astype(F32)).astype(BF16))
    gate_grad, up_grad, down_grad = (
        lax.psum(gate_grad, "rows"),
        lax.psum(up_grad, "rows"),
        lax.psum(down_grad, "rows"),
    )
    gate_grad, up_grad, down_grad, part, ffn_sum = lax.optimization_barrier(
        (gate_grad, up_grad, down_grad, part, ffn_sum)
    )
    gate_grad, up_grad, down_grad = (g.astype(F32) for g in (gate_grad, up_grad, down_grad))
    qkv_grad = unpack_kv(part[:, :qkv_cols])
    attn_gain_grad = part[:, qkv_cols]
    ffn_gain_grad = part[:, qkv_cols + 1]
    outputs = fold((middle + ffn_sum.astype(F32)).astype(BF16))
    return (
        outputs,
        input_grad,
        qkv_grad,
        proj_grad,
        gate_grad,
        up_grad,
        down_grad,
        attn_gain_grad,
        ffn_gain_grad,
    )


def solution(mesh):
    split = P(("rows", "mp"), None)
    line = P(("rows", "mp"))
    in_specs = (
        split,
        split,
        P("rows"),
        P(),
        line,
        split,
        split,
        line,
        P(None, "mp"),
        P(None, "mp"),
        P("mp", None),
    )
    out_specs = (
        split,
        split,
        split,
        split,
        P(None, "mp"),
        P(None, "mp"),
        P("mp", None),
        line,
        line,
    )
    return jax.shard_map(
        on_device, mesh=mesh, in_specs=in_specs, out_specs=out_specs, check_vma=False
    )
```

time: 2250 us -> 819 us (0.36)
  waiting for transfers between devices: 1470 us -> 369 us
  matrix products: 430 us -> 15.1 us
  Pallas kernels: 0 us -> 339 us
  blocking collectives: 91.9 us -> 0 us
  other arithmetic: 110 us -> 37.5 us
  local copies, waits for them, and re-layouts: 82.2 us -> 27.3 us
  loops' own time: 36 us -> 0 us
    reduce_scatter x7 -> x1, waiting for transfers between devices: 877 us -> 91.8 us  [on_device(): ffn_sum = lax.psum_scatter(ffn_part, 'mp', scatter_dimension=0, tiled=True)]
    dot_general x142 -> x3, matrix products: 430 us -> 15.1 us  [the longest x2 10.8 us: dot_nt(): lax.dot_general(left, right, (((1,), (1,)), ((), ())), preferred_element_...]
    pallas_call x0 -> x5, Pallas kernels: none -> 339 us  [the longest x1 151 us: ffn(): pl.pallas_call(functools.partial(ffn_kernel, subs), out_shape=(jax.ShapeD...]
    all_gather x7 -> x4, waiting for transfers between devices: 411 us -> 200 us  [the longest x1 76.1 us: on_device(): cot_all = lax.all_gather(cot, 'mp', axis=0, tiled=True)]
    psum x1, waiting for transfers between devices: 180 us -> 44.5 us  [on_device(): lax.psum(gate_grad, 'rows')]
    unnamed x2 -> x0, blocking collectives: 82 us -> none
    dynamic_update_slice x30 -> x0, other arithmetic: 46.2 us -> none  [the longest x20 39.4 us: add_window(): lax.dynamic_update_slice(target, current + update, (start_row, start_col))]
    another operation x12 -> x0, loops' own time: 35.5 us -> none  [the longest x1 27.2 us: on_device(): lax.scan(backward_item, start_state, jnp.arange(count_items))]
  transfers between devices with their start and end apart: 15 -> 10, of which waited for: 15 -> 8; matrix products, arithmetic and copies ran while one was open for 6% -> 6% of each run, Pallas kernels for 0% -> 22%
where the time goes in v1:
time: 819 us; the launch traced here: 812 us
  waiting for transfers between devices  369 us (45%)
  Pallas kernels  339 us (41%)
  other arithmetic  37.5 us (5%)
  local copies, waits for them, and re-layouts  27.3 us (3%)
  between operations  16.5 us (2%)
  matrix products  15.1 us (2%)
    pallas_call x1, Pallas kernels, ffn(): pl.pallas_call(functools.partial(ffn_kernel, subs), out_shape=(jax.ShapeD...  151 us
    pallas_call x1, Pallas kernels, reduce_products(): pl.pallas_call(functools.partial(reduce_kernel, heights), out_shape=tuple...  111 us
    reduce_scatter x1, waiting for transfers between devices, on_device(): ffn_sum = lax.psum_scatter(ffn_part, 'mp', scatter_dimension=0, tiled=True)  91.8 us
    all_gather x1, waiting for transfers between devices, on_device(): cot_all = lax.all_gather(cot, 'mp', axis=0, tiled=True)  76.1 us
    all_gather x1, waiting for transfers between devices, on_device(): qkv_ext = lax.all_gather(shard, both, axis=0, tiled=True)  66 us
    psum x1, waiting for transfers between devices, on_device(): lax.psum(gate_grad, 'rows')  44.5 us
    pallas_call x1, Pallas kernels, attend_back(): pl.pallas_call(attend_back_kernel, in_specs=[vmem] * 9, out_specs=vmem, o...  44.2 us
    all_gather x1, waiting for transfers between devices, on_device(): out_full = lax.all_gather(out_weight, both, axis=0, tiled=True)  35 us
  transfers between devices with their start and end apart: 10, of which 8 were waited for; matrix products, arithmetic and copies ran while one was open for 6% of the time, Pallas kernels for 22%

profile of v1, /device:TPU:0, one launch (start us, length us, event | category | flops | bytes accessed | tf_op | source)
XLA Modules:
  0.0 812.1 jit_solution(4556614901315724718)
XLA Ops:
  7.2 1.0 slice.73
  8.2 0.9 slice.72
  9.8 0.8 copy.27
  10.6 0.8 copy.28
  11.8 0.8 concatenate.50
  12.8 4.6 collective-permute-start
  17.4 0.7 broadcast_multiply_fusion.2
  18.3 0.5 fusion.8
  18.8 1.0 fusion.6
  19.9 12.0 %collective-permute-done = bf16[128,2048]{1,0:T(8,128)(2,1)S(1)} collective-permute-done((bf16[128,2048]{1,0:T(8,128)(2,1)S(1)}, bf16[128,2048]{1,0:T(8,128)(2,1)S(1)}, u32[]{:S(2)}, u32[]{:S(2)}) %collective-permute-start) | collective-permute-done | bytes 524320 | tf_op jit(solution)/shard_map/ppermute | solution.py:1080
  31.9 1.1 pad_maximum_fusion.2.x_ref
  33.0 66.0 %all-gather.5.cloned.1.call-done = bf16[2048,2048]{1,0:T(8,128)(2,1)} async-done(((bf16[64,2048]{1,0:T(8,128)(2,1)}), bf16[2048,2048]{1,0:T(8,128)(2,1)}) %all-gather.5.cloned.1.call-update) | async-done | bytes 8388624 | tf_op jit(solution)/shard_map/all_gather | solution.py:1109
  98.9 1.1 convert_bitcast_fusion
  100.0 1.5 slice_reduce_fusion.4
  101.5 0.9 copy.29.gain_ref
  102.5 6.9 slice.94.w_ref
  109.4 7.3 qkv_project.1
  116.8 0.7 all-gather.9.cloned.1.call-update
  117.6 1.8 collective-permute-start.1
  119.5 20.0 %collective-permute-done.1 = bf16[128,2048]{1,0:T(8,128)(2,1)S(1)} collective-permute-done((bf16[128,2048]{1,0:T(8,128)(2,1)S(1)}, bf16[128,2048]{1,0:T(8,128)(2,1)S(1)}, u32[]{:S(2)}, u32[]{:S(2)}) %collective-permute-start.1) | collective-permute-done | bytes 524320 | tf_op jit(solution)/shard_map/ppermute | solution.py:1080
  139.5 0.8 copy-done.14
  140.3 1.1 pad_maximum_fusion.3
  141.4 0.2 all-reduce.3.cloned.1.call-start
  141.6 0.6 fusion.9
  142.9 0.6 convert_reduce_fusion
  144.2 22.6 %all-gather.7.cloned.1.call-done = bf16[2048,640]{1,0:T(8,128)(2,1)} async-done(((bf16[256,640]{1,0:T(8,128)(2,1)}), bf16[2048,640]{1,0:T(8,128)(2,1)}) %all-gather.7.cloned.1.call-update) | async-done | bytes 2621456 | tf_op jit(solution)/shard_map/all_gather | solution.py:1127
  166.7 1.9 fusion.13
  168.7 1.2 rev.3
  169.8 3.1 pad_maximum_fusion
  172.9 25.7 %attend.1 = (bf16[256,1280]{1,0:T(8,128)(2,1)}, f32[5,2,512]{2,1,0:T(2,128)}) custom-call(s32[2]{0:T(128)} %get-tuple-element.62.block_ref, bf16[256,1280]{1,0:T(8,128)(2,1)} %get-tuple-element.27.q_ref, bf16[2048,640]{1,0:T(8,128)(2,1)} %bitcast.28), custom_call_target="tpu_custom_call" | custom-call | flops 60000002048 | bytes 8000000 | tf_op jit(solution)/shard_map/attend/pallas_call | solution.py:148
  198.6 35.0 %all-gather.9.cloned.1.call-done = bf16[1280,2048]{1,0:T(8,128)(2,1)} async-done(((bf16[40,2048]{1,0:T(8,128)(2,1)}), bf16[1280,2048]{1,0:T(8,128)(2,1)}) %all-gather.9.cloned.1.call-update) | async-done | bytes 5242896 | tf_op jit(solution)/shard_map/all_gather | solution.py:1124
  233.6 4.4 multiply_reduce_fusion.2
  238.0 1.3 copy-done
  239.3 1.2 multiply_convert_fusion.x_ref
  240.5 76.1 %all-gather.11.cloned.1.call-done.cot_ref = bf16[2048,2048]{1,0:T(8,128)(2,1)} async-done(((bf16[256,2048]{1,0:T(8,128)(2,1)}), bf16[2048,2048]{1,0:T(8,128)(2,1)}) %all-gather.11.cloned.1.call-update) | async-done | bytes 8388624 | tf_op jit(solution)/shard_map/all_gather | solution.py:1123
  316.6 150.8 %ffn.1 = (bf16[2048,2048]{1,0:T(8,128)(2,1)}, f32[256,2048]{1,0:T(8,128)}, bf16[2048,768]{1,0:T(8,128)(2,1)}, bf16[2048,768]{1,0:T(8,128)(2,1)}, bf16[768,2048]{1,0:T(8,128)(2,1)}) custom-call(f32[1]{0:T(128)} %bitcast.12.scale_ref, bf16[256,2048]{1,0:T(8,128)(2,1)} %multiply_convert_fusion.x_ref, bf16[2048,2048]{1,0:T(8,128)(2,1)} %all-gather.11.cloned.1.call-done.cot_ref, ...), custom_call_target="tpu_custom_call" | custom-call | flops 60000002048 | bytes 60000000 | tf_op jit(solution)/shard_map/ffn/pallas_call | solution.py:776
  467.6 0.7 copy-done.21
  468.4 0.6 copy-done.1
  469.0 2.1 multiply_reduce_fusion
  471.2 1.2 copy-done.8
  472.6 3.6 fusion.12
  476.2 5.3 convolution_convert_fusion.do_ref
  481.4 44.2 %attend_back.1.refs_2_ = bf16[256,1920]{1,0:T(8,128)(2,1)} custom-call(bf16[256,1280]{1,0:T(8,128)(2,1)} %get-tuple-element.27.q_ref, bf16[2048,640]{1,0:T(8,128)(2,1)} %bitcast.29, bf16[256,1280]{1,0:T(8,128)(2,1)} %get-tuple-element.29.o_ref.refs_1_, bf16[256,1280]{1,0:T(8,128)(2,1)} %convolution_convert_fusion.do_ref, ...), custom_call_target="tpu_custom_call" | custom-call | flops 120000004096 | bytes 12000000 | tf_op jit(solution)/shard_map/attend_back/pallas_call | solution.py:345
  525.7 5.5 fusion.4
  531.3 0.6 fusion.3
  531.9 1.3 copy-done.4
  533.2 1.2 collective-permute-start.3
  534.4 0.7 maximum_maximum_fusion.refs_4_
  535.1 111.1 %reduce_products.1 = (f32[64,2048]{1,0:T(8,128)}, f32[40,2048]{1,0:T(8,128)}) custom-call(bf16[256,2048]{1,0:T(8,128)(2,1)} %get-tuple-element.33.refs_0_, bf16[256,1280]{1,0:T(8,128)(2,1)} %get-tuple-element.29.o_ref.refs_1_, bf16[256,1920]{1,0:T(8,128)(2,1)} %attend_back.1.refs_2_, bf16[256,2048]{1,0:T(8,128)(2,1)} %copy-done.16, ...), custom_call_target="tpu_custom_call" | custom-call | flops 49999998976 | bytes 10000000 | tf_op jit(solution)/shard_map/reduce_products/pallas_call | solution.py:1037
  646.3 1.4 convert_element_type.67
  647.7 44.5 %all-reduce.3.cloned.1.call-done = (bf16[2048,768]{1,0:T(8,128)(2,1)}, bf16[2048,768]{1,0:T(8,128)(2,1)}, bf16[768,2048]{1,0:T(8,128)(2,1)}) async-done(((bf16[2048,768]{1,0:T(8,128)(2,1)}, bf16[2048,768]{1,0:T(8,128)(2,1)}, bf16[768,2048]{1,0:T(8,128)(2,1)}), (bf16[2048,768]{1,0:T(8,128)(2,1)}, bf16[2048,768]{1,0:T(8,128)(2,1)}, bf16[768,2048]{1,0:T(8,128)(2,1)})) %all-reduce.3.cloned.1.call-update) | async-done | bytes 9437200 | tf_op jit(solution)/shard_map/psum | solution.py:1186
  692.1 91.8 %reduce-scatter.2.cloned.1.call-done = bf16[256,2048]{1,0:T(8,128)(2,1)} async-done(((bf16[2048,2048]{1,0:T(8,128)(2,1)}), bf16[256,2048]{1,0:T(8,128)(2,1)}) %reduce-scatter.2.cloned.1.call-update) | async-done | bytes 1048592 | tf_op jit(solution)/shard_map/reduce_scatter | solution.py:1137
  783.9 1.5 add_convert_fusion
  785.5 0.9 fusion.14
  786.3 0.5 slice-done
  786.9 1.5 pad_maximum_fusion.1
  788.4 0.2 reshape.110
  788.9 5.2 convert_element_type.68
  794.2 3.2 convert_element_type.69
  797.4 3.6 convert_element_type.70
  800.9 0.7 slice_reduce_fusion.2
  801.6 0.8 pad_maximum_fusion.5
  802.4 2.1 pad_maximum_fusion.4
  804.5 0.7 copy.38
  (81 shorter events, 2.2 us)
Async XLA Ops:
  7.2 5.5 copy-start.17
  7.2 91.7 %all-gather.5.cloned.1.call-start = ((), (), s32[]{:S(2)}) async-start(), calls=%async_computation.1 | async-start | bytes 8650752 | tf_op jit(solution)/shard_map/all_gather | solution.py:1109
  12.7 154.1 %all-gather.7.cloned.1.call-start = ((), (), s32[]{:S(2)}) async-start(), calls=%async_computation.2 | async-start | bytes 2949120 | tf_op jit(solution)/shard_map/all_gather | solution.py:1127
  12.8 220.8 %copy-start.5 = (bf16[128,2048]{1,0:T(8,128)(2,1)}, bf16[128,2048]{1,0:T(8,128)(2,1)S(1)}, u32[]{:S(2)}) copy-start(bf16[128,2048]{1,0:T(8,128)(2,1)S(1)} %get-tuple-element.70) | copy-start | bytes 1572868
  12.8 19.0 %collective-permute-start = (bf16[128,2048]{1,0:T(8,128)(2,1)S(1)}, bf16[128,2048]{1,0:T(8,128)(2,1)S(1)}, u32[]{:S(2)}, u32[]{:S(2)}) collective-permute-start(bf16[128,2048]{1,0:T(8,128)(2,1)S(1)} %get-tuple-element.71), channel_id=1, source_target_pairs={{0,7},{1,6},{2,5},{3,4},{4,3},{5,2},{6,1},{7,0},{8,15},{9,14},{10,... | collective-permute-start | bytes 1572872 | tf_op jit(solution)/shard_map/ppermute | solution.py:1080
  31.9 67.1 %copy-start.11 = (bf16[128,2048]{1,0:T(8,128)(2,1)}, bf16[128,2048]{1,0:T(8,128)(2,1)S(1)}, u32[]{:S(2)}) copy-start(bf16[128,2048]{1,0:T(8,128)(2,1)S(1)} %collective-permute-done) | copy-start | bytes 1572868
  109.4 8.1 %copy-start.18 = (bf16[256,2048]{1,0:T(8,128)(2,1)S(1)}, bf16[256,2048]{1,0:T(8,128)(2,1)}, u32[]{:S(2)}) copy-start(bf16[256,2048]{1,0:T(8,128)(2,1)} %param.12) | copy-start | bytes 3145732
  116.7 116.8 %all-gather.9.cloned.1.call-start = ((), (), s32[]{:S(2)}) async-start(), calls=%async_computation.3 | async-start | bytes 5406720 | tf_op jit(solution)/shard_map/all_gather | solution.py:1124
  117.5 199.1 %all-gather.11.cloned.1.call-start = ((), (), s32[]{:S(2)}) async-start(), calls=%async_computation.4 | async-start | bytes 9437184 | tf_op jit(solution)/shard_map/all_gather | solution.py:1123
  117.6 21.8 %copy-start.7 = (bf16[128,2048]{1,0:T(8,128)(2,1)}, bf16[128,2048]{1,0:T(8,128)(2,1)S(1)}, u32[]{:S(2)}) copy-start(bf16[128,2048]{1,0:T(8,128)(2,1)S(1)} %get-tuple-element.67) | copy-start | bytes 1572868
  117.6 24.0 %copy-start.23 = (f32[4]{0:T(128)S(1)}, f32[4]{0:T(128)}, u32[]{:S(2)}) copy-start(f32[4]{0:T(128)} %param.14) | copy-start | bytes 52
  117.6 21.8 %collective-permute-start.1 = (bf16[128,2048]{1,0:T(8,128)(2,1)S(1)}, bf16[128,2048]{1,0:T(8,128)(2,1)S(1)}, u32[]{:S(2)}, u32[]{:S(2)}) collective-permute-start(bf16[128,2048]{1,0:T(8,128)(2,1)S(1)} %get-tuple-element.68), channel_id=1, source_target_pairs={{0,7},{1,6},{2,5},{3,4},{4,3},{5,2},{6,1},{7,0},{8,15},{9,14},{10,... | collective-permute-start | bytes 1572872 | tf_op jit(solution)/shard_map/ppermute | solution.py:1080
  139.5 0.8 copy-start.14
  141.4 550.8 %all-reduce.3.cloned.1.call-start = ((), (), s32[]{:S(2)}) async-start(), calls=%async_computation.6 | async-start | bytes 18874368 | tf_op jit(solution)/shard_map/psum | solution.py:1186
  172.9 60.7 %copy-start.12 = (bf16[128,2048]{1,0:T(8,128)(2,1)S(1)}, bf16[128,2048]{1,0:T(8,128)(2,1)}, u32[]{:S(2)}) copy-start(bf16[128,2048]{1,0:T(8,128)(2,1)} %copy-done.11) | copy-start | bytes 1572868
  237.9 1.3 copy-start
  467.4 0.9 copy-start.21
  467.4 1.7 copy-start.1
  467.4 316.5 %reduce-scatter.2.cloned.1.call-start = ((), (), s32[]{:S(2)}) async-start(), calls=%async_computation.5 | async-start | bytes 9437184 | tf_op jit(solution)/shard_map/reduce_scatter | solution.py:1137
  471.2 1.2 copy-start.8
  471.2 1.4 copy-start.15
  476.2 5.3 copy-start.16
  481.4 44.3 %copy-start.6 = (bf16[128,2048]{1,0:T(8,128)(2,1)S(1)}, bf16[128,2048]{1,0:T(8,128)(2,1)}, u32[]{:S(2)}) copy-start(bf16[128,2048]{1,0:T(8,128)(2,1)} %copy-done.5) | copy-start | bytes 1572868
  481.4 44.3 %copy-start.13 = (bf16[128,2048]{1,0:T(8,128)(2,1)S(1)}, bf16[128,2048]{1,0:T(8,128)(2,1)}, u32[]{:S(2)}) copy-start(bf16[128,2048]{1,0:T(8,128)(2,1)} %copy-done.11) | copy-start | bytes 1572868
  481.4 44.3 %copy-start.22 = (f32[2048]{0:T(1024)S(1)}, f32[2048]{0:T(1024)}, u32[]{:S(2)}) copy-start(f32[2048]{0:T(1024)} %get-tuple-element.49) | copy-start | bytes 24580
  525.7 5.5 copy-start.3
  531.9 1.3 copy-start.4
  533.2 113.1 %collective-permute-start.3 = (bf16[128,2048]{1,0:T(8,128)(2,1)S(1)}, bf16[128,2048]{1,0:T(8,128)(2,1)}, u32[]{:S(2)}, u32[]{:S(2)}) collective-permute-start(bf16[128,2048]{1,0:T(8,128)(2,1)S(1)} %slice.116), channel_id=1, source_target_pairs={{0,7},{1,6},{2,5},{3,4},{4,3},{5,2},{6,1},{7,0},{8,15},{9,14},{10,... | collective-permute-start | bytes 1572872 | tf_op jit(solution)/shard_map/ppermute | solution.py:1162
  646.3 137.6 %copy-start.2 = (f32[256,2048]{1,0:T(8,128)S(1)}, f32[256,2048]{1,0:T(8,128)}, u32[]{:S(2)}) copy-start(f32[256,2048]{1,0:T(8,128)} %copy-done) | copy-start | bytes 6291460
  785.5 1.4 slice-start
  786.3 2.0 copy-start.19
  786.3 16.1 %collective-permute-start.2 = (bf16[128,2048]{1,0:T(8,128)(2,1)}, bf16[128,2048]{1,0:T(8,128)(2,1)}, u32[]{:S(2)}, u32[]{:S(2)}) collective-permute-start(bf16[128,2048]{1,0:T(8,128)(2,1)} %get-tuple-element.66), channel_id=1, source_target_pairs={{0,7},{1,6},{2,5},{3,4},{4,3},{5,2},{6,1},{7,0},{8,15},{9,14},{10,... | collective-permute-start | bytes 1572872 | tf_op jit(solution)/shard_map/ppermute | solution.py:1080
  788.9 5.2 copy-start.10
  794.2 3.2 copy-start.9
  800.9 3.6 copy-start.20
Sparse Core Ops, SparseCore 0:
  12.8 86.0 all-gather.4
  116.9 49.8 all-gather.6
  169.6 63.9 all-gather.8
  235.6 80.9 all-gather.10
  467.5 224.5 all-reduce.2
  694.3 89.5 reduce-scatter.1

commit v2 on v1

--- a/solution.py
+++ b/solution.py
@@ -169,12 +169,6 @@
         ),
         name="attend",
     )(blocks, q, kv_all)
-
-
-def block_of(device, sub, subs):
-    if subs == 2:
-        return 2 * device if sub == 0 else 2 * lax.axis_size("mp") - 1 - 2 * device
-    return subs * device + sub
 
 
 def attend_back_kernel(
@@ -256,7 +250,7 @@
         dkv_acc[...] = jnp.zeros_like(dkv_acc)
         for sub in range(subs):
             rows = slice(sub * BLOCK, (sub + 1) * BLOCK)
-            block = block_of(me, sub, subs)
+            block = natural(me, sub, subs)
             queries = heads_to_lanes(q_ref[rows, cols].astype(F32))
             grads = heads_to_lanes(do_ref[rows, cols].astype(F32))
             outs = heads_to_lanes(o_ref[rows, cols].astype(F32))
@@ -302,9 +296,9 @@
 
         for goal in range(chips):
             for sub in range(subs):
-                first = block_of(2 * goal + core, sub, subs) * BLOCK
+                first = natural(2 * goal + core, sub, subs) * BLOCK
                 own_part[g % 2, goal, sub] = dkv_acc[pl.ds(pl.multiple_of(first, BLOCK), BLOCK), :]
-                first = block_of(2 * goal + 1 - core, sub, subs) * BLOCK
+                first = natural(2 * goal + 1 - core, sub, subs) * BLOCK
                 twin_out[g % 2, goal, sub] = dkv_acc[
                     pl.ds(pl.multiple_of(first, BLOCK), BLOCK), :
                 ].astype(BF16)
@@ -397,13 +391,20 @@
 
 
 def half_of(ref, chip, core, sub, rows):
-    tokens = ref.shape[0] // (lax.axis_size("mp") // 2)
-    start = chip * tokens + core * (tokens // 2) + sub * rows
+    subs = ref.shape[0] // (rows * lax.axis_size("mp"))
+    start = natural(2 * chip + core, sub, subs) * rows
+    return ref.at[pl.ds(pl.multiple_of(start, rows), rows)]
+
+
+def part_of(ref, chip, core, sub, rows):
+    subs = ref.shape[0] // (rows * lax.axis_size("mp"))
+    start = (subs * (2 * chip + core) + sub) * rows
     return ref.at[pl.ds(pl.multiple_of(start, rows), rows)]
 
 
 def ffn_kernel(
     subs,
+    quad,
     scale_ref,
     x_ref,
     cot_ref,
@@ -411,6 +412,53 @@
     up_ref,
     down_ref,
     part_ref,
+    part_in,
+    relay_in,
+    part_sum,
+    sum_ref,
+    gate_out,
+    up_out,
+    down_out,
+    *rest,
+):
+    slots = rest[:9] if quad else ()
+    scratch = rest[9:] if quad else rest
+    ffn_body(
+        subs,
+        quad,
+        slots,
+        scale_ref,
+        x_ref,
+        cot_ref,
+        gate_ref,
+        up_ref,
+        down_ref,
+        part_ref,
+        part_in,
+        relay_in,
+        part_sum,
+        sum_ref,
+        gate_out,
+        up_out,
+        down_out,
+        *scratch,
+    )
+
+
+def ffn_body(
+    subs,
+    quad,
+    slots,
+    scale_ref,
+    x_ref,
+    cot_ref,
+    gate_ref,
+    up_ref,
+    down_ref,
+    part_ref,
+    part_in,
+    relay_in,
+    part_sum,
     sum_ref,
     gate_out,
     up_out,
@@ -420,8 +468,7 @@
     dgate,
     dup,
     cot_buf,
-    part_buf,
-    own_buf,
+    part_own,
     twin_buf,
     twin_in,
     send_buf,
@@ -437,10 +484,15 @@
     twin_recv,
     sum_send,
     sum_recv,
+    p_send,
+    p_recv,
+    relay_recv,
+    relay_sem,
     cot_sem,
     part_sem,
     cols_sem,
     out_sem,
+    *row_scratch,
 ):
     chips = lax.axis_size("mp") // 2
     me = lax.axis_index("mp")
@@ -460,7 +512,14 @@
         pl.semaphore_signal(
             barrier, inc=1, device_id=on_chip((chip + step) % chips), device_id_type=MESH
         )
-    pl.semaphore_wait(barrier, chips)
+    down, across = row // 2, row % 2
+    beside_row = row + 1 - 2 * across
+    above_row = (1 - down) * 2 + across
+    neighbours = ((beside_row, me), (above_row, me))
+    if quad:
+        for device in neighbours:
+            pl.semaphore_signal(barrier, inc=1, device_id=device, device_id_type=MESH)
+    pl.semaphore_wait(barrier, chips + 2 if quad else chips)
 
     def order(i):
         near = jnp.minimum(chip, chips - 1 - chip)
@@ -496,23 +555,35 @@
             device_id_type=MESH,
         )
 
-    def twin_sum_copy(other, sub, slot):
+    def twin_sum_copy(slot):
         return pltpu.make_async_remote_copy(
             src_ref=twin_buf.at[slot],
-            dst_ref=twin_in.at[other * subs + sub],
+            dst_ref=twin_in.at[slot],
             send_sem=twin_send.at[slot],
-            recv_sem=twin_recv.at[other * subs + sub],
+            recv_sem=twin_recv.at[slot],
             device_id=twin,
             device_id_type=MESH,
         )
 
     def sum_copy(other, sub):
+        side = jnp.where(other > chip, 1, -1)
+        slot = jnp.where((side == 1) & (other == chip + 1), chips, other)
         return pltpu.make_async_remote_copy(
             src_ref=send_buf.at[other * subs + sub],
-            dst_ref=sums_in.at[(chip - other + chips) % chips - 1, sub],
+            dst_ref=sums_in.at[slot, sub],
             send_sem=sum_send.at[other * subs + sub],
-            recv_sem=sum_recv.at[(chip - other + chips) % chips - 1, sub],
-            device_id=on_chip(other),
+            recv_sem=sum_recv.at[slot, sub],
+            device_id=on_chip(chip + side),
+            device_id_type=MESH,
+        )
+
+    def sum_arrival(slot, sub):
+        return pltpu.make_async_remote_copy(
+            src_ref=send_buf.at[0],
+            dst_ref=sums_in.at[slot, sub],
+            send_sem=sum_send.at[0],
+            recv_sem=sum_recv.at[slot, sub],
+            device_id=twin,
             device_id_type=MESH,
         )
 
@@ -526,15 +597,11 @@
             for c in range(2)
         ]
 
-    def part_copies(other, sub, slot):
-        return [
-            pltpu.make_async_copy(
-                part_buf.at[slot, pl.ds(c * rows, rows)],
-                half_of(part_ref, other, c, sub, rows),
-                part_sem.at[slot, c],
-            )
-            for c in range(2)
-        ]
+    def part_copy(i):
+        other, sub = order(i)
+        return pltpu.make_async_copy(
+            part_own.at[i % 2], part_ref.at[other * subs + sub], part_sem.at[i % 2]
+        )
 
     for sub in range(subs):
         source = x_ref.at[pl.ds(sub * rows, rows)]
@@ -556,17 +623,44 @@
     def reduce_unit(i):
         other, sub = order(i)
         unit = other * subs + sub
-        twin_sum_copy(other, sub, i % 2).wait_recv()
-        total = own_buf[i % 2] + twin_in[unit].astype(F32)
+        slot = i % 2
+        twin_sum_copy(slot).wait_recv()
+        part_own[slot] = (
+            part_own[slot].astype(F32) + twin_in[slot, 1].astype(F32)
+        ).astype(BF16)
+        part_copy(i).start()
+        arrived = twin_in[slot, 0].astype(F32)
+        lines = pl.ds(pl.multiple_of(sub * rows, rows), rows)
 
         @pl.when(other == chip)
         def _():
-            sum_ref[pl.ds(pl.multiple_of(sub * rows, rows), rows), :] = total
+            sum_ref[lines, :] = sum_ref[lines, :] + arrived
 
         @pl.when(other != chip)
         def _():
-            send_buf[unit] = total.astype(BF16)
+            send_buf[unit] = (send_buf[unit].astype(F32) + arrived).astype(BF16)
+
+        @pl.when(((other > chip) & (chip == 0)) | ((other < chip) & (chip == chips - 1)))
+        def _():
             sum_copy(other, sub).start()
+
+    def pass_on(e):
+        right, left = chips - 1 - chip, chip
+        right_first = chip < chips // 2
+        ahead = jnp.where(right_first, right, left)
+        step = jnp.where(e < ahead, e + 1, e - ahead + 1)
+        toward = jnp.where((e < ahead) == right_first, 1, -1)
+        other = chip + toward * step
+
+        @pl.when((chip > 0) & (chip < chips - 1))
+        def _():
+            for sub in range(subs):
+                unit = other * subs + sub
+                sum_arrival(other, sub).wait_recv()
+                send_buf[unit] = (
+                    send_buf[unit].astype(F32) + sums_in[other, sub].astype(F32)
+                ).astype(BF16)
+                sum_copy(other, sub).start()
 
     def unit_step(i, _):
         other, sub = order(i)
@@ -611,30 +705,45 @@
 
         @pl.when(i >= 2)
         def _():
-            for copy in part_copies(*order(i - 2), slot):
-                copy.wait()
-
-        part_buf[slot] = dot(h, down_ref[...]).astype(BF16)
-        for copy in part_copies(other, sub, slot):
-            copy.start()
-
-        @pl.when(i >= 2)
-        def _():
-            twin_sum_copy(*order(i - 2), slot).wait_send()
+            part_copy(i - 2).wait()
+            twin_sum_copy(slot).wait_send()
+
+        part = dot(h, down_ref[...])
+
+        def keep_part(own, away):
+            part_own[slot] = own.astype(BF16)
+            twin_buf[slot, 1] = away.astype(BF16)
+
+        @pl.when(core == 0)
+        def _():
+            keep_part(part[:rows], part[rows:])
+
+        @pl.when(core == 1)
+        def _():
+            keep_part(part[rows:], part[:rows])
 
         dx = dot_nt(dg, gate_ref[...]) + dot_nt(du, up_ref[...])
 
+        def keep(own, away):
+            twin_buf[slot, 0] = away.astype(BF16)
+
+            @pl.when(other == chip)
+            def _():
+                sum_ref[pl.ds(pl.multiple_of(sub * rows, rows), rows), :] = own
+
+            @pl.when(other != chip)
+            def _():
+                send_buf[other * subs + sub] = own.astype(BF16)
+
         @pl.when(core == 0)
         def _():
-            own_buf[slot] = dx[:rows]
-            twin_buf[slot] = dx[rows:].astype(BF16)
+            keep(dx[:rows], dx[rows:])
 
         @pl.when(core == 1)
         def _():
-            own_buf[slot] = dx[rows:]
-            twin_buf[slot] = dx[:rows].astype(BF16)
-
-        twin_sum_copy(other, sub, slot).start()
+            keep(dx[rows:], dx[:rows])
+
+        twin_sum_copy(slot).start()
 
         @pl.when(i >= 1)
         def _():
@@ -644,6 +753,9 @@
 
     lax.fori_loop(0, units, unit_step, 0)
     reduce_unit(units - 1)
+    for i in (units - 2, units - 1):
+        part_copy(i).wait()
+        twin_sum_copy(i % 2).wait_send()
 
     width = x_ref.shape[1]
     ff = gate_ref.shape[1]
@@ -651,53 +763,206 @@
     narrow = tall_buf.shape[2]
     down_cols = cot_cols.shape[2]
     col_steps = width // down_cols
-
-    def cols_copy(j):
-        return pltpu.make_async_copy(
-            cot_ref.at[:, pl.ds(pl.multiple_of(j * down_cols, down_cols), down_cols)],
-            cot_cols.at[j % 2],
-            cols_sem.at[j % 2],
-        )
-
-    def wide_out(j):
-        return pltpu.make_async_copy(
-            wide_buf.at[j % 2],
-            down_out.at[:, pl.ds(pl.multiple_of(j * down_cols, down_cols), down_cols)],
-            out_sem.at[j % 2],
-        )
-
-    cols_copy(0).start()
-
-    def down_step(j, _):
-        @pl.when(j + 1 < col_steps)
-        def _():
-            cols_copy(j + 1).start()
-
-        cols_copy(j).wait()
-
-        @pl.when(j >= 2)
-        def _():
-            wide_out(j - 2).wait()
-
-        wide_buf[j % 2] = (dot_tn(hid[...], cot_cols[j % 2]) * scale_ref[0]).astype(BF16)
-        wide_out(j).start()
-        return 0
-
-    lax.fori_loop(0, col_steps, down_step, 0)
-    for j in range(max(0, col_steps - 2), col_steps):
-        wide_out(j).wait()
-
     pieces = width // tall
     steps = pieces * (ff // narrow)
-
-    for source, target in ((dgate, gate_out), (dup, up_out)):
+    wholes = (gate_out, up_out, down_out)
+
+    if quad:
+        firsts, seconds, finals = slots[0:3], slots[3:6], slots[6:9]
+        tall_in, wide_in, moved, one_send, one_recv, two_send, two_recv, load_sem, fin_sem = (
+            row_scratch[:2] + (row_scratch[2:5],) + row_scratch[5:]
+        )
+
+    def remote(source, dest, send, recv, device):
+        return pltpu.make_async_remote_copy(
+            src_ref=source,
+            dst_ref=dest,
+            send_sem=send,
+            recv_sem=recv,
+            device_id=device,
+            device_id_type=MESH,
+        )
+
+    def block_at(a, block, d):
+        high, wide = firsts[a].shape[2:]
+        lines = pl.ds(pl.multiple_of(block * high, high), high)
+        return wholes[a].at[lines, pl.ds(d * wide, wide)]
+
+    def one_copy(a, d, k):
+        block = k * 2 + 1 - across if d == 0 else (1 - down) * 2 + k
+        return remote(
+            block_at(a, block, d),
+            firsts[a].at[d, k],
+            one_send.at[a, d, k],
+            one_recv.at[a, d, k],
+            neighbours[d],
+        )
+
+    def two_copy(a, d):
+        return remote(
+            moved[a].at[d],
+            seconds[a].at[d],
+            two_send.at[a, d],
+            two_recv.at[a, d],
+            neighbours[1 - d],
+        )
+
+    def fin_copy(a, d):
+        wide = firsts[a].shape[3]
+        return pltpu.make_async_copy(
+            (wide_in if a == 2 else tall_in).at[0],
+            finals[a].at[:, pl.ds(d * wide, wide)],
+            fin_sem.at[d],
+        )
+
+    def load(sources, buf):
+        copies = [
+            pltpu.make_async_copy(source, buf.at[i], load_sem.at[i])
+            for i, source in enumerate(sources)
+        ]
+        for copy in copies:
+            copy.start()
+        for copy in copies:
+            copy.wait()
+
+    def stage_one(a):
+        if quad:
+            for d in range(2):
+                for k in range(2):
+                    one_copy(a, d, k).start()
+
+    def stage_two(a):
+        if quad:
+            buf = wide_in if a == 2 else tall_in
+            for d in range(2):
+                for k in range(2):
+                    one_copy(a, d, k).wait_recv()
+                block = above_row if d == 0 else beside_row
+                other = 1 - down if d == 0 else 1 - across
+                load([block_at(a, block, d), firsts[a].at[d, other]], buf)
+                moved[a][d] = (buf[0].astype(F32) + buf[1].astype(F32)).astype(BF16)
+                two_copy(a, d).start()
+
+    def stage_three(a):
+        if quad:
+            buf = wide_in if a == 2 else tall_in
+            for d in range(2):
+                two_copy(a, d).wait_recv()
+                other = down if d == 0 else across
+                load([block_at(a, row, d), firsts[a].at[d, other], seconds[a].at[d]], buf)
+                buf[0] = (
+                    buf[0].astype(F32) + buf[1].astype(F32) + buf[2].astype(F32)
+                ).astype(BF16)
+                fin_copy(a, d).start()
+                fin_copy(a, d).wait()
+
+    def end_far(source, other):
+        return ((source == 0) & (other >= 2)) | ((source == chips - 1) & (other <= chips - 3))
+
+    def relayed(source, other):
+        return ((source == 1) & (other >= 2)) | ((source == chips - 2) & (other <= chips - 3))
+
+    def p_copy(other, sub, source=None):
+        return remote(
+            part_ref.at[other * subs + sub] if source is None else source,
+            part_in.at[chip, sub],
+            p_send.at[other * subs + sub],
+            p_recv.at[chip, sub],
+            on_chip(other),
+        )
+
+    def relay_copy(other, sub):
+        return remote(
+            part_ref.at[other * subs + sub],
+            relay_in.at[other, sub],
+            p_send.at[other * subs + sub],
+            relay_recv.at[other, sub],
+            on_chip(jnp.where(chip == 0, 1, chips - 2)),
+        )
+
+    def send_parts():
+        for far in (True, False):
+            for step in range(1, chips):
+                other = (chip + step) % chips
+                beyond = end_far(chip, other)
+                for sub in range(subs):
+                    if far:
+
+                        @pl.when(beyond)
+                        def _():
+                            relay_copy(other, sub).start()
+
+                    else:
+
+                        @pl.when(jnp.logical_not(beyond | relayed(chip, other)))
+                        def _():
+                            p_copy(other, sub).start()
+
+    def piece(index):
+        return cot_buf.at[index // 2, pl.ds(index % 2 * rows, rows)]
+
+    def fetch(source, index):
+        copy = pltpu.make_async_copy(source, piece(index), relay_sem.at[index])
+        copy.start()
+        return copy
+
+    def relay_parts():
+        for step in range(1, chips):
+            other = (chip + step) % chips
+
+            @pl.when(relayed(chip, other))
+            def _():
+                for sub in range(subs):
+                    mine = fetch(part_ref.at[other * subs + sub], 2 * sub)
+                    remote(
+                        part_ref.at[0],
+                        relay_in.at[other, sub],
+                        p_send.at[0],
+                        relay_recv.at[other, sub],
+                        twin,
+                    ).wait_recv()
+                    theirs = fetch(relay_in.at[other, sub], 2 * sub + 1)
+                    mine.wait()
+                    theirs.wait()
+                    part_ref_sum = piece(2 * sub)[...].astype(F32) + piece(2 * sub + 1)[
+                        ...
+                    ].astype(F32)
+                    piece(2 * sub)[...] = part_ref_sum.astype(BF16)
+                    back = pltpu.make_async_copy(
+                        piece(2 * sub), part_ref.at[other * subs + sub], relay_sem.at[2 * sub]
+                    )
+                    back.start()
+                    back.wait()
+                    p_copy(other, sub).start()
+
+    def total_parts():
+        for sub in range(subs):
+            lines = slice(sub * rows, (sub + 1) * rows)
+            fetch(part_ref.at[chip * subs + sub], 0).wait()
+            part_sum[lines, :] = piece(0)[...].astype(F32)
+            for step in range(1, chips):
+                other = (chip + step) % chips
+
+                @pl.when(jnp.logical_not(end_far(other, chip)))
+                def _():
+                    remote(
+                        part_ref.at[0],
+                        part_in.at[other, sub],
+                        p_send.at[0],
+                        p_recv.at[other, sub],
+                        twin,
+                    ).wait_recv()
+                    fetch(part_in.at[other, sub], 0).wait()
+                    part_sum[lines, :] = part_sum[lines, :] + piece(0)[...].astype(F32)
+
+    for a, source in enumerate((dgate, dup)):
 
         def tall_out(j):
             first = pl.multiple_of(j % pieces * tall, tall)
             col = pl.multiple_of(j // pieces * narrow, narrow)
             return pltpu.make_async_copy(
                 tall_buf.at[j % 2],
-                target.at[pl.ds(first, tall), pl.ds(col, narrow)],
+                wholes[a].at[pl.ds(first, tall), pl.ds(col, narrow)],
                 out_sem.at[j % 2],
             )
 
@@ -717,20 +982,75 @@
         lax.fori_loop(0, steps, tall_step, 0)
         for j in range(steps - 2, steps):
             tall_out(j).wait()
+        stage_one(a)
+        for e in range(a * (chips - 1) // 3, (a + 1) * (chips - 1) // 3):
+            pass_on(e)
+    send_parts()
+
+    def cols_copy(j):
+        return pltpu.make_async_copy(
+            cot_ref.at[:, pl.ds(pl.multiple_of(j * down_cols, down_cols), down_cols)],
+            cot_cols.at[j % 2],
+            cols_sem.at[j % 2],
+        )
+
+    def wide_out(j):
+        return pltpu.make_async_copy(
+            wide_buf.at[j % 2],
+            down_out.at[:, pl.ds(pl.multiple_of(j * down_cols, down_cols), down_cols)],
+            out_sem.at[j % 2],
+        )
+
+    cols_copy(0).start()
+
+    def down_step(j, _):
+        @pl.when(j + 1 < col_steps)
+        def _():
+            cols_copy(j + 1).start()
+
+        cols_copy(j).wait()
+
+        @pl.when(j >= 2)
+        def _():
+            wide_out(j - 2).wait()
+
+        wide_buf[j % 2] = (dot_tn(hid[...], cot_cols[j % 2]) * scale_ref[0]).astype(BF16)
+        wide_out(j).start()
+        return 0
+
+    lax.fori_loop(0, col_steps, down_step, 0)
+    for j in range(max(0, col_steps - 2), col_steps):
+        wide_out(j).wait()
+    stage_one(2)
+    for e in range(2 * (chips - 1) // 3, chips - 1):
+        pass_on(e)
+    stage_two(0)
+    stage_two(1)
+    stage_three(0)
+    relay_parts()
+    stage_two(2)
+    stage_three(1)
+    stage_three(2)
+    total_parts()
+    if quad:
+        for a in range(3):
+            for d in range(2):
+                two_copy(a, d).wait_send()
+                for k in range(2):
+                    one_copy(a, d, k).wait_send()
 
     for sub in range(subs):
-        total = sum_ref[sub * rows : (sub + 1) * rows, :]
-        for step in range(1, chips):
-            pltpu.make_async_remote_copy(
-                src_ref=send_buf.at[0],
-                dst_ref=sums_in.at[step - 1, sub],
-                send_sem=sum_send.at[0],
-                recv_sem=sum_recv.at[step - 1, sub],
-                device_id=twin,
-                device_id_type=MESH,
-            ).wait_recv()
-            total = total + sums_in[step - 1, sub].astype(F32)
-        sum_ref[sub * rows : (sub + 1) * rows, :] = total
+        lines = slice(sub * rows, (sub + 1) * rows)
+
+        @pl.when(chip < chips - 1)
+        def _():
+            sum_arrival(chip, sub).wait_recv()
+            sum_ref[lines, :] = sum_ref[lines, :] + sums_in[chip, sub].astype(F32)
+
+        @pl.when(chip > 0)
+        def _():
+            sum_arrival(chips, sub).wait_recv()
+            sum_ref[lines, :] = sum_ref[lines, :] + sums_in[chips, sub].astype(F32)
 
     def finish(i, _):
         other, sub = order(i)
@@ -747,12 +1067,7 @@
         @pl.when(other != chip)
         def _():
             sum_copy(other, sub).wait_send()
-
-        @pl.when(i >= units - 2)
-        def _():
-            twin_sum_copy(other, sub, i % 2).wait_send()
-            for copy in part_copies(other, sub, i % 2):
-                copy.wait()
+            p_copy(other, sub).wait_send()
 
         return 0
 
@@ -769,33 +1084,50 @@
     units = chips * subs
     narrow = ff // 3
     tall = 512
-    down_cols = 512
+    down_cols = 256
+    quad = lax.axis_size("rows") == 4
+    extra_out, row_scratch = (), []
     vmem = pl.BlockSpec(memory_space=pltpu.VMEM)
     hbm = pl.BlockSpec(memory_space=pl.ANY)
     dma = pltpu.SemaphoreType.DMA
-    return pl.pallas_call(
-        functools.partial(ffn_kernel, subs),
+    if quad:
+        sizes = ((width // 4, ff // 2), (width // 4, ff // 2), (ff // 4, width // 2))
+        extra_out = (
+            tuple(jax.ShapeDtypeStruct((2, 2, *size), BF16) for size in sizes)
+            + tuple(jax.ShapeDtypeStruct((2, *size), BF16) for size in sizes)
+            + tuple(jax.ShapeDtypeStruct((size[0], 2 * size[1]), BF16) for size in sizes)
+        )
+        row_scratch = (
+            [pltpu.VMEM((3, *sizes[0]), BF16), pltpu.VMEM((3, *sizes[2]), BF16)]
+            + [pltpu.VMEM((2, *size), BF16) for size in sizes]
+            + [dma((3, 2, 2)), dma((3, 2, 2)), dma((3, 2)), dma((3, 2)), dma((3,)), dma((2,))]
+        )
+    out = pl.pallas_call(
+        functools.partial(ffn_kernel, subs, quad),
         out_shape=(
-            jax.ShapeDtypeStruct((tokens, width), BF16),
+            jax.ShapeDtypeStruct((units, rows, width), BF16),
+            jax.ShapeDtypeStruct((chips, subs, rows, width), BF16),
+            jax.ShapeDtypeStruct((chips, subs, rows, width), BF16),
+            jax.ShapeDtypeStruct((rows_dev, width), F32),
             jax.ShapeDtypeStruct((rows_dev, width), F32),
             jax.ShapeDtypeStruct((width, ff), BF16),
             jax.ShapeDtypeStruct((width, ff), BF16),
             jax.ShapeDtypeStruct((ff, width), BF16),
-        ),
+        )
+        + extra_out,
         in_specs=[pl.BlockSpec(memory_space=pltpu.SMEM), vmem, hbm, vmem, vmem, vmem],
-        out_specs=(hbm, vmem, hbm, hbm, hbm),
+        out_specs=(hbm, hbm, hbm, vmem, vmem, hbm, hbm, hbm) + (hbm,) * len(extra_out),
         scratch_shapes=[
             pltpu.VMEM((tokens, width), BF16),
             pltpu.VMEM((tokens, ff), BF16),
             pltpu.VMEM((tokens, ff), BF16),
             pltpu.VMEM((tokens, ff), BF16),
             pltpu.VMEM((2, 2 * rows, width), BF16),
-            pltpu.VMEM((2, 2 * rows, width), BF16),
-            pltpu.VMEM((2, rows, width), F32),
             pltpu.VMEM((2, rows, width), BF16),
+            pltpu.VMEM((2, 2, rows, width), BF16),
+            pltpu.VMEM((2, 2, rows, width), BF16),
             pltpu.VMEM((units, rows, width), BF16),
-            pltpu.VMEM((units, rows, width), BF16),
-            pltpu.VMEM((chips - 1, subs, rows, width), BF16),
+            pltpu.VMEM((chips + 1, subs, rows, width), BF16),
             pltpu.VMEM((2, tokens, down_cols), BF16),
             pltpu.VMEM((2, ff, down_cols), BF16),
             pltpu.VMEM((2, tall, narrow), BF16),
@@ -804,14 +1136,19 @@
             dma((units,)),
             dma((units,)),
             dma((2,)),
+            dma((2,)),
             dma((units,)),
+            dma((chips + 1, subs)),
             dma((units,)),
-            dma((chips - 1, subs)),
-            dma((2, 2)),
+            dma((chips, subs)),
+            dma((chips, subs)),
+            dma((4,)),
             dma((2, 2)),
             dma((2,)),
             dma((2,)),
-        ],
+            dma((2,)),
+        ]
+        + row_scratch,
         compiler_params=pltpu.CompilerParams(
             collective_id=1, has_side_effects=True, vmem_limit_bytes=VMEM_LIMIT
         ),
@@ -820,6 +1157,11 @@
         ),
         name="ffn",
     )(scale.reshape(1), x, cot_all, gate_weight, up_weight, down_weight)
+    if quad:
+        shards = out[14:17]
+    else:
+        shards = [lax.psum(part, "rows") for part in out[5:8]]
+    return (*out[3:5], *shards)
 
 
 def reduce_kernel(heights, *refs):
@@ -1050,6 +1392,342 @@
     )(*[left for left, _ in pairs], *[right for _, right in pairs], gains)
 
 
+def natural(device, sub, subs):
+    if subs == 2:
+        return sub * (2 * lax.axis_size("mp") - 1 - 2 * device) + (1 - sub) * 2 * device
+    return subs * device + sub
+
+
+def front_kernel(
+    shard_ref,
+    x_ref,
+    cos_q,
+    sin_q,
+    cos_kv,
+    sin_kv,
+    w_out,
+    extra_ref,
+    xf_ref,
+    normed_ref,
+    inv_ref,
+    q_ref,
+    kv_out,
+    w_all,
+    x_in,
+    kv_all,
+    swap_send,
+    swap_recv,
+    z_send,
+    z_recv,
+    xy_send,
+    xy_recv,
+    far_send,
+    far_recv,
+    twin_send,
+    twin_recv,
+    kz_send,
+    kz_recv,
+    kt_send,
+    kt_recv,
+    out_sem,
+):
+    mp = lax.axis_size("mp")
+    chips = mp // 2
+    me = lax.axis_index("mp")
+    row = lax.axis_index("rows")
+    chip = me // 2
+    core = me % 2
+    down, across = row // 2, row % 2
+    subs = x_ref.shape[0] // BLOCK
+    height = shard_ref.shape[0]
+    half = w_all.shape[1] // 2
+    beside_row = row + 1 - 2 * across
+    above_row = (1 - down) * 2 + across
+    far_row = (1 - down) * 2 + 1 - across
+    twin = (row, me + 1 - 2 * core)
+    beside = (beside_row, me)
+    above = (above_row, me)
+    mirror = (row, mp - 1 - me)
+
+    barrier = pltpu.get_barrier_semaphore()
+    for device in (twin, beside, above, mirror):
+        pl.semaphore_signal(barrier, inc=1, device_id=device, device_id_type=MESH)
+
+    @pl.when(chip < chips - 1)
+    def _():
+        pl.semaphore_signal(barrier, inc=1, device_id=(row, me + 2), device_id_type=MESH)
+
+    @pl.when(chip > 0)
+    def _():
+        pl.semaphore_signal(barrier, inc=1, device_id=(row, me - 2), device_id_type=MESH)
+
+    ends = jnp.where(chip < chips - 1, 1, 0) + jnp.where(chip > 0, 1, 0)
+    pl.semaphore_wait(barrier, 4 + ends)
+
+    def remote(source, dest, send, recv, device):
+        return pltpu.make_async_remote_copy(
+            src_ref=source,
+            dst_ref=dest,
+            send_sem=send,
+            recv_sem=recv,
+            device_id=device,
+            device_id_type=MESH,
+        )
+
+    def spot(r, k, side=None):
+        lines = pl.ds(pl.multiple_of((r * mp + 2 * k + core) * height, height), height)
+        if side is None:
+            return w_all.at[lines]
+        return w_all.at[lines, pl.ds(side * half, half)]
+
+    def z_copy(k, side):
+        return remote(
+            spot(row, k),
+            spot(row, k),
+            z_send.at[(side + 1) // 2, k],
+            z_recv.at[k],
+            (row, me + 2 * side),
+        )
+
+    def near_copy(k, d):
+        return remote(
+            spot(row, k), spot(row, k), xy_send.at[d, k], xy_recv.at[d, k], (beside, above)[d]
+        )
+
+    def near_row(d):
+        return (beside_row, above_row)[d]
+
+    def far_copy(k, d):
+        place = spot(near_row(d), k, d)
+        return remote(place, place, far_send.at[d, k], far_recv.at[d, k], (above, beside)[d])
+
+    def twin_copy(k, kind):
+        if kind < 3:
+            place = spot((row, beside_row, above_row)[kind], k)
+        else:
+            place = spot(far_row, k, kind - 3)
+        return remote(place, place, twin_send.at[kind, k], twin_recv.at[kind, k], twin)
+
+    def order(i):
+        near = jnp.minimum(chip, chips - 1 - chip)
+        long_side = jnp.where(chip < chips - 1 - chip, 1, -1)
+        paired = i <= 2 * near
+        dist = jnp.where(paired, (i + 1) // 2, i - near)
+        side = jnp.where(paired, 2 * (i % 2) - 1, long_side)
+        return chip + side * dist
+
+    if subs == 2:
+        swap = remote(x_ref.at[pl.ds(BLOCK, BLOCK)], x_in, swap_send, swap_recv, mirror)
+        swap.start()
+    own_lines = pl.ds(pl.multiple_of((row * mp + me) * height, height), height)
+    w_all[own_lines, :] = shard_ref[...]
+
+    def gather_step(n, _):
+        @pl.when(n < chips)
+        def _():
+            k = order(n)
+
+            @pl.when(n > 0)
+            def _():
+                z_copy(k, 1).wait_recv()
+
+            for d in range(2):
+                near_copy(k, d).start()
+
+            @pl.when((k >= chip) & (chip > 0))
+            def _():
+                z_copy(k, -1).start()
+
+            @pl.when((k <= chip) & (chip < chips - 1))
+            def _():
+                z_copy(k, 1).start()
+
+            twin_copy(k, 0).start()
+
+        @pl.when((n >= 1) & (n < chips + 1))
+        def _():
+            k = order(n - 1)
+            for d in range(2):
+                near_copy(k, d).wait_recv()
+                far_copy(k, d).start()
+                twin_copy(k, 1 + d).start()
+
+        @pl.when(n >= 2)
+        def _():
+            k = order(n - 2)
+            for d in range(2):
+                far_copy(k, d).wait_recv()
+                twin_copy(k, 3 + d).start()
+
+        return 0
+
+    lax.fori_loop(0, chips + 2, gather_step, 0)
+
+    xf_ref[:BLOCK, :] = x_ref[:BLOCK, :]
+    if subs == 2:
+        swap.wait_recv()
+        xf_ref[BLOCK:, :] = x_in[...]
+
+    def drain_step(k, _):
+        for kind in range(5):
+            twin_copy(k, kind).wait_recv()
+        return 0
+
+    lax.fori_loop(0, chips, drain_step, 0)
+    save = pltpu.make_async_copy(w_all, w_out, out_sem)
+    save.start()
+    cols = Q_WIDTH + 2 * KV_WIDTH
+    extra = w_all[:, cols:].astype(F32).T[:8, :]
+    extra_ref[...] = extra
+    x = xf_ref[...].astype(F32)
+    inverse = lax.rsqrt(jnp.mean(x * x, axis=-1, keepdims=True) + EPS)
+    inv_ref[...] = inverse
+    normed_ref[...] = (x * inverse * extra[0:1, :]).astype(BF16)
+
+    def place_of(device, sub):
+        first = natural(device, sub, subs) * BLOCK
+        return kv_all.at[pl.ds(pl.multiple_of(first, BLOCK), BLOCK)]
+
+    part = dot(normed_ref[...], w_all[:, Q_WIDTH:cols])
+    for g in range(KV_HEADS):
+        slab = part[:, g * SLAB : (g + 1) * SLAB]
+        turned = (slab * cos_kv[...] + swap_halves(slab) * sin_kv[...]).astype(BF16)
+        for sub in range(subs):
+            place_of(me, sub)[:, g * SLAB : (g + 1) * SLAB] = turned[
+                sub * BLOCK : (sub + 1) * BLOCK, :
+            ]
+
+    def kz_copy(k, sub, side):
+        place = place_of(2 * k + core, sub)
+        return remote(
+            place,
+            place,
+            kz_send.at[(side + 1) // 2, k * subs + sub],
+            kz_recv.at[k * subs + sub],
+            (row, me + 2 * side),
+        )
+
+    def kt_copy(k, sub):
+        place = place_of(2 * k + core, sub)
+        return remote(
+            place, place, kt_send.at[k * subs + sub], kt_recv.at[k * subs + sub], twin
+        )
+
+    def spread(n, _):
+        k = order(n)
+        for sub in range(subs):
+
+            @pl.when(n > 0)
+            def _():
+                kz_copy(k, sub, 1).wait_recv()
+
+            @pl.when((k >= chip) & (chip > 0))
+            def _():
+                kz_copy(k, sub, -1).start()
+
+            @pl.when((k <= chip) & (chip < chips - 1))
+            def _():
+                kz_copy(k, sub, 1).start()
+
+            kt_copy(k, sub).start()
+
+        return 0
+
+    spread(0, 0)
+    for s in range(Q_WIDTH // 256):
+        part = dot(normed_ref[...], w_all[:, s * 256 : (s + 1) * 256])
+        for t in range(2):
+            slab = part[:, t * SLAB : (t + 1) * SLAB]
+            col = s * 256 + t * SLAB
+            turned = slab * cos_q[...] + swap_halves(slab) * sin_q[...]
+            q_ref[:, col : col + SLAB] = (
+                turned.astype(BF16).astype(F32) * HEAD_DIM ** (-0.5)
+            ).astype(BF16)
+    lax.fori_loop(1, chips, spread, 0)
+
+    def finish(k, _):
+        for sub in range(subs):
+            kt_copy(k, sub).wait_recv()
+            kt_copy(k, sub).wait_send()
+        for kind in range(5):
+            twin_copy(k, kind).wait_send()
+        for d in range(2):
+            near_copy(k, d).wait_send()
+            far_copy(k, d).wait_send()
+
+        @pl.when((k >= chip) & (chip > 0))
+        def _():
+            z_copy(k, -1).wait_send()
+            for sub in range(subs):
+                kz_copy(k, sub, -1).wait_send()
+
+        @pl.when((k <= chip) & (chip < chips - 1))
+        def _():
+            z_copy(k, 1).wait_send()
+            for sub in range(subs):
+                kz_copy(k, sub, 1).wait_send()
+
+        return 0
+
+    lax.fori_loop(0, chips, finish, 0)
+    if subs == 2:
+        swap.wait_send()
+    kv_out[...] = kv_all[...]
+    save.wait()
+
+
+def front(shard, x, tables):
+    rows, width = x.shape
+    subs = rows // BLOCK
+    chips = lax.axis_size("mp") // 2
+    cols = shard.shape[1]
+    total = shard.shape[0] * lax.axis_size("rows") * lax.axis_size("mp")
+    vmem = pl.BlockSpec(memory_space=pltpu.VMEM)
+    hbm = pl.BlockSpec(memory_space=pl.ANY)
+    dma = pltpu.SemaphoreType.DMA
+    return pl.pallas_call(
+        front_kernel,
+        out_shape=(
+            jax.ShapeDtypeStruct((total, cols), BF16),
+            jax.ShapeDtypeStruct((8, total), F32),
+            jax.ShapeDtypeStruct((rows, width), BF16),
+            jax.ShapeDtypeStruct((rows, width), BF16),
+            jax.ShapeDtypeStruct((rows, 1), F32),
+            jax.ShapeDtypeStruct((rows, Q_WIDTH), BF16),
+            jax.ShapeDtypeStruct((LEN, 2 * KV_WIDTH), BF16),
+        ),
+        in_specs=[vmem] * 6,
+        out_specs=(hbm,) + (vmem,) * 6,
+        scratch_shapes=[
+            pltpu.VMEM((total, cols), BF16),
+            pltpu.VMEM((BLOCK, width), BF16),
+            pltpu.VMEM((LEN, 2 * KV_WIDTH), BF16),
+            dma,
+            dma,
+            dma((2, chips)),
+            dma((chips,)),
+            dma((2, chips)),
+            dma((2, chips)),
+            dma((2, chips)),
+            dma((2, chips)),
+            dma((5, chips)),
+            dma((5, chips)),
+            dma((2, chips * subs)),
+            dma((chips * subs,)),
+            dma((chips * subs,)),
+            dma((chips * subs,)),
+            dma,
+        ],
+        compiler_params=pltpu.CompilerParams(
+            collective_id=4, has_side_effects=True, vmem_limit_bytes=VMEM_LIMIT
+        ),
+        cost_estimate=pl.CostEstimate(
+            flops=30_000_000_000, bytes_accessed=12_000_000, transcendentals=0
+        ),
+        name="front",
+    )(shard, x, *tables)
+
+
 def on_device(
     inputs,
     cotangent,
@@ -1106,9 +1784,19 @@
         axis=1,
     )
     qkv_cols = Q_WIDTH + 2 * KV_WIDTH
-    qkv_ext = lax.all_gather(shard, both, axis=0, tiled=True)
-    qkv_full = qkv_ext[:, :qkv_cols]
-    extras = qkv_ext[:, qkv_cols : qkv_cols + 3].astype(F32).T
+    cot_all = lax.all_gather(cotangent, "mp", axis=0, tiled=True)
+    out_full = lax.all_gather(out_weight, both, axis=0, tiled=True)
+    tables = rope_tables(positions)
+    if row_groups == 4:
+        qkv_ext, extras, x, normed_one, inverse_one, q, kv_all = front(shard, inputs, tables)
+        qkv_full = qkv_ext[:, :qkv_cols]
+    else:
+        qkv_ext = lax.all_gather(shard, both, axis=0, tiled=True)
+        qkv_full = qkv_ext[:, :qkv_cols]
+        extras = qkv_ext[:, qkv_cols:].astype(F32).T
+        x = fold(inputs)
+        normed_one, inverse_one, q, kv = qkv_project(x, extras[0:1], qkv_full, tables)
+        kv_all = to_order(lax.all_gather(kv, "mp", axis=0, tiled=True))
     gain_one, gain_two = extras[0:1], extras[1:2]
     all_ids = extras[2].reshape(row_groups, -1)[:, 0]
     my_id = corpus_ids[0].astype(F32)
@@ -1117,25 +1805,24 @@
         jnp.where(jnp.arange(corpora) == corpus_ids[0], corpus_weight, 0.0)
     )
     seq_scale = weight_seq * row_groups / (corpora * count)
-
-    x = fold(inputs)
-    cot = fold(cotangent)
-    cot_all = lax.all_gather(cot, "mp", axis=0, tiled=True)
-    out_full = lax.all_gather(out_weight, both, axis=0, tiled=True)
-    tables = rope_tables(positions)
-    normed_one, inverse_one, q, kv = qkv_project(x, gain_one, qkv_full, tables)
-    kv_all = to_order(lax.all_gather(kv, "mp", axis=0, tiled=True))
     o, totals = attend(blocks, q, kv_all)
 
     residual = x.astype(F32)
     middle = residual + dot(o, out_full)
     inverse_two = lax.rsqrt(jnp.mean(middle * middle, axis=-1, keepdims=True) + EPS)
     normed_two = (middle * inverse_two * gain_two).astype(BF16)
-    ffn_part, grad_normed_two, gate_grad, up_grad, down_grad = ffn(
+    ffn_sum, grad_normed_two, gate_grad, up_grad, down_grad = ffn(
         seq_scale, normed_two, cot_all, gate_weight, up_weight, down_weight
     )
-    ffn_sum = lax.psum_scatter(ffn_part, "mp", scatter_dimension=0, tiled=True)
-
+    outputs = fold((middle + ffn_sum).astype(BF16))
+
+    cot = jnp.concatenate(
+        [
+            lax.dynamic_slice(cot_all, (blocks[sub] * BLOCK, 0), (BLOCK, width))
+            for sub in range(subs)
+        ],
+        axis=0,
+    )
     grad_out = cot.astype(F32) * seq_scale
     scaled_two = grad_normed_two * gain_two
     ffn_gain_part = jnp.sum(grad_normed_two * middle * inverse_two, axis=0)
@@ -1145,6 +1832,14 @@
         - middle * inverse_two**3 * jnp.mean(scaled_two * middle, axis=-1, keepdims=True)
     )
     grad_middle_low = grad_middle.astype(BF16)
+    if row_groups == 4:
+        gate_grad, up_grad, down_grad, grad_middle_low = lax.optimization_barrier(
+            (gate_grad, up_grad, down_grad, grad_middle_low)
+        )
+        gate_grad, up_grad, down_grad = (
+            lax.all_gather(g, "rows", axis=0, tiled=True)
+            for g in (gate_grad, up_grad, down_grad)
+        )
     grad_o = dot_nt(grad_middle_low, out_full).astype(BF16)
     grad_qkv = attend_back(q, kv_all, o, grad_o, totals, tables)
     grad_normed_one = dot_nt(grad_qkv, qkv_full)
@@ -1181,20 +1876,13 @@
     qkv_grad = unpack_kv(part[:, :qkv_cols])
     attn_gain_grad = part[:, qkv_cols]
     ffn_gain_grad = part[:, qkv_cols + 1]
-    outputs = fold((middle + ffn_sum.astype(F32)).astype(BF16))
-    gate_grad, up_grad, down_grad = (
-        lax.psum(gate_grad, "rows"),
-        lax.psum(up_grad, "rows"),
-        lax.psum(down_grad, "rows"),
-    )
-    gate_grad, up_grad, down_grad, part, ffn_sum = lax.optimization_barrier(
-        (gate_grad, up_grad, down_grad, part, ffn_sum)
+    gate_grad, up_grad, down_grad, part = lax.optimization_barrier(
+        (gate_grad, up_grad, down_grad, part)
     )
     gate_grad, up_grad, down_grad = (g.astype(F32) for g in (gate_grad, up_grad, down_grad))
     qkv_grad = unpack_kv(part[:, :qkv_cols])
     attn_gain_grad = part[:, qkv_cols]
     ffn_gain_grad = part[:, qkv_cols + 1]
-    outputs = fold((middle + ffn_sum.astype(F32)).astype(BF16))
     return (
         outputs,
         input_grad,

time: 819 us -> 622 us (0.76)
  waiting for transfers between devices: 369 us -> 6.21 us
  Pallas kernels: 339 us -> 535 us
  local copies, waits for them, and re-layouts: 27.3 us -> 12.7 us
  other arithmetic: 37.5 us -> 27.8 us
    pallas_call x2, Pallas kernels: 158 us -> 344 us  [the longest x1 210 us: ffn(): pl.pallas_call(functools.partial(ffn_kernel, subs, quad), out_shape=(jax....]
    all_gather x3 -> x4, waiting for transfers between devices: 165 us -> 4.5 us  [the longest x1 4.5 us: on_device(): cot_all = lax.all_gather(cotangent, 'mp', axis=0, tiled=True)]
    reduce_scatter x1 -> x0, waiting for transfers between devices: 91.8 us -> none  [on_device(): ffn_sum = lax.psum_scatter(ffn_part, 'mp', scatter_dimension=0, tiled=True)]
    psum x1 -> x0, waiting for transfers between devices: 44.5 us -> none  [on_device(): lax.psum(gate_grad, 'rows')]
    all_gather x1, waiting for transfers between devices: 35 us -> 0.01 us  [on_device(): out_full = lax.all_gather(out_weight, both, axis=0, tiled=True)]
    ppermute x3 -> x1, waiting for transfers between devices: 32 us -> 0.01 us  [fold(): lax.ppermute(rows[BLOCK:], 'mp', mirror)]
    pallas_call x1, Pallas kernels: 44.2 us -> 61.7 us  [attend_back(): pl.pallas_call(attend_back_kernel, in_specs=[vmem] * 9, out_specs=vmem, o...]
    slice x2 -> x0, local copies, waits for them, and re-layouts: 8.86 us -> none  [the longest x1 6.93 us: on_device(): qkv_full = qkv_ext[:, :qkv_cols]]
  transfers between devices with their start and end apart: 10 -> 7, of which waited for: 8 -> 1; matrix products, arithmetic and copies ran while one was open for 6% -> 5% of each run, Pallas kernels for 22% -> 53%
where the time goes in v2:
time: 622 us; the launch traced here: 619 us
  Pallas kernels  535 us (86%)
  other arithmetic  27.8 us (4%)
  between operations  16.6 us (3%)
  matrix products  16.4 us (3%)
  local copies, waits for them, and re-layouts  12.7 us (2%)
    pallas_call x1, Pallas kernels, ffn(): pl.pallas_call(functools.partial(ffn_kernel, subs, quad), out_shape=(jax....  210 us
    pallas_call x1, Pallas kernels, front(): pl.pallas_call(front_kernel, out_shape=(jax.ShapeDtypeStruct((total, cols...  134 us
    pallas_call x1, Pallas kernels, reduce_products(): pl.pallas_call(functools.partial(reduce_kernel, heights), out_shape=tuple...  103 us
    pallas_call x1, Pallas kernels, attend_back(): pl.pallas_call(attend_back_kernel, in_specs=[vmem] * 9, out_specs=vmem, o...  61.7 us
    pallas_call x1, Pallas kernels, attend(): pl.pallas_call(attend_kernel, grid_spec=pltpu.PrefetchScalarGridSpec(num_...  25.6 us
  transfers between devices with their start and end apart: 7, of which 1 were waited for; matrix products, arithmetic and copies ran while one was open for 5% of the time, Pallas kernels for 53%

profile of v2, /device:TPU:0, one launch (start us, length us, event | category | flops | bytes accessed | tf_op | source)
XLA Modules:
  0.0 618.7 jit_solution(14510234929091035361)
XLA Ops:
  7.2 0.0 all-gather.6.cloned.1.call-start
  7.3 0.7 all-gather.6.cloned.1.call-update
  7.9 0.0 all-gather.8.cloned.1.call-start
  8.0 0.7 all-gather.8.cloned.1.call-update
  8.7 0.0 all-gather.10.cloned.1.call-start
  8.7 0.9 slice.50
  9.6 0.1 pad.13.clone
  9.7 0.1 pad.16.clone
  10.5 0.2 copy.30
  10.6 0.2 copy.25
  10.8 0.2 reshape.100
  10.9 0.1 copy.26
  11.1 0.1 copy.27
  11.2 0.8 concatenate.46.shard_ref
  12.0 0.6 broadcast_multiply_fusion.2
  12.6 0.1 convert_bitcast_fusion
  12.7 0.5 fusion.10
  13.2 1.0 fusion.8
  14.3 134.1 %front.1 = (bf16[2048,2048]{1,0:T(8,128)(2,1)}, f32[8,2048]{1,0:T(8,128)}, bf16[256,2048]{1,0:T(8,128)(2,1)}, bf16[256,2048]{1,0:T(8,128)(2,1)}, f32[256,1]{1,0:...) custom-call(bf16[64,2048]{1,0:T(8,128)(2,1)} %concatenate.46.shard_ref, bf16[256,2048]{1,0:T(8,128)(2,1)} %x_ref.1, ...), custom_call_target="tpu_custom_call" | custom-call | flops 30000001024 | bytes 12000000 | tf_op jit(solution)/shard_map/front/pallas_call | solution.py:1688
  148.3 1.6 fusion.15
  149.9 0.6 convert_reduce_fusion
  151.2 0.6 fusion.11
  152.5 25.6 %attend.1 = (bf16[256,1280]{1,0:T(8,128)(2,1)}, f32[5,2,512]{2,1,0:T(2,128)}) custom-call(s32[2]{0:T(128)} %get-tuple-element.68.block_ref, bf16[256,1280]{1,0:T(8,128)(2,1)} %get-tuple-element.34.q_ref, bf16[2048,640]{1,0:T(8,128)(2,1)} %get-tuple-element.35.kv_ref), custom_call_target="tpu_custom_call" | custom-call | flops 60000002048 | bytes 8000000 | tf_op jit(solution)/shard_map/attend/pallas_call | solution.py:148
  178.1 4.4 multiply_reduce_fusion.2
  182.6 1.3 copy-done
  183.9 1.2 multiply_convert_fusion.x_ref
  185.1 4.5 all-gather.8.cloned.1.call-done.cot_ref
  189.6 209.8 %ffn.1 = (bf16[8,128,2048]{2,1,0:T(8,128)(2,1)}, bf16[4,2,128,2048]{3,2,1,0:T(8,128)(2,1)}, bf16[4,2,128,2048]{3,2,1,0:T(8,128)(2,1)}, f32[256,2048]{1,0:T(8,128...) custom-call(f32[1]{0:T(128)} %bitcast.9.scale_ref, ...), custom_call_target="tpu_custom_call" | custom-call | flops 60000002048 | bytes 60000000 | tf_op jit(solution)/shard_map/ffn/pallas_call | solution.py:1105
  399.4 2.9 multiply_reduce_fusion
  402.3 1.4 constant_dynamic-slice_fusion.1
  403.8 0.6 copy-done.1
  404.4 2.1 fusion.13
  406.5 0.0 all-gather.10.cloned.1.call-update
  406.5 0.0 all-gather.12.cloned.1.call-start
  406.6 0.1 pad.4.clone
  406.7 0.1 fusion.12
  406.8 0.3 all-gather.12.cloned.1.call-update
  407.1 0.2 all-gather.14.cloned.1.call-start
  407.3 4.9 convolution_convert_fusion.do_ref
  412.2 61.7 %attend_back.1.refs_2_ = bf16[256,1920]{1,0:T(8,128)(2,1)} custom-call(bf16[256,1280]{1,0:T(8,128)(2,1)} %get-tuple-element.34.q_ref, bf16[2048,640]{1,0:T(8,128)(2,1)} %get-tuple-element.35.kv_ref, bf16[256,1280]{1,0:T(8,128)(2,1)} %get-tuple-element.36.o_ref.refs_1_, bf16[256,1280]{1,0:T(8,128)(2,1)} %convolution_convert_fusion.do_ref, ...), custom_call_target="tpu_custom_call" | custom-call | flops 120000004096 | bytes 12000000 | tf_op jit(solution)/shard_map/attend_back/pallas_call | solution.py:339
  474.0 0.0 copy-start.2
  474.0 7.1 %fusion.6 = (f32[2048]{0:T(1024)S(1)}, f32[256]{0:T(256)S(1)}, f32[256,2048]{1,0:T(8,128)S(1)}) fusion(bf16[256,2048]{1,0:T(8,128)(2,1)} %get-tuple-element.33, f32[256]{0:T(256)S(1)} %get-tuple-element.63, f32[2048]{0:T(1024)S(1)} %bitcast.32, bf16[256,1920]{1,0:T(8,128)(2,1)} %attend_back.1.refs_2_, bf16[2048,2048]{1,0:T(8,128)(2,1)} %get-tuple-element.46), kind=kOutput, calls=%fused_computation.11 | convolution fusion | flops 2016933632 | bytes 12011520 | tf_op jit(solution)/shard_map/dot_general | solution.py:386
  481.1 0.6 fusion.3
  481.8 0.0 copy-start.4
  481.8 1.3 copy-done.4
  483.1 0.9 slice.78
  483.9 4.1 collective-permute-start.1
  488.0 0.9 fusion.14
  488.9 0.0 all-gather.14.cloned.1.call-update
  489.0 0.7 maximum_maximum_fusion.refs_4_
  489.7 103.4 %reduce_products.1 = (f32[64,2048]{1,0:T(8,128)}, f32[40,2048]{1,0:T(8,128)}) custom-call(bf16[256,2048]{1,0:T(8,128)(2,1)} %get-tuple-element.50.refs_0_, bf16[256,1280]{1,0:T(8,128)(2,1)} %get-tuple-element.36.o_ref.refs_1_, bf16[256,1920]{1,0:T(8,128)(2,1)} %attend_back.1.refs_2_, bf16[256,2048]{1,0:T(8,128)(2,1)} %copy-done.10, ...), custom_call_target="tpu_custom_call" | custom-call | flops 49999998976 | bytes 10000000 | tf_op jit(solution)/shard_map/reduce_products/pallas_call | solution.py:1379
  593.1 0.0 slice-start
  593.1 1.2 convert_element_type.62
  594.4 1.1 pad_maximum_fusion.1
  595.4 1.5 pad_maximum_fusion
  597.0 0.7 slice_reduce_fusion
  597.7 5.2 convert_element_type.63
  602.9 3.2 convert_element_type.64
  606.1 3.6 convert_element_type.65
  609.7 0.2 reshape.102
  609.9 0.2 copy.28
  610.1 0.1 copy.29
  610.2 0.8 pad_maximum_fusion.2
  611.0 0.7 copy.33
  (53 shorter events, 0.2 us)
Async XLA Ops:
  7.2 4.0 slice-start.1
  7.2 3.8 copy-start.15
  7.2 3.9 copy-start.16
  7.2 170.9 %all-gather.6.cloned.1.call-start = ((), (), s32[]{:S(2)}) async-start(), calls=%async_computation | async-start | bytes 5406720 | tf_op jit(solution)/shard_map/all_gather | solution.py:1788
  7.9 181.7 %all-gather.8.cloned.1.call-start = ((), (), s32[]{:S(2)}) async-start(), calls=%async_computation.1 | async-start | bytes 9437184 | tf_op jit(solution)/shard_map/all_gather | solution.py:1787
  8.7 588.2 %all-gather.10.cloned.1.call-start = ((), (), s32[]{:S(2)}) async-start(), calls=%async_computation.2 | async-start | bytes 3932160 | tf_op jit(solution)/shard_map/all_gather | solution.py:1840
  14.3 136.9 %copy-start.17 = (f32[4]{0:T(128)S(1)}, f32[4]{0:T(128)}, u32[]{:S(2)}) copy-start(f32[4]{0:T(128)} %param.14) | copy-start | bytes 52
  152.5 25.7 %copy-start.8 = (bf16[256,2048]{1,0:T(8,128)(2,1)S(1)}, bf16[256,2048]{1,0:T(8,128)(2,1)}, u32[]{:S(2)}) copy-start(bf16[256,2048]{1,0:T(8,128)(2,1)} %get-tuple-element.33) | copy-start | bytes 3145732
  182.6 1.3 copy-start
  399.4 4.4 copy-start.3
  399.4 4.4 copy-start.7
  402.3 2.0 copy-start.1
  404.4 2.3 copy-start.13
  406.5 5.7 copy-start.10
  406.5 190.4 %all-gather.12.cloned.1.call-start = ((), (), s32[]{:S(2)}) async-start(), calls=%async_computation.3 | async-start | bytes 3932160 | tf_op jit(solution)/shard_map/all_gather | solution.py:1840
  407.1 189.8 %all-gather.14.cloned.1.call-start = ((), (), s32[]{:S(2)}) async-start(), calls=%async_computation.4 | async-start | bytes 3932160 | tf_op jit(solution)/shard_map/all_gather | solution.py:1840
  412.2 61.7 %copy-start.14 = (f32[1,2048]{1,0:T(1,128)S(1)}, f32[1,2048]{1,0:T(1,128)}, u32[]{:S(2)}) copy-start(f32[1,2048]{1,0:T(1,128)} %get-tuple-element.78) | copy-start | bytes 24580
  474.0 7.2 %copy-start.2 = (f32[256,2048]{1,0:T(8,128)S(1)}, f32[256,2048]{1,0:T(8,128)}, u32[]{:S(2)}) copy-start(f32[256,2048]{1,0:T(8,128)} %get-tuple-element.66) | copy-start | bytes 6291460
  474.0 7.2 %copy-start.9 = (bf16[256,2048]{1,0:T(8,128)(2,1)S(1)}, bf16[256,2048]{1,0:T(8,128)(2,1)}, u32[]{:S(2)}) copy-start(bf16[256,2048]{1,0:T(8,128)(2,1)} %get-tuple-element.33) | copy-start | bytes 3145732
  481.8 1.3 copy-start.4
  483.9 109.2 %collective-permute-start.1 = (bf16[128,2048]{1,0:T(8,128)(2,1)}, bf16[128,2048]{1,0:T(8,128)(2,1)}, u32[]{:S(2)}, u32[]{:S(2)}) collective-permute-start(bf16[128,2048]{1,0:T(8,128)(2,1)} %slice.78), channel_id=1, source_target_pairs={{0,7},{1,6},{2,5},{3,4},{4,3},{5,2},{6,1},{7,0},{8,15},{9,14},{10,... | collective-permute-start | bytes 1572872 | tf_op jit(solution)/shard_map/ppermute | solution.py:1857
  488.9 105.4 %collective-permute-start = (bf16[128,2048]{1,0:T(8,128)(2,1)}, bf16[128,2048]{1,0:T(8,128)(2,1)S(1)}, u32[]{:S(2)}, u32[]{:S(2)}) collective-permute-start(bf16[128,2048]{1,0:T(8,128)(2,1)} %get-tuple-element.73), channel_id=1, source_target_pairs={{0,7},{1,6},{2,5},{3,4},{4,3},{5,2},{6,1},{7,0},{8,15},{9,14},{10,... | collective-permute-start | bytes 1572872 | tf_op jit(solution)/shard_map/ppermute | solution.py:1758
  593.1 2.3 slice-start
  595.4 1.5 copy-start.11
  597.7 5.2 copy-start.5
  602.9 3.2 copy-start.6
  609.7 1.4 copy-start.12
Sparse Core Ops, SparseCore 0:
  10.9 87.4 all-gather.5
  100.0 89.5 all-gather.7
  406.7 60.8 all-gather.9
  469.3 53.2 all-gather.11
  524.2 69.0 all-gather.13

commit v3 on v2

--- a/solution.py
+++ b/solution.py
@@ -171,29 +171,18 @@
     )(blocks, q, kv_all)
 
 
-def attend_back_kernel(
-    q_ref,
-    kv_ref,
-    o_ref,
-    do_ref,
-    total_ref,
-    cos_q,
-    sin_q,
-    cos_kv,
-    sin_kv,
-    grad_ref,
-    dkv_acc,
-    own_part,
-    twin_out,
-    twin_in,
-    sum_out,
-    sum_in,
-    mine,
-    twin_send,
-    twin_recv,
-    sum_send,
-    sum_recv,
-):
+def attend_back_kernel(height, *refs):
+    if height:
+        low_ref, grad_ref, proj_ref = refs[9:12]
+        attend_back_body(refs[:9], grad_ref, refs[12:23], (height, low_ref, proj_ref, refs[23:]))
+    else:
+        attend_back_body(refs[:9], refs[9], refs[10:], None)
+
+
+def attend_back_body(inputs, grad_ref, scratch, product):
+    q_ref, kv_ref, o_ref, do_ref, total_ref, cos_q, sin_q, cos_kv, sin_kv = inputs
+    (dkv_acc, own_part, twin_out, twin_in, sum_out, sum_in, mine) = scratch[:7]
+    (twin_send, twin_recv, sum_send, sum_recv) = scratch[7:]
     subs = q_ref.shape[0] // BLOCK
     chips = lax.axis_size("mp") // 2
     me = lax.axis_index("mp")
@@ -212,7 +201,13 @@
             device_id=(row, 2 * ((chip + step) % chips) + core),
             device_id_type=MESH,
         )
-    pl.semaphore_wait(barrier, chips)
+    if product:
+        down, across = row // 2, row % 2
+        for device in ((row + 1 - 2 * across, me), ((1 - down) * 2 + across, me)):
+            pl.semaphore_signal(barrier, inc=1, device_id=device, device_id_type=MESH)
+    pl.semaphore_wait(barrier, chips + 2 if product else chips)
+    if product:
+        reducer = Reducer(product[0], o_ref, product[1], None, product[2], product[3])
 
     def twin_copy(g):
         return pltpu.make_async_remote_copy(
@@ -245,6 +240,8 @@
         mine[g] = own_part[g % 2, chip] + twin_in[g, chip].astype(F32)
 
     def head_step(g, _):
+        if product:
+            reducer.round(g)
         cols = pl.ds(pl.multiple_of(g * width, width), width)
         pair = pl.ds(pl.multiple_of(g * SLAB, SLAB), SLAB)
         dkv_acc[...] = jnp.zeros_like(dkv_acc)
@@ -312,6 +309,8 @@
 
     lax.fori_loop(0, KV_HEADS, head_step, 0)
     combine(KV_HEADS - 1)
+    if product:
+        lax.fori_loop(KV_HEADS, chips + 3, reducer.round, 0)
 
     for g in range(KV_HEADS):
         total = mine[g]
@@ -327,20 +326,29 @@
             sum_copy(g, step).wait_send()
     for g in range(KV_HEADS - 2, KV_HEADS):
         twin_copy(g).wait_send()
-
-
-def attend_back(q, kv_all, o, grad_o, totals, tables):
+    if product:
+        reducer.close()
+
+
+def attend_back(q, kv_all, o, grad_o, totals, tables, low):
     rows = q.shape[0]
     subs = rows // BLOCK
     chips = lax.axis_size("mp") // 2
     vmem = pl.BlockSpec(memory_space=pltpu.VMEM)
     dma = pltpu.SemaphoreType.DMA
     part = (chips, subs, BLOCK, SLAB)
+    args = (q, kv_all, o, grad_o, totals, *tables)
+    out_shape = (jax.ShapeDtypeStruct((rows, Q_WIDTH + 2 * KV_WIDTH), BF16),)
+    height, more = 0, []
+    if lax.axis_size("rows") == 4:
+        height, product, more = reducer_buffers(o, low)
+        args += (low,)
+        out_shape += (product,)
     return pl.pallas_call(
-        attend_back_kernel,
-        in_specs=[vmem] * 9,
-        out_specs=vmem,
-        out_shape=jax.ShapeDtypeStruct((rows, Q_WIDTH + 2 * KV_WIDTH), BF16),
+        functools.partial(attend_back_kernel, height),
+        in_specs=[vmem] * len(args),
+        out_specs=(vmem,) * len(out_shape),
+        out_shape=out_shape,
         scratch_shapes=[
             pltpu.VMEM((LEN, SLAB), F32),
             pltpu.VMEM((2,) + part, F32),
@@ -353,7 +361,8 @@
             dma((KV_HEADS,)),
             dma((KV_HEADS, chips - 1)),
             dma((KV_HEADS, chips - 1)),
-        ],
+        ]
+        + more,
         compiler_params=pltpu.CompilerParams(
             collective_id=3, has_side_effects=True, vmem_limit_bytes=VMEM_LIMIT
         ),
@@ -361,7 +370,7 @@
             flops=120_000_000_000, bytes_accessed=12_000_000, transcendentals=6_000_000
         ),
         name="attend_back",
-    )(q, kv_all, o, grad_o, totals, *tables)
+    )(*args)
 
 
 def pack_kv(columns):
@@ -880,8 +889,8 @@
             on_chip(jnp.where(chip == 0, 1, chips - 2)),
         )
 
-    def send_parts():
-        for far in (True, False):
+    def send_parts(far):
+        if True:
             for step in range(1, chips):
                 other = (chip + step) % chips
                 beyond = end_far(chip, other)
@@ -955,6 +964,7 @@
                     fetch(part_in.at[other, sub], 0).wait()
                     part_sum[lines, :] = part_sum[lines, :] + piece(0)[...].astype(F32)
 
+    send_parts(True)
     for a, source in enumerate((dgate, dup)):
 
         def tall_out(j):
@@ -985,7 +995,7 @@
         stage_one(a)
         for e in range(a * (chips - 1) // 3, (a + 1) * (chips - 1) // 3):
             pass_on(e)
-    send_parts()
+    send_parts(False)
 
     def cols_copy(j):
         return pltpu.make_async_copy(
@@ -1025,9 +1035,9 @@
     for e in range(2 * (chips - 1) // 3, chips - 1):
         pass_on(e)
     stage_two(0)
+    relay_parts()
     stage_two(1)
     stage_three(0)
-    relay_parts()
     stage_two(2)
     stage_three(1)
     stage_three(2)
@@ -1164,47 +1174,24 @@
     return (*out[3:5], *shards)
 
 
-def reduce_kernel(heights, *refs):
-    count = len(heights)
-    lefts = refs[:count]
-    rights = refs[count : 2 * count]
-    gains = refs[2 * count]
-    outs = refs[2 * count + 1 : 3 * count + 1]
-    scratch = refs[3 * count + 1 :]
-    per = 17
-    chips = lax.axis_size("mp") // 2
-    me = lax.axis_index("mp")
-    row = lax.axis_index("rows")
-    chip = me // 2
-    core = me % 2
-    down, across = row // 2, row % 2
-    twin = (row, me + 1 - 2 * core)
-    beside = (row + 1 - 2 * across, me)
-    above = ((1 - down) * 2 + across, me)
-
-    barrier = pltpu.get_barrier_semaphore()
-    for device in (twin, beside, above):
-        pl.semaphore_signal(barrier, inc=1, device_id=device, device_id_type=MESH)
-    for step in range(1, chips):
-        pl.semaphore_signal(
-            barrier,
-            inc=1,
-            device_id=(row, 2 * ((chip + step) % chips) + core),
-            device_id_type=MESH,
-        )
-    pl.semaphore_wait(barrier, chips + 2)
-
-    streams = []
-    for s in range(count):
-        streams.append((heights[s], rights[s].shape[1], scratch[s * per : (s + 1) * per]))
-    for s in range(count):
-        turned = streams[s][2][0]
-        turned[...] = lefts[s][...].T
-
-    def target(i):
-        return (chip + 1 + i) % chips
-
-    def remote(source, dest, send, recv, device):
+class Reducer:
+    def __init__(self, height, left, right, gains, out, bufs):
+        self.height, self.right, self.gains, self.out = height, right, gains, out
+        (self.turned, self.own, self.twin_out, self.twin_in, self.out1, self.in1) = bufs[:6]
+        (self.out2, self.in2, self.out3, self.in3) = bufs[6:10]
+        (self.s0, self.r0, self.s1, self.r1, self.s2, self.r2, self.s3) = bufs[10:]
+        self.cols = self.own.shape[-1]
+        self.chips = lax.axis_size("mp") // 2
+        me = lax.axis_index("mp")
+        self.row = lax.axis_index("rows")
+        self.chip, self.core = me // 2, me % 2
+        self.down, self.across = self.row // 2, self.row % 2
+        self.twin = (self.row, me + 1 - 2 * self.core)
+        self.beside = (self.row + 1 - 2 * self.across, me)
+        self.above = ((1 - self.down) * 2 + self.across, me)
+        self.turned[...] = left[...].T
+
+    def remote(self, source, dest, send, recv, device):
         return pltpu.make_async_remote_copy(
             src_ref=source,
             dst_ref=dest,
@@ -1214,149 +1201,161 @@
             device_id_type=MESH,
         )
 
-    def copies(s, i):
-        height, cols, bufs = streams[s]
-        (_, own, twin_out, twin_in, out1, in1, out2, in2, out3, in3, s0, r0, s1, r1, s2, r2, s3) = bufs
-        goal = target(i)
-        return dict(
-            twin=lambda: remote(twin_out.at[i], twin_in.at[i], s0.at[i], r0.at[i], twin),
-            first=lambda d: remote(
-                out1.at[i, d], in1.at[i, d], s1.at[i, d], r1.at[i, d], (beside, above)[d]
-            ),
-            second=lambda d: remote(
-                out2.at[i, d], in2.at[i, d], s2.at[i, d], r2.at[i, d], (above, beside)[d]
-            ),
-            last=lambda: remote(
-                out3.at[i], in3.at[i], s3.at[0, i], s3.at[1, i], (row, 2 * goal + core)
-            ),
-        )
-
-    def make(s, i):
-        height, cols, bufs = streams[s]
-        turned, own, twin_out = bufs[:3]
-        goal = target(i)
+    def goal(self, i):
+        return (self.chip + 1 + i) % self.chips
+
+    def twin_copy(self, i):
+        return self.remote(
+            self.twin_out.at[i], self.twin_in.at[i], self.s0.at[i], self.r0.at[i], self.twin
+        )
+
+    def first_copy(self, i, d):
+        return self.remote(
+            self.out1.at[i, d],
+            self.in1.at[i, d],
+            self.s1.at[i, d],
+            self.r1.at[i, d],
+            (self.beside, self.above)[d],
+        )
+
+    def second_copy(self, i, d):
+        return self.remote(
+            self.out2.at[i, d],
+            self.in2.at[i, d],
+            self.s2.at[i, d],
+            self.r2.at[i, d],
+            (self.above, self.beside)[d],
+        )
+
+    def last_copy(self, i):
+        return self.remote(
+            self.out3.at[i],
+            self.in3.at[i],
+            self.s3.at[0, i],
+            self.s3.at[1, i],
+            (self.row, 2 * self.goal(i) + self.core),
+        )
+
+    def make(self, i):
+        height = self.height
         for r in range(4):
-            first = (r * chips + goal) * 2 * height
+            first = (r * self.chips + self.goal(i)) * 2 * height
             lines = pl.ds(pl.multiple_of(first, 16), 2 * height)
-            block = dot(turned[lines, :], rights[s][...])
-            spare = cols_of(s) - block.shape[1]
+            block = dot(self.turned[lines, :], self.right[...])
+            spare = self.cols - block.shape[1]
             if spare:
-                piece = gains[:, pl.ds(pl.multiple_of(first, 128), 2 * height)]
+                piece = self.gains[:, pl.ds(pl.multiple_of(first, 128), 2 * height)]
                 piece = jnp.concatenate(
                     [piece, jnp.zeros((spare - piece.shape[0], 2 * height), F32)], axis=0
                 ).T
                 block = jnp.concatenate([block, piece], axis=1)
 
-            @pl.when(core == 0)
+            @pl.when(self.core == 0)
             def _():
-                own[i, r] = block[:height]
-                twin_out[i, r] = block[height:].astype(BF16)
-
-            @pl.when(core == 1)
+                self.own[i, r] = block[:height]
+                self.twin_out[i, r] = block[height:].astype(BF16)
+
+            @pl.when(self.core == 1)
             def _():
-                own[i, r] = block[height:]
-                twin_out[i, r] = block[:height].astype(BF16)
-
-        copies(s, i)["twin"]().start()
-
-    def cols_of(s):
-        return streams[s][2][1].shape[-1]
-
-    def first_stage(s, i):
-        height, cols, bufs = streams[s]
-        (_, own, twin_out, twin_in, out1, in1, out2, in2, out3, in3, s0, r0, s1, r1, s2, r2, s3) = bufs
-        half = cols_of(s) // 2
-        c = copies(s, i)
-        c["twin"]().wait_recv()
+                self.own[i, r] = block[height:]
+                self.twin_out[i, r] = block[:height].astype(BF16)
+
+        self.twin_copy(i).start()
+
+    def first_stage(self, i):
+        half = self.cols // 2
+        own = self.own
+        self.twin_copy(i).wait_recv()
         for r in range(4):
-            own[i, r] = own[i, r] + twin_in[i, r].astype(F32)
+            own[i, r] = own[i, r] + self.twin_in[i, r].astype(F32)
         for k in range(2):
-            out1[i, 0, k] = own[i, k * 2 + 1 - across, :, :half].astype(BF16)
-            out1[i, 1, k] = own[i, (1 - down) * 2 + k, :, half:].astype(BF16)
+            self.out1[i, 0, k] = own[i, k * 2 + 1 - self.across, :, :half].astype(BF16)
+            self.out1[i, 1, k] = own[i, (1 - self.down) * 2 + k, :, half:].astype(BF16)
         for d in range(2):
-            c["first"](d).start()
-
-    def second_stage(s, i):
-        height, cols, bufs = streams[s]
-        (_, own, twin_out, twin_in, out1, in1, out2, in2, out3, in3, s0, r0, s1, r1, s2, r2, s3) = bufs
-        half = cols_of(s) // 2
-        c = copies(s, i)
+            self.first_copy(i, d).start()
+
+    def second_stage(self, i):
+        half = self.cols // 2
         for d in range(2):
-            c["first"](d).wait_recv()
-        other_down = (1 - down) * 2 + across
-        other_across = down * 2 + 1 - across
-        out2[i, 0] = (own[i, other_down, :, :half] + in1[i, 0, 1 - down].astype(F32)).astype(BF16)
-        out2[i, 1] = (own[i, other_across, :, half:] + in1[i, 1, 1 - across].astype(F32)).astype(BF16)
+            self.first_copy(i, d).wait_recv()
+        above = (1 - self.down) * 2 + self.across
+        beside = self.down * 2 + 1 - self.across
+        self.out2[i, 0] = (
+            self.own[i, above, :, :half] + self.in1[i, 0, 1 - self.down].astype(F32)
+        ).astype(BF16)
+        self.out2[i, 1] = (
+            self.own[i, beside, :, half:] + self.in1[i, 1, 1 - self.across].astype(F32)
+        ).astype(BF16)
         for d in range(2):
-            c["second"](d).start()
-
-    def third_stage(s, i):
-        height, cols, bufs = streams[s]
-        (_, own, twin_out, twin_in, out1, in1, out2, in2, out3, in3, s0, r0, s1, r1, s2, r2, s3) = bufs
-        half = cols_of(s) // 2
-        c = copies(s, i)
+            self.second_copy(i, d).start()
+
+    def third_stage(self, i):
+        half = self.cols // 2
         for d in range(2):
-            c["second"](d).wait_recv()
-        left = own[i, row, :, :half] + in1[i, 0, down].astype(F32) + in2[i, 0].astype(F32)
-        right = own[i, row, :, half:] + in1[i, 1, across].astype(F32) + in2[i, 1].astype(F32)
-
-        @pl.when(i < chips - 1)
-        def _():
-            out3[i, :, :half] = left.astype(BF16)
-            out3[i, :, half:] = right.astype(BF16)
-            c["last"]().start()
-
-        @pl.when(i == chips - 1)
-        def _():
-            outs[s][:, :half] = left
-            outs[s][:, half:] = right
-
-    def round_step(n, _):
-        for stage, work in enumerate((make, first_stage, second_stage, third_stage)):
-
-            @pl.when((n >= stage) & (n < chips + stage))
+            self.second_copy(i, d).wait_recv()
+        left = (
+            self.own[i, self.row, :, :half]
+            + self.in1[i, 0, self.down].astype(F32)
+            + self.in2[i, 0].astype(F32)
+        )
+        right = (
+            self.own[i, self.row, :, half:]
+            + self.in1[i, 1, self.across].astype(F32)
+            + self.in2[i, 1].astype(F32)
+        )
+
+        @pl.when(i < self.chips - 1)
+        def _():
+            self.out3[i, :, :half] = left.astype(BF16)
+            self.out3[i, :, half:] = right.astype(BF16)
+            self.last_copy(i).start()
+
+        @pl.when(i == self.chips - 1)
+        def _():
+            self.out[:, :half] = left
+            self.out[:, half:] = right
+
+    def round(self, n, _=None):
+        stages = (self.make, self.first_stage, self.second_stage, self.third_stage)
+        for stage, work in enumerate(stages):
+
+            @pl.when((n >= stage) & (n < self.chips + stage))
             def _():
-                for s in range(count):
-                    work(s, n - stage)
+                work(n - stage)
 
         return 0
 
-    lax.fori_loop(0, chips + 3, round_step, 0)
-    for s in range(count):
-        in3 = streams[s][2][9]
-        for i in range(chips - 1):
-            copies(s, i)["last"]().wait_recv()
-            outs[s][...] = outs[s][...] + in3[i].astype(F32)
-
-    def finish(i, _):
-        for s in range(count):
-            c = copies(s, i)
-            c["twin"]().wait_send()
+    def close(self):
+        for i in range(self.chips - 1):
+            self.last_copy(i).wait_recv()
+            self.out[...] = self.out[...] + self.in3[i].astype(F32)
+
+        def finish(i, _):
+            self.twin_copy(i).wait_send()
             for d in range(2):
-                c["first"](d).wait_send()
-                c["second"](d).wait_send()
-
-            @pl.when(i < chips - 1)
+                self.first_copy(i, d).wait_send()
+                self.second_copy(i, d).wait_send()
+
+            @pl.when(i < self.chips - 1)
             def _():
-                c["last"]().wait_send()
-
-        return 0
-
-    lax.fori_loop(0, chips, finish, 0)
-
-
-def reduce_products(pairs, gains):
+                self.last_copy(i).wait_send()
+
+            return 0
+
+        lax.fori_loop(0, self.chips, finish, 0)
+
+
+def reducer_buffers(left, right):
     chips = lax.axis_size("mp") // 2
     shards = lax.axis_size("rows") * lax.axis_size("mp")
-    heights = tuple(left.shape[1] // shards for left, _ in pairs)
+    height = left.shape[1] // shards
+    cols = -(-right.shape[1] // 256) * 256
+    half = cols // 2
     dma = pltpu.SemaphoreType.DMA
-    out_shape, scratch = [], []
-    for s, (left, right) in enumerate(pairs):
-        height = heights[s]
-        cols = -(-right.shape[1] // 256) * 256
-        half = cols // 2
-        out_shape.append(jax.ShapeDtypeStruct((height, cols), F32))
-        scratch += [
+    return (
+        height,
+        jax.ShapeDtypeStruct((height, cols), F32),
+        [
             pltpu.VMEM((left.shape[1], left.shape[0]), BF16),
             pltpu.VMEM((chips, 4, height, cols), F32),
             pltpu.VMEM((chips, 4, height, cols), BF16),
@@ -1374,13 +1373,38 @@
             dma((chips, 2)),
             dma((chips, 2)),
             dma((2, chips)),
-        ]
+        ],
+    )
+
+
+def reduce_kernel(height, left, right, gains, out, *bufs):
+    chips = lax.axis_size("mp") // 2
+    me = lax.axis_index("mp")
+    row = lax.axis_index("rows")
+    chip, core = me // 2, me % 2
+    down, across = row // 2, row % 2
+    barrier = pltpu.get_barrier_semaphore()
+    devices = [
+        (row, me + 1 - 2 * core),
+        (row + 1 - 2 * across, me),
+        ((1 - down) * 2 + across, me),
+    ] + [(row, 2 * ((chip + step) % chips) + core) for step in range(1, chips)]
+    for device in devices:
+        pl.semaphore_signal(barrier, inc=1, device_id=device, device_id_type=MESH)
+    pl.semaphore_wait(barrier, chips + 2)
+    reducer = Reducer(height, left, right, gains, out, bufs)
+    lax.fori_loop(0, chips + 3, reducer.round, 0)
+    reducer.close()
+
+
+def reduce_product(left, right, gains):
+    height, out_shape, scratch = reducer_buffers(left, right)
     vmem = pl.BlockSpec(memory_space=pltpu.VMEM)
     return pl.pallas_call(
-        functools.partial(reduce_kernel, heights),
-        out_shape=tuple(out_shape),
-        in_specs=[vmem] * (2 * len(pairs) + 1),
-        out_specs=(vmem,) * len(pairs),
+        functools.partial(reduce_kernel, height),
+        out_shape=out_shape,
+        in_specs=[vmem] * 3,
+        out_specs=vmem,
         scratch_shapes=scratch,
         compiler_params=pltpu.CompilerParams(
             collective_id=2, has_side_effects=True, vmem_limit_bytes=VMEM_LIMIT
@@ -1388,8 +1412,8 @@
         cost_estimate=pl.CostEstimate(
             flops=50_000_000_000, bytes_accessed=10_000_000, transcendentals=0
         ),
-        name="reduce_products",
-    )(*[left for left, _ in pairs], *[right for _, right in pairs], gains)
+        name="reduce_product",
+    )(left, right, gains)
 
 
 def natural(device, sub, subs):
@@ -1833,15 +1857,12 @@
     )
     grad_middle_low = grad_middle.astype(BF16)
     if row_groups == 4:
-        gate_grad, up_grad, down_grad, grad_middle_low = lax.optimization_barrier(
-            (gate_grad, up_grad, down_grad, grad_middle_low)
-        )
         gate_grad, up_grad, down_grad = (
             lax.all_gather(g, "rows", axis=0, tiled=True)
             for g in (gate_grad, up_grad, down_grad)
         )
     grad_o = dot_nt(grad_middle_low, out_full).astype(BF16)
-    grad_qkv = attend_back(q, kv_all, o, grad_o, totals, tables)
+    grad_qkv, *proj = attend_back(q, kv_all, o, grad_o, totals, tables, grad_middle_low)
     grad_normed_one = dot_nt(grad_qkv, qkv_full)
     scaled_one = grad_normed_one * gain_one
     attn_gain_part = jnp.sum(grad_normed_one * residual * inverse_one, axis=0)
@@ -1862,9 +1883,8 @@
         [attn_gain_part[None], ffn_gain_part[None], jnp.zeros((6, width), F32)], axis=0
     )
     if row_groups == 4:
-        part, proj_grad = reduce_products(
-            ((normed_one, grad_qkv), (o, grad_middle_low)), gain_parts
-        )
+        proj_grad = proj[0]
+        part = reduce_product(normed_one, grad_qkv, gain_parts)
     else:
         part = jnp.concatenate(
             [dot_tn(normed_one, grad_qkv), gain_parts.T, jnp.zeros((width, 120), F32)], axis=1
@@ -1876,10 +1896,12 @@
     qkv_grad = unpack_kv(part[:, :qkv_cols])
     attn_gain_grad = part[:, qkv_cols]
     ffn_gain_grad = part[:, qkv_cols + 1]
-    gate_grad, up_grad, down_grad, part = lax.optimization_barrier(
-        (gate_grad, up_grad, down_grad, part)
-    )
-    gate_grad, up_grad, down_grad = (g.astype(F32) for g in (gate_grad, up_grad, down_grad))
+    gate_grad, part = lax.optimization_barrier((gate_grad, part))
+    gate_grad = gate_grad.astype(F32)
+    up_grad, part = lax.optimization_barrier((up_grad, part))
+    up_grad = up_grad.astype(F32)
+    down_grad, part = lax.optimization_barrier((down_grad, part))
+    down_grad = down_grad.astype(F32)
     qkv_grad = unpack_kv(part[:, :qkv_cols])
     attn_gain_grad = part[:, qkv_cols]
     ffn_gain_grad = part[:, qkv_cols + 1]

time: 622 us -> 601 us (0.966)
  Pallas kernels: 535 us -> 507 us
    pallas_call x2, Pallas kernels: 165 us -> 145 us  [the longest x1 73.8 us: reduce_product(): pl.pallas_call(functools.partial(reduce_kernel, height), out_shape=out_sh...]
    pallas_call x1, Pallas kernels: 210 us -> 202 us  [ffn(): pl.pallas_call(functools.partial(ffn_kernel, subs, quad), out_shape=(jax....]
  transfers between devices with their start and end apart: 7 -> 7, of which waited for: 1 -> 1; matrix products, arithmetic and copies ran while one was open for 5% -> 7% of each run, Pallas kernels for 53% -> 51%
where the time goes in v3:
time: 601 us; the launch traced here: 593 us
  Pallas kernels  507 us (84%)
  other arithmetic  30.2 us (5%)
  between operations  16.3 us (3%)
  matrix products  16.2 us (3%)
  local copies, waits for them, and re-layouts  12.4 us (2%)
    pallas_call x1, Pallas kernels, ffn(): pl.pallas_call(functools.partial(ffn_kernel, subs, quad), out_shape=(jax....  202 us
    pallas_call x1, Pallas kernels, front(): pl.pallas_call(front_kernel, out_shape=(jax.ShapeDtypeStruct((total, cols...  134 us
    pallas_call x1, Pallas kernels, reduce_product(): pl.pallas_call(functools.partial(reduce_kernel, height), out_shape=out_sh...  73.8 us
    pallas_call x1, Pallas kernels, attend_back(): pl.pallas_call(functools.partial(attend_back_kernel, height), in_specs=[v...  71.4 us
    pallas_call x1, Pallas kernels, attend(): pl.pallas_call(attend_kernel, grid_spec=pltpu.PrefetchScalarGridSpec(num_...  25.6 us
  transfers between devices with their start and end apart: 7, of which 1 were waited for; matrix products, arithmetic and copies ran while one was open for 7% of the time, Pallas kernels for 51%

profile of v3, /device:TPU:0, one launch (start us, length us, event | category | flops | bytes accessed | tf_op | source)
XLA Modules:
  0.0 593.4 jit_solution(12951396114007302008)
XLA Ops:
  7.2 0.0 all-gather.6.cloned.1.call-start
  7.3 0.7 all-gather.6.cloned.1.call-update
  7.9 0.0 all-gather.8.cloned.1.call-start
  8.0 0.7 all-gather.8.cloned.1.call-update
  8.7 0.0 all-gather.14.cloned.1.call-start
  8.7 0.9 slice.50
  9.6 0.1 pad.13.clone
  9.7 0.1 pad.16.clone
  10.5 0.2 copy.30
  10.6 0.2 copy.25
  10.8 0.2 reshape.100
  10.9 0.1 copy.26
  11.1 0.1 copy.27
  11.2 0.8 concatenate.46.shard_ref
  12.0 0.6 broadcast_multiply_fusion.2
  12.6 0.1 convert_bitcast_fusion
  12.7 0.5 fusion.10
  13.2 1.0 fusion.8
  14.3 134.0 %front.1 = (bf16[2048,2048]{1,0:T(8,128)(2,1)}, f32[8,2048]{1,0:T(8,128)}, bf16[256,2048]{1,0:T(8,128)(2,1)}, bf16[256,2048]{1,0:T(8,128)(2,1)}, f32[256,1]{1,0:...) custom-call(bf16[64,2048]{1,0:T(8,128)(2,1)} %concatenate.46.shard_ref, bf16[256,2048]{1,0:T(8,128)(2,1)} %x_ref.1, ...), custom_call_target="tpu_custom_call" | custom-call | flops 30000001024 | bytes 12000000 | tf_op jit(solution)/shard_map/front/pallas_call | solution.py:1712
  148.2 1.6 fusion.15
  149.9 0.6 convert_reduce_fusion
  151.1 0.6 fusion.11
  152.4 25.6 %attend.1 = (bf16[256,1280]{1,0:T(8,128)(2,1)}, f32[5,2,512]{2,1,0:T(2,128)}) custom-call(s32[2]{0:T(128)} %get-tuple-element.64.block_ref, bf16[256,1280]{1,0:T(8,128)(2,1)} %get-tuple-element.32.q_ref.refs_0_, bf16[2048,640]{1,0:T(8,128)(2,1)} %get-tuple-element.33.kv_ref.refs_1_), custom_call_target="tpu_custom_call" | custom-call | flops 60000002048 | bytes 8000000 | tf_op jit(solution)/shard_map/attend/pallas_call | solution.py:148
  178.1 4.4 multiply_reduce_fusion.2
  182.5 1.3 copy-done
  183.8 1.2 multiply_convert_fusion.x_ref
  185.0 4.6 all-gather.8.cloned.1.call-done.cot_ref
  189.6 201.9 %ffn.1 = (bf16[8,128,2048]{2,1,0:T(8,128)(2,1)}, bf16[4,2,128,2048]{3,2,1,0:T(8,128)(2,1)}, bf16[4,2,128,2048]{3,2,1,0:T(8,128)(2,1)}, f32[256,2048]{1,0:T(8,128...) custom-call(f32[1]{0:T(128)} %bitcast.9.scale_ref, ...), custom_call_target="tpu_custom_call" | custom-call | flops 60000002048 | bytes 60000000 | tf_op jit(solution)/shard_map/ffn/pallas_call | solution.py:1115
  391.5 0.0 all-gather.14.cloned.1.call-update
  391.5 0.0 all-gather.12.cloned.1.call-start
  391.6 0.1 pad.4.clone
  391.7 0.1 fusion.12
  391.8 2.8 multiply_reduce_fusion
  394.6 0.0 all-gather.12.cloned.1.call-update
  394.7 0.0 all-gather.10.cloned.1.call-start
  394.7 1.4 constant_dynamic-slice_fusion.1
  396.1 0.4 copy-done.1
  396.5 4.8 fusion.13
  401.3 5.3 convolution_convert_fusion.refs_3_
  406.6 71.4 %attend_back.1 = (bf16[256,1920]{1,0:T(8,128)(2,1)}, f32[40,2048]{1,0:T(8,128)}) custom-call(bf16[256,1280]{1,0:T(8,128)(2,1)} %get-tuple-element.32.q_ref.refs_0_, bf16[2048,640]{1,0:T(8,128)(2,1)} %get-tuple-element.33.kv_ref.refs_1_, bf16[256,1280]{1,0:T(8,128)(2,1)} %get-tuple-element.34.refs_2_, bf16[256,1280]{1,0:T(8,128)(2,1)} %convolution_convert_fusion.refs_3_, ...), custom_call_target="tpu_custom_call" | custom-call | flops 120000004096 | bytes 12000000 | tf_op jit(solution)/shard_map/attend_back/pallas_call | solution.py:347
  478.0 0.0 copy-start.2
  478.0 6.5 %fusion.6 = (f32[2048]{0:T(1024)S(1)}, f32[256]{0:T(256)S(1)}, f32[256,2048]{1,0:T(8,128)S(1)}) fusion(bf16[256,2048]{1,0:T(8,128)(2,1)} %get-tuple-element.31, f32[256]{0:T(256)S(1)} %get-tuple-element.59, f32[2048]{0:T(1024)S(1)} %bitcast.32, bf16[256,1920]{1,0:T(8,128)(2,1)} %get-tuple-element.40.right, bf16[2048,2048]{1,0:T(8,128)(2,1)} %get-tuple-element.41), kind=kOutput, calls=%fused_computation.11 | convolution fusion | flops 2016933632 | bytes 12011520 | tf_op jit(solution)/shard_map/dot_general | solution.py:395
  484.5 0.6 fusion.3
  485.1 0.0 copy-start.3
  485.1 1.3 copy-done.3
  486.4 0.9 slice.78
  487.3 5.3 collective-permute-start.1
  492.6 0.9 fusion.14
  493.4 0.0 all-gather.10.cloned.1.call-update
  493.4 0.7 maximum_maximum_fusion.gains
  494.1 73.8 %reduce_product.1 = f32[64,2048]{1,0:T(8,128)} custom-call(bf16[256,2048]{1,0:T(8,128)(2,1)} %get-tuple-element.45.left, bf16[256,1920]{1,0:T(8,128)(2,1)} %get-tuple-element.40.right, f32[8,2048]{1,0:T(8,128)} %maximum_maximum_fusion.gains), custom_call_target="tpu_custom_call" | custom-call | flops 49999998976 | bytes 10000000 | tf_op jit(solution)/shard_map/reduce_product/pallas_call | solution.py:1403
  568.0 0.0 slice-start
  568.0 1.2 convert_element_type.62
  569.2 1.1 pad_maximum_fusion.1
  570.3 1.5 pad_maximum_fusion
  571.8 0.7 slice_reduce_fusion
  572.5 5.6 convert_element_type.65
  578.1 3.2 convert_element_type.64
  581.3 3.2 convert_element_type.63
  584.5 0.2 reshape.102
  584.7 0.2 copy.28
  584.9 0.1 copy.29
  585.1 0.8 pad_maximum_fusion.2
  585.9 0.7 copy.33
  (51 shorter events, 0.1 us)
Async XLA Ops:
  7.2 4.0 slice-start.3
  7.2 3.8 copy-start.13
  7.2 3.9 copy-start.14
  7.2 170.9 %all-gather.6.cloned.1.call-start = ((), (), s32[]{:S(2)}) async-start(), calls=%async_computation | async-start | bytes 5406720 | tf_op jit(solution)/shard_map/all_gather | solution.py:1812
  7.9 181.7 %all-gather.8.cloned.1.call-start = ((), (), s32[]{:S(2)}) async-start(), calls=%async_computation.1 | async-start | bytes 9437184 | tf_op jit(solution)/shard_map/all_gather | solution.py:1811
  8.7 563.1 %all-gather.14.cloned.1.call-start = ((), (), s32[]{:S(2)}) async-start(), calls=%async_computation.4 | async-start | bytes 3932160 | tf_op jit(solution)/shard_map/all_gather | solution.py:1861
  14.3 136.9 %copy-start.15 = (f32[4]{0:T(128)S(1)}, f32[4]{0:T(128)}, u32[]{:S(2)}) copy-start(f32[4]{0:T(128)} %param.14) | copy-start | bytes 52
  152.4 25.6 %copy-start.7 = (bf16[256,2048]{1,0:T(8,128)(2,1)S(1)}, bf16[256,2048]{1,0:T(8,128)(2,1)}, u32[]{:S(2)}) copy-start(bf16[256,2048]{1,0:T(8,128)(2,1)} %get-tuple-element.31) | copy-start | bytes 3145732
  182.5 1.3 copy-start
  189.6 202.1 %copy-start.11 = (f32[256,1]{1,0:T(8,128)S(1)}, f32[256,1]{1,0:T(8,128)}, u32[]{:S(2)}) copy-start(f32[256,1]{1,0:T(8,128)} %get-tuple-element.38) | copy-start | bytes 3076
  391.5 180.3 %all-gather.12.cloned.1.call-start = ((), (), s32[]{:S(2)}) async-start(), calls=%async_computation.3 | async-start | bytes 3932160 | tf_op jit(solution)/shard_map/all_gather | solution.py:1861
  394.6 1.9 copy-start.1
  394.7 177.2 %all-gather.10.cloned.1.call-start = ((), (), s32[]{:S(2)}) async-start(), calls=%async_computation.2 | async-start | bytes 3932160 | tf_op jit(solution)/shard_map/all_gather | solution.py:1861
  401.3 5.3 copy-start.9
  406.6 71.4 %copy-start.12 = (f32[1,2048]{1,0:T(1,128)S(1)}, f32[1,2048]{1,0:T(1,128)}, u32[]{:S(2)}) copy-start(f32[1,2048]{1,0:T(1,128)} %get-tuple-element.74) | copy-start | bytes 24580
  478.0 6.5 %copy-start.2 = (f32[256,2048]{1,0:T(8,128)S(1)}, f32[256,2048]{1,0:T(8,128)}, u32[]{:S(2)}) copy-start(f32[256,2048]{1,0:T(8,128)} %get-tuple-element.62) | copy-start | bytes 6291460
  478.0 6.5 %copy-start.8 = (bf16[256,2048]{1,0:T(8,128)(2,1)S(1)}, bf16[256,2048]{1,0:T(8,128)(2,1)}, u32[]{:S(2)}) copy-start(bf16[256,2048]{1,0:T(8,128)(2,1)} %get-tuple-element.31) | copy-start | bytes 3145732
  485.1 1.3 copy-start.3
  487.3 80.7 %collective-permute-start.1 = (bf16[128,2048]{1,0:T(8,128)(2,1)}, bf16[128,2048]{1,0:T(8,128)(2,1)}, u32[]{:S(2)}, u32[]{:S(2)}) collective-permute-start(bf16[128,2048]{1,0:T(8,128)(2,1)} %slice.78), channel_id=1, source_target_pairs={{0,7},{1,6},{2,5},{3,4},{4,3},{5,2},{6,1},{7,0},{8,15},{9,14},{10,... | collective-permute-start | bytes 1572872 | tf_op jit(solution)/shard_map/ppermute | solution.py:1878
  493.4 75.8 %collective-permute-start = (bf16[128,2048]{1,0:T(8,128)(2,1)}, bf16[128,2048]{1,0:T(8,128)(2,1)S(1)}, u32[]{:S(2)}, u32[]{:S(2)}) collective-permute-start(bf16[128,2048]{1,0:T(8,128)(2,1)} %get-tuple-element.69), channel_id=1, source_target_pairs={{0,7},{1,6},{2,5},{3,4},{4,3},{5,2},{6,1},{7,0},{8,15},{9,14},{10,... | collective-permute-start | bytes 1572872 | tf_op jit(solution)/shard_map/ppermute | solution.py:1782
  568.0 2.3 slice-start
  570.3 1.5 copy-start.6
  572.5 5.6 copy-start.5
  578.1 3.2 copy-start.4
  581.3 3.2 slice-start.1
  581.3 3.7 slice-start.2
  584.5 1.4 copy-start.10
Sparse Core Ops, SparseCore 0:
  10.9 87.4 all-gather.5
  100.0 89.5 all-gather.7
  391.6 48.0 all-gather.13
  441.4 49.6 all-gather.11
  493.6 71.3 all-gather.9

commit v4 on v3

--- a/solution.py
+++ b/solution.py
@@ -430,12 +430,21 @@
     down_out,
     *rest,
 ):
+    rest, weights, weight_sem = rest[:-4], rest[-4:-1], rest[-1]
+    loads = [
+        pltpu.make_async_copy(source, target, weight_sem.at[i])
+        for i, (source, target) in enumerate(zip((gate_ref, up_ref, down_ref), weights))
+    ]
+    for copy in loads:
+        copy.start()
+    gate_ref, up_ref, down_ref = weights
     slots = rest[:9] if quad else ()
     scratch = rest[9:] if quad else rest
     ffn_body(
         subs,
         quad,
         slots,
+        loads,
         scale_ref,
         x_ref,
         cot_ref,
@@ -458,6 +467,7 @@
     subs,
     quad,
     slots,
+    loads,
     scale_ref,
     x_ref,
     cot_ref,
@@ -760,6 +770,8 @@
 
         return 0
 
+    for copy in loads:
+        copy.wait()
     lax.fori_loop(0, units, unit_step, 0)
     reduce_unit(units - 1)
     for i in (units - 2, units - 1):
@@ -833,12 +845,6 @@
             copy.start()
         for copy in copies:
             copy.wait()
-
-    def stage_one(a):
-        if quad:
-            for d in range(2):
-                for k in range(2):
-                    one_copy(a, d, k).start()
 
     def stage_two(a):
         if quad:
@@ -947,22 +953,85 @@
     def total_parts():
         for sub in range(subs):
             lines = slice(sub * rows, (sub + 1) * rows)
-            fetch(part_ref.at[chip * subs + sub], 0).wait()
-            part_sum[lines, :] = piece(0)[...].astype(F32)
-            for step in range(1, chips):
-                other = (chip + step) % chips
-
-                @pl.when(jnp.logical_not(end_far(other, chip)))
-                def _():
-                    remote(
-                        part_ref.at[0],
-                        part_in.at[other, sub],
-                        p_send.at[0],
-                        p_recv.at[other, sub],
-                        twin,
-                    ).wait_recv()
-                    fetch(part_in.at[other, sub], 0).wait()
-                    part_sum[lines, :] = part_sum[lines, :] + piece(0)[...].astype(F32)
+            for base in range(1, chips, 3):
+                group = range(base, min(base + 3, chips))
+                if base == 1:
+                    mine = fetch(part_ref.at[chip * subs + sub], 0)
+                for step in group:
+                    other = (chip + step) % chips
+
+                    @pl.when(jnp.logical_not(end_far(other, chip)))
+                    def _():
+                        remote(
+                            part_ref.at[0],
+                            part_in.at[other, sub],
+                            p_send.at[0],
+                            p_recv.at[other, sub],
+                            twin,
+                        ).wait_recv()
+                        fetch(part_in.at[other, sub], step - base + 1)
+
+                if base == 1:
+                    mine.wait()
+                    part_sum[lines, :] = piece(0)[...].astype(F32)
+                for step in group:
+                    other = (chip + step) % chips
+                    index = step - base + 1
+
+                    @pl.when(jnp.logical_not(end_far(other, chip)))
+                    def _():
+                        pltpu.make_async_copy(
+                            part_in.at[other, sub], piece(index), relay_sem.at[index]
+                        ).wait()
+                        part_sum[lines, :] = part_sum[lines, :] + piece(index)[...].astype(F32)
+
+    def spread_blocks(a, source):
+        def where(j):
+            d, k = j % 2, (j // 2) % 2
+            first = jnp.where(d == 0, k * 2 + 1 - across, (1 - down) * 2 + k)
+            late = jnp.where(j < 6, jnp.where(d == 0, above_row, beside_row), row)
+            return jnp.where(j < 4, first, late), d, k
+
+        def place(ref, block, d):
+            lines = pl.ds(pl.multiple_of(block * tall, tall), tall)
+            return ref.at[lines, pl.ds(pl.multiple_of(d * narrow, narrow), narrow)]
+
+        def block_out(j):
+            block, d, _ = where(j)
+            return pltpu.make_async_copy(
+                tall_buf.at[j % 2], place(wholes[a], block, d), out_sem.at[j % 2]
+            )
+
+        def block_send(j):
+            block, d, k = where(j)
+            target = jnp.where(d == 0, beside_row, above_row)
+            return remote(
+                place(wholes[a], block, d),
+                firsts[a].at[d, k],
+                one_send.at[a, d, k],
+                one_recv.at[a, d, k],
+                (target, me),
+            )
+
+        def block_step(j, _):
+            block, d, _ = where(j)
+            lines = pl.ds(pl.multiple_of(block * tall, tall), tall)
+            cols = pl.ds(pl.multiple_of(d * narrow, narrow), narrow)
+            tall_buf[j % 2] = dot_tn(x_all[:, lines], source[:, cols]).astype(BF16)
+
+            @pl.when(j >= 1)
+            def _():
+                block_out(j - 1).wait()
+
+            @pl.when((j >= 1) & (j <= 4))
+            def _():
+                block_send(j - 1).start()
+
+            block_out(j).start()
+            return 0
+
+        lax.fori_loop(0, 8, block_step, 0)
+        block_out(7).wait()
 
     send_parts(True)
     for a, source in enumerate((dgate, dup)):
@@ -989,10 +1058,12 @@
             tall_out(j).start()
             return 0
 
-        lax.fori_loop(0, steps, tall_step, 0)
-        for j in range(steps - 2, steps):
-            tall_out(j).wait()
-        stage_one(a)
+        if quad:
+            spread_blocks(a, source)
+        else:
+            lax.fori_loop(0, steps, tall_step, 0)
+            for j in range(steps - 2, steps):
+                tall_out(j).wait()
         for e in range(a * (chips - 1) // 3, (a + 1) * (chips - 1) // 3):
             pass_on(e)
     send_parts(False)
@@ -1024,6 +1095,13 @@
         def _():
             wide_out(j - 2).wait()
 
+        if quad:
+
+            @pl.when(j == col_steps // 2 + 1)
+            def _():
+                for k in range(2):
+                    one_copy(2, 0, k).start()
+
         wide_buf[j % 2] = (dot_tn(hid[...], cot_cols[j % 2]) * scale_ref[0]).astype(BF16)
         wide_out(j).start()
         return 0
@@ -1031,7 +1109,9 @@
     lax.fori_loop(0, col_steps, down_step, 0)
     for j in range(max(0, col_steps - 2), col_steps):
         wide_out(j).wait()
-    stage_one(2)
+    if quad:
+        for k in range(2):
+            one_copy(2, 1, k).start()
     for e in range(2 * (chips - 1) // 3, chips - 1):
         pass_on(e)
     stage_two(0)
@@ -1092,10 +1172,10 @@
     subs = max(1, rows_dev // BLOCK)
     rows = rows_dev // subs
     units = chips * subs
-    narrow = ff // 3
-    tall = 512
+    quad = lax.axis_size("rows") == 4
+    narrow = ff // 2 if quad else ff // 3
+    tall = width // 4
     down_cols = 256
-    quad = lax.axis_size("rows") == 4
     extra_out, row_scratch = (), []
     vmem = pl.BlockSpec(memory_space=pltpu.VMEM)
     hbm = pl.BlockSpec(memory_space=pl.ANY)
@@ -1125,7 +1205,7 @@
             jax.ShapeDtypeStruct((ff, width), BF16),
         )
         + extra_out,
-        in_specs=[pl.BlockSpec(memory_space=pltpu.SMEM), vmem, hbm, vmem, vmem, vmem],
+        in_specs=[pl.BlockSpec(memory_space=pltpu.SMEM), vmem, hbm, hbm, hbm, hbm],
         out_specs=(hbm, hbm, hbm, vmem, vmem, hbm, hbm, hbm) + (hbm,) * len(extra_out),
         scratch_shapes=[
             pltpu.VMEM((tokens, width), BF16),
@@ -1158,7 +1238,13 @@
             dma((2,)),
             dma((2,)),
         ]
-        + row_scratch,
+        + row_scratch
+        + [
+            pltpu.VMEM((width, ff), BF16),
+            pltpu.VMEM((width, ff), BF16),
+            pltpu.VMEM((ff, width), BF16),
+            dma((3,)),
+        ],
         compiler_params=pltpu.CompilerParams(
             collective_id=1, has_side_effects=True, vmem_limit_bytes=VMEM_LIMIT
         ),
@@ -1377,35 +1463,105 @@
     )
 
 
-def reduce_kernel(height, left, right, gains, out, *bufs):
-    chips = lax.axis_size("mp") // 2
+def reduce_kernel(height, left, right, gains, half_ref, low_ref, out, swapped, wide_ref, *bufs):
+    bufs, (land, low_buf, wide_buf, swap_sems, low_sems, wide_sems) = bufs[:-6], bufs[-6:]
+    mp = lax.axis_size("mp")
+    chips = mp // 2
     me = lax.axis_index("mp")
     row = lax.axis_index("rows")
     chip, core = me // 2, me % 2
     down, across = row // 2, row % 2
+    mirror = (row, mp - 1 - me)
     barrier = pltpu.get_barrier_semaphore()
     devices = [
+        mirror,
         (row, me + 1 - 2 * core),
         (row + 1 - 2 * across, me),
         ((1 - down) * 2 + across, me),
     ] + [(row, 2 * ((chip + step) % chips) + core) for step in range(1, chips)]
     for device in devices:
         pl.semaphore_signal(barrier, inc=1, device_id=device, device_id_type=MESH)
-    pl.semaphore_wait(barrier, chips + 2)
+    pl.semaphore_wait(barrier, chips + 3)
+    swap = pltpu.make_async_remote_copy(
+        src_ref=half_ref,
+        dst_ref=land,
+        send_sem=swap_sems.at[0],
+        recv_sem=swap_sems.at[1],
+        device_id=mirror,
+        device_id_type=MESH,
+    )
+    swap.start()
     reducer = Reducer(height, left, right, gains, out, bufs)
-    lax.fori_loop(0, chips + 3, reducer.round, 0)
+    tall = low_buf.shape[1]
+    pieces = low_ref.shape[0] // tall
+
+    def low_copy(j):
+        lines = pl.ds(pl.multiple_of(j * tall, tall), tall)
+        return pltpu.make_async_copy(low_ref.at[lines], low_buf.at[j % 2], low_sems.at[j % 2])
+
+    def wide_copy(j):
+        lines = pl.ds(pl.multiple_of(j * tall, tall), tall)
+        return pltpu.make_async_copy(wide_buf.at[j % 2], wide_ref.at[lines], wide_sems.at[j % 2])
+
+    def widen(j, _=None):
+        @pl.when(j + 1 < pieces)
+        def _():
+            low_copy(j + 1).start()
+
+        low_copy(j).wait()
+
+        @pl.when(j >= 2)
+        def _():
+            wide_copy(j - 2).wait()
+
+        wide_buf[j % 2] = low_buf[j % 2].astype(F32)
+        wide_copy(j).start()
+        return 0
+
+    low_copy(0).start()
+
+    def both(n, _):
+        reducer.round(n)
+        widen(n)
+        return 0
+
+    rounds = chips + 3
+    lax.fori_loop(0, min(rounds, pieces), both, 0)
+    if pieces > rounds:
+        lax.fori_loop(rounds, pieces, widen, 0)
+    else:
+        lax.fori_loop(pieces, rounds, reducer.round, 0)
     reducer.close()
-
-
-def reduce_product(left, right, gains):
+    for j in (pieces - 2, pieces - 1):
+        wide_copy(j).wait()
+    swap.wait()
+    swapped[...] = land[...].astype(F32)
+
+
+def reduce_product(left, right, gains, half, low):
     height, out_shape, scratch = reducer_buffers(left, right)
     vmem = pl.BlockSpec(memory_space=pltpu.VMEM)
+    hbm = pl.BlockSpec(memory_space=pl.ANY)
+    dma = pltpu.SemaphoreType.DMA
+    tall = low.shape[0] // 8
     return pl.pallas_call(
         functools.partial(reduce_kernel, height),
-        out_shape=out_shape,
-        in_specs=[vmem] * 3,
-        out_specs=vmem,
-        scratch_shapes=scratch,
+        out_shape=(
+            out_shape,
+            jax.ShapeDtypeStruct(half.shape, F32),
+            jax.ShapeDtypeStruct(low.shape, F32),
+        ),
+        in_specs=[vmem] * 4 + [hbm],
+        out_specs=(vmem, vmem, hbm),
+        scratch_shapes=scratch
+        + [
+            pltpu.VMEM(half.shape, BF16),
+            pltpu.VMEM((2, tall, low.shape[1]), BF16),
+            pltpu.VMEM((2, tall, low.shape[1]), F32),
+            dma((2,)),
+            dma((2,)),
+            dma((2,)),
+        ],
         compiler_params=pltpu.CompilerParams(
             collective_id=2, has_side_effects=True, vmem_limit_bytes=VMEM_LIMIT
         ),
@@ -1413,7 +1569,7 @@
             flops=50_000_000_000, bytes_accessed=10_000_000, transcendentals=0
         ),
         name="reduce_product",
-    )(left, right, gains)
+    )(left, right, gains, half, low)
 
 
 def natural(device, sub, subs):
@@ -1871,7 +2027,7 @@
         + inverse_one * scaled_one
         - residual * inverse_one**3 * jnp.mean(scaled_one * residual, axis=-1, keepdims=True)
     )
-    if folded:
+    if folded and row_groups != 4:
         input_grad = jnp.concatenate(
             [
                 input_grad[:BLOCK],
@@ -1884,7 +2040,11 @@
     )
     if row_groups == 4:
         proj_grad = proj[0]
-        part = reduce_product(normed_one, grad_qkv, gain_parts)
+        part, swapped, gate_grad = reduce_product(
+            normed_one, grad_qkv, gain_parts, input_grad[-BLOCK:].astype(BF16), gate_grad
+        )
+        if folded:
+            input_grad = jnp.concatenate([input_grad[:BLOCK], swapped], axis=0)
     else:
         part = jnp.concatenate(
             [dot_tn(normed_one, grad_qkv), gain_parts.T, jnp.zeros((width, 120), F32)], axis=1
@@ -1896,8 +2056,8 @@
     qkv_grad = unpack_kv(part[:, :qkv_cols])
     attn_gain_grad = part[:, qkv_cols]
     ffn_gain_grad = part[:, qkv_cols + 1]
-    gate_grad, part = lax.optimization_barrier((gate_grad, part))
-    gate_grad = gate_grad.astype(F32)
+    if row_groups != 4:
+        gate_grad = gate_grad.astype(F32)
     up_grad, part = lax.optimization_barrier((up_grad, part))
     up_grad = up_grad.astype(F32)
     down_grad, part = lax.optimization_barrier((down_grad, part))

time: 601 us -> 586 us (0.975)
  Pallas kernels: 507 us -> 482 us
  waiting for transfers between devices: 6 us -> 13.9 us
  local copies, waits for them, and re-layouts: 12.4 us -> 20.1 us
    pallas_call x1, Pallas kernels: 202 us -> 191 us  [ffn(): pl.pallas_call(functools.partial(ffn_kernel, subs, quad), out_shape=(jax....]
    pallas_call x1, Pallas kernels: 73.8 us -> 65.4 us  [reduce_product(): pl.pallas_call(functools.partial(reduce_kernel, height), out_shape=(out_s...]
    all_gather x3, waiting for transfers between devices: 0.01 us -> 7.95 us  [on_device(): lax.all_gather(g, 'rows', axis=0, tiled=True)]
  transfers between devices with their start and end apart: 7 -> 6, of which waited for: 1 -> 2; matrix products, arithmetic and copies ran while one was open for 7% -> 6% of each run, Pallas kernels for 51% -> 50%
where the time goes in v4:
time: 586 us; the launch traced here: 578 us
  Pallas kernels  482 us (82%)
  other arithmetic  24.4 us (4%)
  local copies, waits for them, and re-layouts  20.1 us (3%)
  between operations  16.6 us (3%)
  matrix products  14.8 us (3%)
  waiting for transfers between devices  13.9 us (2%)
    pallas_call x1, Pallas kernels, ffn(): pl.pallas_call(functools.partial(ffn_kernel, subs, quad), out_shape=(jax....  191 us
    pallas_call x1, Pallas kernels, front(): pl.pallas_call(front_kernel, out_shape=(jax.ShapeDtypeStruct((total, cols...  134 us
    pallas_call x1, Pallas kernels, attend_back(): pl.pallas_call(functools.partial(attend_back_kernel, height), in_specs=[v...  66.3 us
    pallas_call x1, Pallas kernels, reduce_product(): pl.pallas_call(functools.partial(reduce_kernel, height), out_shape=(out_s...  65.4 us
    pallas_call x1, Pallas kernels, attend(): pl.pallas_call(attend_kernel, grid_spec=pltpu.PrefetchScalarGridSpec(num_...  25.6 us
  transfers between devices with their start and end apart: 6, of which 2 were waited for; matrix products, arithmetic and copies ran while one was open for 6% of the time, Pallas kernels for 50%

profile of v4, /device:TPU:0, one launch (start us, length us, event | category | flops | bytes accessed | tf_op | source)
XLA Modules:
  0.0 578.0 jit_solution(15926647838002651743)
XLA Ops:
  7.2 0.0 all-gather.6.cloned.1.call-start
  7.3 0.7 all-gather.6.cloned.1.call-update
  7.9 0.0 all-gather.8.cloned.1.call-start
  8.0 0.7 all-gather.8.cloned.1.call-update
  8.7 0.0 all-gather.10.cloned.1.call-start
  8.7 0.9 slice.50
  9.6 0.1 pad.13.clone
  9.7 0.1 pad.16.clone
  10.5 0.2 copy.30
  10.6 0.2 copy.25
  10.8 0.2 reshape.100
  10.9 0.1 copy.26
  11.1 0.1 copy.27
  11.2 0.8 concatenate.46.shard_ref
  12.0 0.6 broadcast_multiply_fusion.2
  12.6 0.1 convert_bitcast_fusion
  12.7 0.5 fusion.10
  13.2 1.0 fusion.8
  14.3 134.0 %front.1 = (bf16[2048,2048]{1,0:T(8,128)(2,1)}, f32[8,2048]{1,0:T(8,128)}, bf16[256,2048]{1,0:T(8,128)(2,1)}, bf16[256,2048]{1,0:T(8,128)(2,1)}, f32[256,1]{1,0:...) custom-call(bf16[64,2048]{1,0:T(8,128)(2,1)} %concatenate.46.shard_ref, bf16[256,2048]{1,0:T(8,128)(2,1)} %x_ref.1, ...), custom_call_target="tpu_custom_call" | custom-call | flops 30000001024 | bytes 12000000 | tf_op jit(solution)/shard_map/front/pallas_call | solution.py:1868
  148.3 1.6 fusion.14
  149.9 0.6 convert_reduce_fusion
  151.2 0.6 fusion.11
  152.5 25.6 %attend.1 = (bf16[256,1280]{1,0:T(8,128)(2,1)}, f32[5,2,512]{2,1,0:T(2,128)}) custom-call(s32[2]{0:T(128)} %get-tuple-element.66.block_ref, bf16[256,1280]{1,0:T(8,128)(2,1)} %get-tuple-element.33.q_ref.refs_0_, bf16[2048,640]{1,0:T(8,128)(2,1)} %get-tuple-element.34.kv_ref.refs_1_), custom_call_target="tpu_custom_call" | custom-call | flops 60000002048 | bytes 8000000 | tf_op jit(solution)/shard_map/attend/pallas_call | solution.py:148
  178.1 4.4 multiply_reduce_fusion.2
  182.6 1.3 copy-done
  183.9 1.2 multiply_convert_fusion.x_ref
  185.1 4.5 all-gather.8.cloned.1.call-done.cot_ref
  189.6 190.9 %ffn.1 = (bf16[8,128,2048]{2,1,0:T(8,128)(2,1)}, bf16[4,2,128,2048]{3,2,1,0:T(8,128)(2,1)}, bf16[4,2,128,2048]{3,2,1,0:T(8,128)(2,1)}, f32[256,2048]{1,0:T(8,128...) custom-call(f32[1]{0:T(128)} %bitcast.9.scale_ref, ...), custom_call_target="tpu_custom_call" | custom-call | flops 60000002048 | bytes 60000000 | tf_op jit(solution)/shard_map/ffn/pallas_call | solution.py:1195
  380.5 0.0 all-gather.10.cloned.1.call-update
  380.6 0.0 all-gather.14.cloned.1.call-start
  380.6 0.1 pad.6.clone
  380.7 0.1 fusion.7
  380.9 2.9 multiply_reduce_fusion
  383.8 1.4 constant_dynamic-slice_fusion.1
  385.3 0.6 copy-done.1
  385.9 2.1 fusion.12
  388.0 0.9 fusion.13
  389.0 5.6 collective-permute-start
  394.5 0.0 all-gather.14.cloned.1.call-update
  394.6 0.0 all-gather.12.cloned.1.call-start
  394.6 4.9 convolution_convert_fusion.refs_3_
  399.5 66.3 %attend_back.1 = (bf16[256,1920]{1,0:T(8,128)(2,1)}, f32[40,2048]{1,0:T(8,128)}) custom-call(bf16[256,1280]{1,0:T(8,128)(2,1)} %get-tuple-element.33.q_ref.refs_0_, bf16[2048,640]{1,0:T(8,128)(2,1)} %get-tuple-element.34.kv_ref.refs_1_, bf16[256,1280]{1,0:T(8,128)(2,1)} %get-tuple-element.35.refs_2_, bf16[256,1280]{1,0:T(8,128)(2,1)} %convolution_convert_fusion.refs_3_, ...), custom_call_target="tpu_custom_call" | custom-call | flops 120000004096 | bytes 12000000 | tf_op jit(solution)/shard_map/attend_back/pallas_call | solution.py:347
  465.9 5.5 fusion.4
  471.4 0.6 fusion.3
  472.0 0.9 slice.78.half_ref
  472.9 0.1 slice.67
  473.0 0.0 all-gather.12.cloned.1.call-update
  473.0 0.7 maximum_maximum_fusion.gains
  473.7 2.1 pad_maximum_fusion.1
  475.8 65.4 %reduce_product.1 = (f32[64,2048]{1,0:T(8,128)}, f32[128,2048]{1,0:T(8,128)}, f32[2048,768]{1,0:T(8,128)}) custom-call(bf16[256,2048]{1,0:T(8,128)(2,1)} %get-tuple-element.43.left, bf16[256,1920]{1,0:T(8,128)(2,1)} %get-tuple-element.41.right, f32[8,2048]{1,0:T(8,128)} %maximum_maximum_fusion.gains, bf16[128,2048]{1,0:T(8,128)(2,1)} %slice.78.half_ref, ...), custom_call_target="tpu_custom_call" | custom-call | flops 49999998976 | bytes 10000000 | tf_op jit(solution)/shard_map/reduce_product/pallas_call | solution.py:1547
  541.3 0.0 all-gather.14.cloned.1.call-done
  541.3 7.9 %all-gather.12.cloned.1.call-done = bf16[768,2048]{1,0:T(8,128)(2,1)} async-done(((bf16[192,2048]{1,0:T(8,128)(2,1)}), bf16[768,2048]{1,0:T(8,128)(2,1)}) %all-gather.12.cloned.1.call-update) | async-done | bytes 3145744 | tf_op jit(solution)/shard_map/all_gather | solution.py:2017
  549.2 0.9 slice.61
  550.2 1.0 slice.60
  551.2 1.6 slice_reduce_fusion
  552.7 5.6 convert_element_type.57
  558.3 3.2 convert_element_type.56
  561.5 0.2 reshape.102
  561.7 0.2 copy.28
  561.9 0.1 copy.29
  562.1 0.8 pad_maximum_fusion.2
  562.9 1.5 pad_maximum_fusion
  564.4 0.7 copy.34
  565.1 5.9 %copy.35 = f32[2048,768]{1,0:T(8,128)} copy(f32[2048,768]{1,0:T(8,128)} %get-tuple-element.102) | data formatting | bytes 12582912
  (45 shorter events, 0.1 us)
Async XLA Ops:
  7.2 4.0 slice-start
  7.2 3.8 copy-start.13
  7.2 3.9 copy-start.14
  7.2 170.9 %all-gather.6.cloned.1.call-start = ((), (), s32[]{:S(2)}) async-start(), calls=%async_computation | async-start | bytes 5406720 | tf_op jit(solution)/shard_map/all_gather | solution.py:1968
  7.9 181.7 %all-gather.8.cloned.1.call-start = ((), (), s32[]{:S(2)}) async-start(), calls=%async_computation.1 | async-start | bytes 9437184 | tf_op jit(solution)/shard_map/all_gather | solution.py:1967
  8.7 467.1 %all-gather.10.cloned.1.call-start = ((), (), s32[]{:S(2)}) async-start(), calls=%async_computation.2 | async-start | bytes 3932160 | tf_op jit(solution)/shard_map/all_gather | solution.py:2017
  14.3 136.9 %copy-start.15 = (f32[4]{0:T(128)S(1)}, f32[4]{0:T(128)}, u32[]{:S(2)}) copy-start(f32[4]{0:T(128)} %param.14) | copy-start | bytes 52
  152.4 25.7 %copy-start.6 = (bf16[256,2048]{1,0:T(8,128)(2,1)S(1)}, bf16[256,2048]{1,0:T(8,128)(2,1)}, u32[]{:S(2)}) copy-start(bf16[256,2048]{1,0:T(8,128)(2,1)} %get-tuple-element.32) | copy-start | bytes 3145732
  182.5 1.3 copy-start
  189.6 191.1 %copy-start.11 = (f32[256,1]{1,0:T(8,128)S(1)}, f32[256,1]{1,0:T(8,128)}, u32[]{:S(2)}) copy-start(f32[256,1]{1,0:T(8,128)} %get-tuple-element.39) | copy-start | bytes 3076
  380.6 160.7 %all-gather.14.cloned.1.call-start = ((), (), s32[]{:S(2)}) async-start(), calls=%async_computation.4 | async-start | bytes 3932160 | tf_op jit(solution)/shard_map/all_gather | solution.py:2017
  380.9 4.4 copy-start.3
  380.9 4.4 copy-start.5
  383.8 2.0 copy-start.1
  388.0 11.5 %copy-start.8 = (bf16[256,2048]{1,0:T(8,128)(2,1)}, bf16[256,2048]{1,0:T(8,128)(2,1)S(1)}, u32[]{:S(2)}) copy-start(bf16[256,2048]{1,0:T(8,128)(2,1)S(1)} %get-tuple-element.63.refs_9_) | copy-start | bytes 3145732
  389.0 84.8 %collective-permute-start = (bf16[128,2048]{1,0:T(8,128)(2,1)}, bf16[128,2048]{1,0:T(8,128)(2,1)}, u32[]{:S(2)}, u32[]{:S(2)}) collective-permute-start(bf16[128,2048]{1,0:T(8,128)(2,1)} %get-tuple-element.71), channel_id=1, source_target_pairs={{0,7},{1,6},{2,5},{3,4},{4,3},{5,2},{6,1},{7,0},{8,15},{9,14},{10,... | collective-permute-start | bytes 1572872 | tf_op jit(solution)/shard_map/ppermute | solution.py:1938
  394.6 154.7 %all-gather.12.cloned.1.call-start = ((), (), s32[]{:S(2)}) async-start(), calls=%async_computation.3 | async-start | bytes 3932160 | tf_op jit(solution)/shard_map/all_gather | solution.py:2017
  399.5 66.4 %copy-start.7 = (bf16[256,2048]{1,0:T(8,128)(2,1)S(1)}, bf16[256,2048]{1,0:T(8,128)(2,1)}, u32[]{:S(2)}) copy-start(bf16[256,2048]{1,0:T(8,128)(2,1)} %get-tuple-element.32) | copy-start | bytes 3145732
  399.5 66.4 %copy-start.12 = (f32[1,2048]{1,0:T(1,128)S(1)}, f32[1,2048]{1,0:T(1,128)}, u32[]{:S(2)}) copy-start(f32[1,2048]{1,0:T(1,128)} %get-tuple-element.76) | copy-start | bytes 24580
  465.9 5.5 copy-start.2
  552.7 5.6 copy-start.4
  561.5 1.4 copy-start.9
  562.9 1.5 copy-start.10
Sparse Core Ops, SparseCore 0:
  10.9 87.4 all-gather.5
  100.0 89.5 all-gather.7
  380.7 61.4 all-gather.9
  443.9 45.4 all-gather.13
  491.0 58.1 all-gather.11

commit v5 on v4

--- a/solution.py
+++ b/solution.py
@@ -2062,7 +2062,6 @@
     up_grad = up_grad.astype(F32)
     down_grad, part = lax.optimization_barrier((down_grad, part))
     down_grad = down_grad.astype(F32)
-    qkv_grad = unpack_kv(part[:, :qkv_cols])
     attn_gain_grad = part[:, qkv_cols]
     ffn_gain_grad = part[:, qkv_cols + 1]
     return (

time: 586 us -> 584 us (level)
  transfers between devices with their start and end apart: 6 -> 6, of which waited for: 2 -> 2; matrix products, arithmetic and copies ran while one was open for 6% -> 7% of each run, Pallas kernels for 50% -> 51%
where the time goes in v5:
time: 584 us; the launch traced here: 576 us
  Pallas kernels  482 us (83%)
  other arithmetic  24.4 us (4%)
  local copies, waits for them, and re-layouts  20.1 us (3%)
  between operations  16.6 us (3%)
  matrix products  14.8 us (3%)
  waiting for transfers between devices  12 us (2%)
    pallas_call x1, Pallas kernels, ffn(): pl.pallas_call(functools.partial(ffn_kernel, subs, quad), out_shape=(jax....  191 us
    pallas_call x1, Pallas kernels, front(): pl.pallas_call(front_kernel, out_shape=(jax.ShapeDtypeStruct((total, cols...  134 us
    pallas_call x1, Pallas kernels, attend_back(): pl.pallas_call(functools.partial(attend_back_kernel, height), in_specs=[v...  66.3 us
    pallas_call x1, Pallas kernels, reduce_product(): pl.pallas_call(functools.partial(reduce_kernel, height), out_shape=(out_s...  65.4 us
    pallas_call x1, Pallas kernels, attend(): pl.pallas_call(attend_kernel, grid_spec=pltpu.PrefetchScalarGridSpec(num_...  25.6 us
  transfers between devices with their start and end apart: 6, of which 2 were waited for; matrix products, arithmetic and copies ran while one was open for 7% of the time, Pallas kernels for 51%

profile of v5, /device:TPU:0, one launch (start us, length us, event | category | flops | bytes accessed | tf_op | source)
XLA Modules:
  0.0 576.0 jit_solution(10504343717742045459)
XLA Ops:
  7.2 0.0 all-gather.6.cloned.1.call-start
  7.3 0.7 all-gather.6.cloned.1.call-update
  7.9 0.0 all-gather.8.cloned.1.call-start
  8.0 0.7 all-gather.8.cloned.1.call-update
  8.7 0.0 all-gather.10.cloned.1.call-start
  8.7 0.9 slice.50
  9.6 0.1 pad.13.clone
  9.7 0.1 pad.16.clone
  10.5 0.2 copy.30
  10.6 0.2 copy.25
  10.8 0.2 reshape.100
  10.9 0.1 copy.26
  11.1 0.1 copy.27
  11.2 0.8 concatenate.46.shard_ref
  12.0 0.6 broadcast_multiply_fusion.2
  12.6 0.1 convert_bitcast_fusion
  12.7 0.5 fusion.10
  13.2 1.0 fusion.8
  14.3 134.0 %front.1 = (bf16[2048,2048]{1,0:T(8,128)(2,1)}, f32[8,2048]{1,0:T(8,128)}, bf16[256,2048]{1,0:T(8,128)(2,1)}, bf16[256,2048]{1,0:T(8,128)(2,1)}, f32[256,1]{1,0:...) custom-call(bf16[64,2048]{1,0:T(8,128)(2,1)} %concatenate.46.shard_ref, bf16[256,2048]{1,0:T(8,128)(2,1)} %x_ref.1, ...), custom_call_target="tpu_custom_call" | custom-call | flops 30000001024 | bytes 12000000 | tf_op jit(solution)/shard_map/front/pallas_call | solution.py:1868
  148.3 1.6 fusion.14
  149.9 0.6 convert_reduce_fusion
  151.2 0.6 fusion.11
  152.5 25.6 %attend.1 = (bf16[256,1280]{1,0:T(8,128)(2,1)}, f32[5,2,512]{2,1,0:T(2,128)}) custom-call(s32[2]{0:T(128)} %get-tuple-element.66.block_ref, bf16[256,1280]{1,0:T(8,128)(2,1)} %get-tuple-element.33.q_ref.refs_0_, bf16[2048,640]{1,0:T(8,128)(2,1)} %get-tuple-element.34.kv_ref.refs_1_), custom_call_target="tpu_custom_call" | custom-call | flops 60000002048 | bytes 8000000 | tf_op jit(solution)/shard_map/attend/pallas_call | solution.py:148
  178.1 4.4 multiply_reduce_fusion.2
  182.6 1.3 copy-done
  183.9 1.2 multiply_convert_fusion.x_ref
  185.1 4.5 all-gather.8.cloned.1.call-done.cot_ref
  189.6 190.9 %ffn.1 = (bf16[8,128,2048]{2,1,0:T(8,128)(2,1)}, bf16[4,2,128,2048]{3,2,1,0:T(8,128)(2,1)}, bf16[4,2,128,2048]{3,2,1,0:T(8,128)(2,1)}, f32[256,2048]{1,0:T(8,128...) custom-call(f32[1]{0:T(128)} %bitcast.9.scale_ref, ...), custom_call_target="tpu_custom_call" | custom-call | flops 60000002048 | bytes 60000000 | tf_op jit(solution)/shard_map/ffn/pallas_call | solution.py:1195
  380.5 0.0 all-gather.10.cloned.1.call-update
  380.6 0.0 all-gather.12.cloned.1.call-start
  380.6 0.1 pad.6.clone
  380.7 0.1 fusion.7
  380.9 2.9 multiply_reduce_fusion
  383.8 1.4 constant_dynamic-slice_fusion.1
  385.3 0.6 copy-done.1
  385.9 2.1 fusion.12
  388.0 0.9 fusion.13
  389.0 5.6 collective-permute-start
  394.5 0.0 all-gather.12.cloned.1.call-update
  394.6 0.0 all-gather.14.cloned.1.call-start
  394.6 4.9 convolution_convert_fusion.refs_3_
  399.5 66.3 %attend_back.1 = (bf16[256,1920]{1,0:T(8,128)(2,1)}, f32[40,2048]{1,0:T(8,128)}) custom-call(bf16[256,1280]{1,0:T(8,128)(2,1)} %get-tuple-element.33.q_ref.refs_0_, bf16[2048,640]{1,0:T(8,128)(2,1)} %get-tuple-element.34.kv_ref.refs_1_, bf16[256,1280]{1,0:T(8,128)(2,1)} %get-tuple-element.35.refs_2_, bf16[256,1280]{1,0:T(8,128)(2,1)} %convolution_convert_fusion.refs_3_, ...), custom_call_target="tpu_custom_call" | custom-call | flops 120000004096 | bytes 12000000 | tf_op jit(solution)/shard_map/attend_back/pallas_call | solution.py:347
  465.9 5.5 fusion.4
  471.4 0.6 fusion.3
  472.0 0.9 slice.78.half_ref
  472.9 0.1 slice.67
  473.0 0.0 all-gather.14.cloned.1.call-update
  473.0 0.7 maximum_maximum_fusion.gains
  473.7 2.1 pad_maximum_fusion.1
  475.8 65.4 %reduce_product.1 = (f32[64,2048]{1,0:T(8,128)}, f32[128,2048]{1,0:T(8,128)}, f32[2048,768]{1,0:T(8,128)}) custom-call(bf16[256,2048]{1,0:T(8,128)(2,1)} %get-tuple-element.43.left, bf16[256,1920]{1,0:T(8,128)(2,1)} %get-tuple-element.41.right, f32[8,2048]{1,0:T(8,128)} %maximum_maximum_fusion.gains, bf16[128,2048]{1,0:T(8,128)(2,1)} %slice.78.half_ref, ...), custom_call_target="tpu_custom_call" | custom-call | flops 49999998976 | bytes 10000000 | tf_op jit(solution)/shard_map/reduce_product/pallas_call | solution.py:1547
  541.3 0.9 slice.61
  542.2 1.0 slice.60
  543.2 0.0 all-gather.12.cloned.1.call-done
  543.2 6.0 %all-gather.14.cloned.1.call-done = bf16[768,2048]{1,0:T(8,128)(2,1)} async-done(((bf16[192,2048]{1,0:T(8,128)(2,1)}), bf16[768,2048]{1,0:T(8,128)(2,1)}) %all-gather.14.cloned.1.call-update) | async-done | bytes 3145744 | tf_op jit(solution)/shard_map/all_gather | solution.py:2017
  549.2 5.6 convert_element_type.57
  554.8 1.6 slice_reduce_fusion
  556.4 3.2 convert_element_type.56
  559.6 0.2 reshape.102
  559.8 0.2 copy.28
  560.0 0.1 copy.29
  560.1 0.8 pad_maximum_fusion.2
  561.0 1.5 pad_maximum_fusion
  562.4 0.7 copy.34
  563.2 5.9 %copy.35 = f32[2048,768]{1,0:T(8,128)} copy(f32[2048,768]{1,0:T(8,128)} %get-tuple-element.102) | data formatting | bytes 12582912
  (45 shorter events, 0.1 us)
Async XLA Ops:
  7.2 4.0 slice-start
  7.2 3.8 copy-start.13
  7.2 3.9 copy-start.14
  7.2 170.9 %all-gather.6.cloned.1.call-start = ((), (), s32[]{:S(2)}) async-start(), calls=%async_computation | async-start | bytes 5406720 | tf_op jit(solution)/shard_map/all_gather | solution.py:1968
  7.9 181.7 %all-gather.8.cloned.1.call-start = ((), (), s32[]{:S(2)}) async-start(), calls=%async_computation.1 | async-start | bytes 9437184 | tf_op jit(solution)/shard_map/all_gather | solution.py:1967
  8.7 467.1 %all-gather.10.cloned.1.call-start = ((), (), s32[]{:S(2)}) async-start(), calls=%async_computation.2 | async-start | bytes 3932160 | tf_op jit(solution)/shard_map/all_gather | solution.py:2017
  14.3 136.9 %copy-start.15 = (f32[4]{0:T(128)S(1)}, f32[4]{0:T(128)}, u32[]{:S(2)}) copy-start(f32[4]{0:T(128)} %param.14) | copy-start | bytes 52
  152.4 25.7 %copy-start.6 = (bf16[256,2048]{1,0:T(8,128)(2,1)S(1)}, bf16[256,2048]{1,0:T(8,128)(2,1)}, u32[]{:S(2)}) copy-start(bf16[256,2048]{1,0:T(8,128)(2,1)} %get-tuple-element.32) | copy-start | bytes 3145732
  182.5 1.3 copy-start
  189.6 191.1 %copy-start.11 = (f32[256,1]{1,0:T(8,128)S(1)}, f32[256,1]{1,0:T(8,128)}, u32[]{:S(2)}) copy-start(f32[256,1]{1,0:T(8,128)} %get-tuple-element.39) | copy-start | bytes 3076
  380.6 162.7 %all-gather.12.cloned.1.call-start = ((), (), s32[]{:S(2)}) async-start(), calls=%async_computation.3 | async-start | bytes 3932160 | tf_op jit(solution)/shard_map/all_gather | solution.py:2017
  380.9 4.4 copy-start.3
  380.9 4.4 copy-start.5
  383.8 2.0 copy-start.1
  388.0 11.5 %copy-start.8 = (bf16[256,2048]{1,0:T(8,128)(2,1)}, bf16[256,2048]{1,0:T(8,128)(2,1)S(1)}, u32[]{:S(2)}) copy-start(bf16[256,2048]{1,0:T(8,128)(2,1)S(1)} %get-tuple-element.63.refs_9_) | copy-start | bytes 3145732
  389.0 84.8 %collective-permute-start = (bf16[128,2048]{1,0:T(8,128)(2,1)}, bf16[128,2048]{1,0:T(8,128)(2,1)}, u32[]{:S(2)}, u32[]{:S(2)}) collective-permute-start(bf16[128,2048]{1,0:T(8,128)(2,1)} %get-tuple-element.71), channel_id=1, source_target_pairs={{0,7},{1,6},{2,5},{3,4},{4,3},{5,2},{6,1},{7,0},{8,15},{9,14},{10,... | collective-permute-start | bytes 1572872 | tf_op jit(solution)/shard_map/ppermute | solution.py:1938
  394.6 154.7 %all-gather.14.cloned.1.call-start = ((), (), s32[]{:S(2)}) async-start(), calls=%async_computation.4 | async-start | bytes 3932160 | tf_op jit(solution)/shard_map/all_gather | solution.py:2017
  399.5 66.4 %copy-start.7 = (bf16[256,2048]{1,0:T(8,128)(2,1)S(1)}, bf16[256,2048]{1,0:T(8,128)(2,1)}, u32[]{:S(2)}) copy-start(bf16[256,2048]{1,0:T(8,128)(2,1)} %get-tuple-element.32) | copy-start | bytes 3145732
  399.5 66.4 %copy-start.12 = (f32[1,2048]{1,0:T(1,128)S(1)}, f32[1,2048]{1,0:T(1,128)}, u32[]{:S(2)}) copy-start(f32[1,2048]{1,0:T(1,128)} %get-tuple-element.76) | copy-start | bytes 24580
  465.9 5.5 copy-start.2
  549.2 7.2 %copy-start.4 = (bf16[2048,768]{1,0:T(8,128)(2,1)S(1)}, bf16[2048,768]{1,0:T(8,128)(2,1)}, u32[]{:S(2)}) copy-start(bf16[2048,768]{1,0:T(8,128)(2,1)} %all-gather.12.cloned.1.call-done) | copy-start | bytes 9437188
  559.6 1.4 copy-start.9
  561.0 1.5 copy-start.10
Sparse Core Ops, SparseCore 0:
  10.9 87.4 all-gather.5
  100.0 89.5 all-gather.7
  380.7 61.4 all-gather.9
  443.9 45.4 all-gather.11
  491.0 58.1 all-gather.13
